TPU v7x, 128 devices: a whole 4x4x4 slice. The times are simulated.
128 devices in a mesh: ctx: 32 (over x, y, z_lo), tp: 4 (over z_hi, core).
Axes of the slice: x: 4, y: 4, z: 4 (z_hi: 2, z_lo: 2; z = z_hi * 2 + z_lo), core: 2. Of those that a mesh axis runs over, the one named last changes fastest.
Arguments:
- block_input: bfloat16 [4096, 1024], P(('ctx', 'tp')), may hold values from -6 to 6
- block_map: int32 [32], replicated, may hold values from 0 to 31, each once
- attn_gain: float32 [1024], replicated, may hold values from 0.1 to 1.9
- query_weight: bfloat16 [1024, 1024], P(None, 'tp'), may hold values from -0.1875 to 0.1875
- key_weight: bfloat16 [1024, 512], P(None, 'tp'), may hold values from -0.1875 to 0.1875
- value_weight: bfloat16 [1024, 512], P(None, 'tp'), may hold values from -0.1875 to 0.1875
- query_gain: float32 [64], replicated, may hold values from 0.5 to 2
- key_gain: float32 [64], replicated, may hold values from 0.5 to 2
- output_weight: bfloat16 [1024, 1024], P('tp'), may hold values from -3 to 3
- ffn_gain: float32 [1024], replicated, may hold values from 0.1 to 1.9
- gate_weight: bfloat16 [1024, 4608], P(None, 'tp'), may hold values from -0.1875 to 0.1875
- up_weight: bfloat16 [1024, 4608], P(None, 'tp'), may hold values from -0.1875 to 0.1875
- down_weight: bfloat16 [4608, 1024], P('tp'), may hold values from -0.09375 to 0.09375
- cotangent: bfloat16 [4096, 1024], P(('ctx', 'tp')), may hold values from -6 to 6
Outputs:
- block_output: float32 [4096, 1024], P(('ctx', 'tp'))
- input_grad: float32 [4096, 1024], P(('ctx', 'tp'))
- grad_attn_gain: float32 [1024], replicated
- grad_query: float32 [1024, 1024], P(None, 'tp')
- grad_key: float32 [1024, 512], P(None, 'tp')
- grad_value: float32 [1024, 512], P(None, 'tp')
- grad_query_gain: float32 [64], replicated
- grad_key_gain: float32 [64], replicated
- grad_output: float32 [1024, 1024], P('tp')
- grad_ffn_gain: float32 [1024], replicated
- grad_gate: float32 [1024, 4608], P(None, 'tp')
- grad_up: float32 [1024, 4608], P(None, 'tp')
- grad_down: float32 [4608, 1024], P('tp')
Inputs may be any that keep to these rules, and one draw needn't show every extreme that they name: Each value appears once; ctx index e holds, for sequence 0 and then sequence 1, the position blocks block_map[e] and 63 - block_map[e] of 32 tokens each, in that order.
All inputs are finite; a program needn't handle non-finite values.
Results may differ from a plain program's by a relative error of at most 0.034.
Values may be sent and summed in bfloat16 or wider, within the bound.
A program may use at most 128 MiB of HBM per device.

v0:
```python
import math

import jax
import jax.numpy as jnp
from jax import lax
from jax.sharding import PartitionSpec as P

EPS = 1e-05
THETA = 1000000.0
NEGATIVE = -1e30


def rms_forward(values, norm_gain):
    inverse = lax.rsqrt(jnp.mean(values * values, axis=-1, keepdims=True) + EPS)
    return (values * inverse * norm_gain, inverse)


def rms_backward(values, inverse, norm_gain, upstream):
    scaled = upstream * norm_gain
    inner_mean = jnp.mean(scaled * values, axis=-1, keepdims=True)
    through = inverse * (scaled - values * inverse * inverse * inner_mean)
    return (through, upstream * values * inverse)


def rope_tables(positions, head_dim):
    halfway = head_dim // 2
    frequency = THETA ** (-(jnp.arange(halfway, dtype=jnp.float32) * 2.0 / head_dim))
    angles = positions.astype(jnp.float32)[:, None] * frequency[None, :]
    return (jnp.cos(angles)[:, None, :], jnp.sin(angles)[:, None, :])


def rope_apply(values, cosine, sine_table):
    halfway = values.shape[-1] // 2
    first_half = values[..., :halfway]
    second_half = values[..., halfway:]
    return jnp.concatenate(
        [
            first_half * cosine - second_half * sine_table,
            second_half * cosine + first_half * sine_table,
        ],
        axis=-1,
    )


def rope_back(upstream, cosine, sine_table):
    halfway = upstream.shape[-1] // 2
    first_half = upstream[..., :halfway]
    second_half = upstream[..., halfway:]
    return jnp.concatenate(
        [
            first_half * cosine + second_half * sine_table,
            second_half * cosine - first_half * sine_table,
        ],
        axis=-1,
    )


def row_places(block_map, holder, rows_total, place_count):
    piece_len = rows_total // 4
    within = jnp.arange(rows_total, dtype=jnp.int32)
    picked = jnp.sum(jnp.where(jnp.arange(place_count, dtype=jnp.int32) == holder, block_map, 0))
    later = within // piece_len % 2
    piece_index = jnp.where(later == 1, 2 * place_count - 1 - picked, picked)
    return piece_index * piece_len + within % piece_len


def span_places(block_map, first_anchor, shard_span, seq_rows, place_count):
    piece_len = seq_rows // 2
    anchors = first_anchor + jnp.arange(shard_span, dtype=jnp.int32)
    picked = jnp.sum(
        jnp.where(
            jnp.arange(place_count, dtype=jnp.int32)[None, :] == anchors[:, None],
            block_map[None, :],
            0,
        ),
        axis=1,
    )
    within = jnp.arange(seq_rows, dtype=jnp.int32)
    later = within // piece_len % 2
    piece_index = jnp.where(
        later[None, :] == 1, 2 * place_count - 1 - picked[:, None], picked[:, None]
    )
    return (piece_index * piece_len + (within % piece_len)[None, :]).reshape(shard_span * seq_rows)


def gather_rows(rows_low):
    return lax.all_gather(rows_low, "tp", axis=0, tiled=True)


def reduce_rows(partial_rows):
    return lax.psum_scatter(
        partial_rows.astype(jnp.bfloat16), "tp", scatter_dimension=0, tiled=True
    ).astype(jnp.float32)


def per_device(
    block_input,
    block_map,
    attn_gain,
    query_weight,
    key_weight,
    value_weight,
    query_gain,
    key_gain,
    output_weight,
    ffn_gain,
    gate_weight,
    up_weight,
    down_weight,
    cotangent,
):
    place_count = lax.axis_size("ctx")
    place_index = lax.axis_index("ctx")
    head_dim = query_gain.shape[0]
    query_heads = query_weight.shape[1] // head_dim
    kv_heads = key_weight.shape[1] // head_dim
    group_size = query_heads // kv_heads
    score_scale = 1.0 / math.sqrt(head_dim)
    shard_span = 4
    residual_in = block_input.astype(jnp.float32)
    normed_one, inverse_one = rms_forward(residual_in, attn_gain)
    rows_one = gather_rows(normed_one.astype(jnp.bfloat16))
    rows_total = rows_one.shape[0]
    seq_rows = rows_total // 2
    kv_width = kv_heads * head_dim
    own_places = row_places(block_map, place_index, rows_total, place_count)
    query_raw = jnp.dot(rows_one, query_weight, preferred_element_type=jnp.float32).reshape(
        rows_total, query_heads, head_dim
    )
    key_raw = jnp.dot(rows_one, key_weight, preferred_element_type=jnp.float32).reshape(
        rows_total, kv_heads, head_dim
    )
    values_own = jnp.dot(rows_one, value_weight, preferred_element_type=jnp.float32).astype(
        jnp.bfloat16
    )
    query_normed, query_inverse = rms_forward(query_raw, query_gain)
    key_normed, key_inverse = rms_forward(key_raw, key_gain)
    cosine, sine_table = rope_tables(own_places, head_dim)
    query_rot = rope_apply(query_normed, cosine, sine_table).astype(jnp.bfloat16)
    keys_own = (
        rope_apply(key_normed, cosine, sine_table)
        .astype(jnp.bfloat16)
        .reshape(rows_total, kv_width)
    )
    query_blocks = query_rot.reshape(2, seq_rows, kv_heads, group_size, head_dim)
    query_places = own_places[:seq_rows]

    def span_heads(flat_rows):
        return jnp.transpose(
            flat_rows.reshape(shard_span, 2, seq_rows, kv_heads, head_dim), (1, 0, 2, 3, 4)
        ).reshape(2, shard_span * seq_rows, kv_heads, head_dim)

    def span_flat(head_rows):
        return jnp.transpose(
            head_rows.reshape(2, shard_span, seq_rows, kv_width), (1, 0, 2, 3)
        ).reshape(shard_span * rows_total, kv_width)

    def scores_for(key_heads, key_places):
        scores = (
            jnp.einsum(
                "sqhgd,skhd->shgqk", query_blocks, key_heads, preferred_element_type=jnp.float32
            )
            * score_scale
        )
        allowed = key_places[None, :] <= query_places[:, None]
        return (scores, allowed)

    def forward_step(softmax_state, key_heads, value_heads, key_places):
        running_top, running_total, running_acc = softmax_state
        scores, allowed = scores_for(key_heads, key_places)
        scores = jnp.where(allowed, scores, NEGATIVE)
        new_top = jnp.maximum(running_top, jnp.max(scores, axis=-1))
        weights = jnp.where(allowed, jnp.exp(scores - new_top[..., None]), 0.0)
        fading = jnp.exp(running_top - new_top)
        running_total = running_total * fading + jnp.sum(weights, axis=-1)
        running_acc = running_acc * fading[..., None] + jnp.einsum(
            "shgqk,skhd->shgqd",
            weights.astype(jnp.bfloat16),
            value_heads,
            preferred_element_type=jnp.float32,
        )
        return (new_top, running_total, running_acc)

    start_state = (
        jnp.full((2, kv_heads, group_size, seq_rows), NEGATIVE, jnp.float32),
        jnp.zeros((2, kv_heads, group_size, seq_rows), jnp.float32),
        jnp.zeros((2, kv_heads, group_size, seq_rows, head_dim), jnp.float32),
    )
    span_count = place_count // shard_span
    span_rows = shard_span * rows_total
    whole_keys, whole_values = (
        lax.all_gather(keys_own, "ctx", axis=0, tiled=True),
        lax.all_gather(values_own, "ctx", axis=0, tiled=True),
    )

    def whole_forward(span_index, softmax_state):
        first_anchor = span_index * shard_span
        keys_flat = lax.dynamic_slice_in_dim(whole_keys, first_anchor * rows_total, span_rows, 0)
        values_flat = lax.dynamic_slice_in_dim(
            whole_values, first_anchor * rows_total, span_rows, 0
        )
        key_places = span_places(block_map, first_anchor, shard_span, seq_rows, place_count)
        return forward_step(
            softmax_state, span_heads(keys_flat), span_heads(values_flat), key_places
        )

    softmax_state = lax.fori_loop(0, span_count, whole_forward, start_state)
    running_top, running_total, running_acc = softmax_state
    log_total = running_top + jnp.log(running_total)
    attn_rows = jnp.transpose(running_acc / running_total[..., None], (0, 3, 1, 2, 4))
    attn_low = attn_rows.reshape(rows_total, query_heads * head_dim).astype(jnp.bfloat16)
    residual_mid = residual_in + reduce_rows(
        jnp.dot(attn_low, output_weight, preferred_element_type=jnp.float32)
    )
    normed_two, inverse_two = rms_forward(residual_mid, ffn_gain)
    rows_two = gather_rows(normed_two.astype(jnp.bfloat16))
    gate_pre = jnp.dot(rows_two, gate_weight, preferred_element_type=jnp.float32)
    up_pre = jnp.dot(rows_two, up_weight, preferred_element_type=jnp.float32)
    gate_sig = jax.nn.sigmoid(gate_pre)
    activated = (gate_pre * gate_sig * up_pre).astype(jnp.bfloat16)
    block_output = residual_mid + reduce_rows(
        jnp.dot(activated, down_weight, preferred_element_type=jnp.float32)
    )
    grad_rows = gather_rows(cotangent)
    grad_down = jnp.dot(activated.T, grad_rows, preferred_element_type=jnp.float32)
    grad_act = jnp.dot(grad_rows, down_weight.T, preferred_element_type=jnp.float32)
    grad_gate_pre = (grad_act * up_pre * gate_sig * (1.0 + gate_pre * (1.0 - gate_sig))).astype(
        jnp.bfloat16
    )
    grad_up_pre = (grad_act * gate_pre * gate_sig).astype(jnp.bfloat16)
    grad_gate = jnp.dot(rows_two.T, grad_gate_pre, preferred_element_type=jnp.float32)
    grad_up = jnp.dot(rows_two.T, grad_up_pre, preferred_element_type=jnp.float32)
    grad_normed_two = reduce_rows(
        jnp.dot(grad_gate_pre, gate_weight.T, preferred_element_type=jnp.float32)
        + jnp.dot(grad_up_pre, up_weight.T, preferred_element_type=jnp.float32)
    )
    through_two, ffn_terms = rms_backward(residual_mid, inverse_two, ffn_gain, grad_normed_two)
    grad_mid = cotangent.astype(jnp.float32) + through_two
    grad_mid_rows = gather_rows(grad_mid.astype(jnp.bfloat16))
    grad_output = jnp.dot(attn_low.T, grad_mid_rows, preferred_element_type=jnp.float32)
    grad_attn = jnp.dot(grad_mid_rows, output_weight.T, preferred_element_type=jnp.float32).astype(
        jnp.bfloat16
    )
    grad_attn_blocks = grad_attn.reshape(2, seq_rows, kv_heads, group_size, head_dim)
    delta_rows = jnp.sum(grad_attn_blocks.astype(jnp.float32) * attn_rows, axis=-1)
    delta_rows = jnp.transpose(delta_rows, (0, 2, 3, 1))

    def backward_step(key_heads, value_heads, key_places):
        scores, allowed = scores_for(key_heads, key_places)
        probs = jnp.where(allowed, jnp.exp(scores - log_total[..., None]), 0.0)
        grad_value_block = jnp.einsum(
            "shgqk,sqhgd->skhd",
            probs.astype(jnp.bfloat16),
            grad_attn_blocks,
            preferred_element_type=jnp.float32,
        )
        grad_probs = jnp.einsum(
            "sqhgd,skhd->shgqk", grad_attn_blocks, value_heads, preferred_element_type=jnp.float32
        )
        grad_scores = (score_scale * probs * (grad_probs - delta_rows[..., None])).astype(
            jnp.bfloat16
        )
        grad_query_block = jnp.einsum(
            "shgqk,skhd->sqhgd", grad_scores, key_heads, preferred_element_type=jnp.float32
        )
        grad_key_block = jnp.einsum(
            "shgqk,sqhgd->skhd", grad_scores, query_blocks, preferred_element_type=jnp.float32
        )
        return (grad_query_block, grad_key_block, grad_value_block)

    key_grad_whole = jnp.zeros((place_count * rows_total, kv_width), jnp.float32)
    start_grads = (
        jnp.zeros((2, seq_rows, kv_heads, group_size, head_dim), jnp.float32),
        key_grad_whole,
        key_grad_whole,
    )

    def whole_backward(span_index, grad_carry):
        query_acc, key_grad_all, value_grad_all = grad_carry
        first_anchor = span_index * shard_span
        keys_flat = lax.dynamic_slice_in_dim(whole_keys, first_anchor * rows_total, span_rows, 0)
        values_flat = lax.dynamic_slice_in_dim(
            whole_values, first_anchor * rows_total, span_rows, 0
        )
        key_places = span_places(block_map, first_anchor, shard_span, seq_rows, place_count)
        add_query, add_key, add_value = backward_step(
            span_heads(keys_flat), span_heads(values_flat), key_places
        )
        key_grad_all = lax.dynamic_update_slice_in_dim(
            key_grad_all, span_flat(add_key), first_anchor * rows_total, 0
        )
        value_grad_all = lax.dynamic_update_slice_in_dim(
            value_grad_all, span_flat(add_value), first_anchor * rows_total, 0
        )
        return (query_acc + add_query, key_grad_all, value_grad_all)

    query_acc, key_grad_all, value_grad_all = lax.fori_loop(
        0, span_count, whole_backward, start_grads
    )
    grad_keys_flat, grad_values_flat = (
        lax.psum_scatter(
            key_grad_all.astype(jnp.bfloat16), "ctx", scatter_dimension=0, tiled=True
        ).astype(jnp.float32),
        lax.psum_scatter(
            value_grad_all.astype(jnp.bfloat16), "ctx", scatter_dimension=0, tiled=True
        ).astype(jnp.float32),
    )
    grad_query_rot = query_acc.reshape(rows_total, query_heads, head_dim)
    grad_key_rot = grad_keys_flat.reshape(rows_total, kv_heads, head_dim)
    grad_query_raw, query_terms = rms_backward(
        query_raw, query_inverse, query_gain, rope_back(grad_query_rot, cosine, sine_table)
    )
    grad_key_raw, key_terms = rms_backward(
        key_raw, key_inverse, key_gain, rope_back(grad_key_rot, cosine, sine_table)
    )
    grad_query_low = grad_query_raw.reshape(rows_total, query_heads * head_dim).astype(jnp.bfloat16)
    grad_key_low = grad_key_raw.reshape(rows_total, kv_width).astype(jnp.bfloat16)
    grad_value_low = grad_values_flat.astype(jnp.bfloat16)
    grad_query = jnp.dot(rows_one.T, grad_query_low, preferred_element_type=jnp.float32)
    grad_key = jnp.dot(rows_one.T, grad_key_low, preferred_element_type=jnp.float32)
    grad_value = jnp.dot(rows_one.T, grad_value_low, preferred_element_type=jnp.float32)
    grad_normed_one = reduce_rows(
        jnp.dot(grad_query_low, query_weight.T, preferred_element_type=jnp.float32)
        + jnp.dot(grad_key_low, key_weight.T, preferred_element_type=jnp.float32)
        + jnp.dot(grad_value_low, value_weight.T, preferred_element_type=jnp.float32)
    )
    through_one, attn_terms = rms_backward(residual_in, inverse_one, attn_gain, grad_normed_one)
    input_grad = grad_mid + through_one
    summed_query, summed_key, summed_value, summed_output, summed_gate, summed_up, summed_down = (
        lax.psum_scatter(
            grad_query.astype(jnp.bfloat16), "ctx", scatter_dimension=0, tiled=True
        ).astype(jnp.float32),
        lax.psum_scatter(
            grad_key.astype(jnp.bfloat16), "ctx", scatter_dimension=0, tiled=True
        ).astype(jnp.float32),
        lax.psum_scatter(
            grad_value.astype(jnp.bfloat16), "ctx", scatter_dimension=0, tiled=True
        ).astype(jnp.float32),
        lax.psum_scatter(
            grad_output.astype(jnp.bfloat16), "ctx", scatter_dimension=0, tiled=True
        ).astype(jnp.float32),
        lax.psum_scatter(
            grad_gate.astype(jnp.bfloat16), "ctx", scatter_dimension=0, tiled=True
        ).astype(jnp.float32),
        lax.psum_scatter(
            grad_up.astype(jnp.bfloat16), "ctx", scatter_dimension=0, tiled=True
        ).astype(jnp.float32),
        lax.psum_scatter(
            grad_down.astype(jnp.bfloat16), "ctx", scatter_dimension=0, tiled=True
        ).astype(jnp.float32),
    )
    shared_query, shared_key, shared_value, shared_output, shared_gate, shared_up, shared_down = (
        lax.all_gather(summed_query.astype(jnp.bfloat16), "ctx", axis=0, tiled=True).astype(
            summed_query.dtype
        ),
        lax.all_gather(summed_key.astype(jnp.bfloat16), "ctx", axis=0, tiled=True).astype(
            summed_key.dtype
        ),
        lax.all_gather(summed_value.astype(jnp.bfloat16), "ctx", axis=0, tiled=True).astype(
            summed_value.dtype
        ),
        lax.all_gather(summed_output.astype(jnp.bfloat16), "ctx", axis=0, tiled=True).astype(
            summed_output.dtype
        ),
        lax.all_gather(summed_gate.astype(jnp.bfloat16), "ctx", axis=0, tiled=True).astype(
            summed_gate.dtype
        ),
        lax.all_gather(summed_up.astype(jnp.bfloat16), "ctx", axis=0, tiled=True).astype(
            summed_up.dtype
        ),
        lax.all_gather(summed_down.astype(jnp.bfloat16), "ctx", axis=0, tiled=True).astype(
            summed_down.dtype
        ),
    )
    gain_attn, gain_query, gain_key, gain_ffn = lax.psum(
        (
            jnp.sum(attn_terms, axis=0),
            jnp.sum(query_terms, axis=(0, 1)),
            jnp.sum(key_terms, axis=(0, 1)),
            jnp.sum(ffn_terms, axis=0),
        ),
        ("ctx", "tp"),
    )
    return (
        block_output,
        input_grad,
        gain_attn,
        shared_query,
        shared_key,
        shared_value,
        gain_query,
        gain_key,
        shared_output,
        gain_ffn,
        shared_gate,
        shared_up,
        shared_down,
    )


def solution(mesh):
    return jax.shard_map(
        per_device,
        mesh=mesh,
        in_specs=(
            P(("ctx", "tp"), None),
            P(),
            P(),
            P(None, "tp"),
            P(None, "tp"),
            P(None, "tp"),
            P(),
            P(),
            P("tp", None),
            P(),
            P(None, "tp"),
            P(None, "tp"),
            P("tp", None),
            P(("ctx", "tp"), None),
        ),
        out_specs=(
            P(("ctx", "tp"), None),
            P(("ctx", "tp"), None),
            P(),
            P(None, "tp"),
            P(None, "tp"),
            P(None, "tp"),
            P(),
            P(),
            P("tp", None),
            P(),
            P(None, "tp"),
            P(None, "tp"),
            P("tp", None),
        ),
        check_vma=False,
    )
```

profile of v0, /device:TPU:28, one launch (start us, length us, event | category | flops | bytes accessed | tf_op | source)
XLA Modules:
  0.0 2340.4 jit_solution(7701935905645911283)
XLA Ops:
  12.5 8.1 all_gather.39
  24.0 1.8 convolution_convert_fusion.10
  28.4 115.8 %all-gather.7.cloned.1.call-done = bf16[4096,128]{0,1:T(8,128)(2,1)} async-done(((bf16[128,128]{0,1:T(8,128)(2,1)}), bf16[4096,128]{0,1:T(8,128)(2,1)}) %all-gather.7.cloned.1.call-update) | async-done | bytes 1048592 | tf_op jit(solution)/shard_map/all_gather | solution.py:192
  144.2 2.3 copy.129
  146.5 140.7 %all-gather.9.cloned.1.call-done = bf16[4096,128]{1,0:T(8,128)(2,1)} async-done(((bf16[128,128]{1,0:T(8,128)(2,1)}), bf16[4096,128]{1,0:T(8,128)(2,1)}) %all-gather.9.cloned.1.call-update) | async-done | bytes 1048592 | tf_op jit(solution)/shard_map/all_gather | solution.py:193
  287.2 57.9 %while.42 = (s32[]{:T(128)}, f32[2,2,2,64]{3,2,1,0:T(2,128)}, f32[2,2,2,64]{3,2,1,0:T(2,128)}, f32[2,2,2,64,64]{4,3,2,1,0:T(8,128)S(1)}, s32[32]{0:T(128)}, /*in...) while((s32[]{:T(128)}, f32[2,2,2,64]{3,2,1,0:T(2,128)}, ...), condition=%wide.region_8.9_spmd.clone, body=%wide.region_4.8_spmd.clone.sunk | while | flops 34854156 | bytes 4363595 | solution.py:207
  346.3 2.0 convolution_convert_fusion.8
  348.4 7.5 all_gather.43
  355.9 31.0 %reduce-scatter.17.cloned.1.call-done = bf16[32,1024]{1,0:T(8,128)(2,1)} async-done(((bf16[128,1024]{1,0:T(8,128)(2,1)}), bf16[32,1024]{1,0:T(8,128)(2,1)}) %reduce-scatter.17.cloned.1.call-update) | async-done | bytes 65552 | tf_op jit(solution)/shard_map/reduce_scatter | solution.py:91
  389.0 7.3 all_gather.42
  396.3 2.3 fusion.69
  399.2 1.7 multiply_convert_fusion
  402.8 1.6 fusion.31
  405.1 25.7 %reduce-scatter.21.cloned.1.call-done = bf16[32,1024]{1,0:T(8,128)(2,1)} async-done(((bf16[128,1024]{1,0:T(8,128)(2,1)}), bf16[32,1024]{1,0:T(8,128)(2,1)}) %reduce-scatter.21.cloned.1.call-update) | async-done | bytes 65552 | tf_op jit(solution)/shard_map/reduce_scatter | solution.py:91
  433.4 7.3 all_gather.44
  445.4 84.9 %while.43 = (s32[]{:T(128)}, f32[2,64,2,2,64]{1,4,3,2,0:T(8,128)}, bf16[4096,128]{0,1:T(8,128)(2,1)}, bf16[4096,128]{1,0:T(8,128)(2,1)}, bf16[4096,128]{1,0:T(8,...) while((s32[]{:T(128)}, f32[2,64,2,2,64]{1,4,3,2,0:T(8,128)}, ...), condition=%wide.region_17.18_spmd.clone, body=%wide.region_15.17_spmd.clone.sunk | while | flops 85019400 | bytes 8570337 | solution.py:297
  449.3 1.6 constant_dynamic-update-slice_fusion.6
  451.7 1.9 fusion.164
  459.8 1.6 constant_dynamic-update-slice_fusion.6
  462.3 2.0 fusion.164
  470.4 1.6 constant_dynamic-update-slice_fusion.6
  472.9 2.0 fusion.164
  481.1 1.6 constant_dynamic-update-slice_fusion.6
  483.5 2.0 fusion.164
  491.7 1.6 constant_dynamic-update-slice_fusion.6
  494.1 2.0 fusion.164
  502.3 1.6 constant_dynamic-update-slice_fusion.6
  504.8 2.0 fusion.164
  512.9 1.6 constant_dynamic-update-slice_fusion.6
  515.4 2.0 fusion.164
  523.6 1.6 constant_dynamic-update-slice_fusion.6
  526.0 2.0 fusion.164
  530.3 2.3 copy.157
  533.5 2.2 convolution_convert_fusion.2
  535.8 2.2 convolution_convert_fusion.1
  539.5 1.7 copy.141
  549.0 126.1 %reduce-scatter.39.cloned.1.call-done = bf16[128,128]{1,0:T(8,128)(2,1)} async-done(((bf16[4096,128]{1,0:T(8,128)(2,1)}), bf16[128,128]{1,0:T(8,128)(2,1)}) %reduce-scatter.39.cloned.1.call-update) | async-done | bytes 32784
  676.0 158.8 %reduce-scatter.23.cloned.1.call-done = bf16[128,128]{1,0:T(8,128)(2,1)} async-done(((bf16[4096,128]{1,0:T(8,128)(2,1)}), bf16[128,128]{1,0:T(8,128)(2,1)}) %reduce-scatter.23.cloned.1.call-update) | async-done | bytes 32784 | tf_op jit(solution)/shard_map/reduce_scatter | solution.py:304
  834.8 1.7 convolution_convert_fusion.5
  841.0 1.9 fusion.30
  844.3 2.2 convolution_convert_fusion
  846.6 108.5 %fusion = bf16[40,1024]{1,0:T(8,128)(2,1)S(1)} fusion(bf16[1152,1024]{1,0:T(8,128)(2,1)} %convolution_convert_fusion), kind=kCustom, calls=%all-reduce-scatter | all-reduce-scatter fusion | flops 1310721 | bytes 2441728
  955.1 9.3 collective-permute-start.2
  964.4 3.0 collective-permute-start.1
  967.4 3.6 collective-permute-start
  971.1 6.0 collective-permute-start.3
  979.8 19.4 reduce-scatter.35.cloned.1.call-done
  999.3 164.6 %reduce-scatter.37.cloned.1.call-done = bf16[32,1152]{1,0:T(8,128)(2,1)} async-done(((bf16[1024,1152]{1,0:T(8,128)(2,1)}), bf16[32,1152]{1,0:T(8,128)(2,1)}) %reduce-scatter.37.cloned.1.call-update) | async-done | bytes 73744 | tf_op jit(solution)/shard_map/reduce_scatter | solution.py:345
  1164.0 159.6 %reduce-scatter.33.cloned.1.call-done = bf16[8,1024]{1,0:T(8,128)(2,1)} async-done(((bf16[256,1024]{1,0:T(8,128)(2,1)}), bf16[8,1024]{1,0:T(8,128)(2,1)}) %reduce-scatter.33.cloned.1.call-update) | async-done | bytes 16400 | tf_op jit(solution)/shard_map/reduce_scatter | solution.py:339
  1323.6 77.8 %all_gather.48 = bf16[256,1024]{1,0:T(8,128)(2,1)S(1)} all-gather(bf16[8,1024]{1,0:T(8,128)(2,1)} %reduce-scatter.33.cloned.1.call-done), channel_id=1, replica_groups=mesh['ctx'=32,'tp'=4] {'ctx'}, dimensions={0}, use_global_device_ids=true | all-gather | bytes 540672 | tf_op jit(solution)/shard_map/all_gather | solution.py:362
  1402.5 80.7 %reduce-scatter.27.cloned.1.call-done = bf16[32,256]{1,0:T(8,128)(2,1)} async-done(((bf16[1024,256]{1,0:T(8,128)(2,1)}), bf16[32,256]{1,0:T(8,128)(2,1)}) %reduce-scatter.27.cloned.1.call-update) | async-done | bytes 16400 | tf_op jit(solution)/shard_map/reduce_scatter | solution.py:330
  1483.2 78.0 %all_gather.45 = bf16[1024,256]{1,0:T(8,128)(2,1)S(1)} all-gather(bf16[32,256]{1,0:T(8,128)(2,1)} %reduce-scatter.27.cloned.1.call-done), channel_id=1, replica_groups=mesh['ctx'=32,'tp'=4] {'ctx'}, dimensions={0}, use_global_device_ids=true | all-gather | bytes 540672 | tf_op jit(solution)/shard_map/all_gather | solution.py:353
  1562.4 79.1 %reduce-scatter.31.cloned.1.call-done = bf16[32,128]{1,0:T(8,128)(2,1)} async-done(((bf16[1024,128]{1,0:T(8,128)(2,1)}), bf16[32,128]{1,0:T(8,128)(2,1)}) %reduce-scatter.31.cloned.1.call-update) | async-done | bytes 8208 | tf_op jit(solution)/shard_map/reduce_scatter | solution.py:336
  1641.5 76.6 %all_gather.47 = bf16[1024,128]{1,0:T(8,128)(2,1)S(1)} all-gather(bf16[32,128]{1,0:T(8,128)(2,1)} %reduce-scatter.31.cloned.1.call-done), channel_id=1, replica_groups=mesh['ctx'=32,'tp'=4] {'ctx'}, dimensions={0}, use_global_device_ids=true | all-gather | bytes 270336 | tf_op jit(solution)/shard_map/all_gather | solution.py:359
  1718.9 80.8 %reduce-scatter.29.cloned.1.call-done = bf16[32,128]{1,0:T(8,128)(2,1)} async-done(((bf16[1024,128]{1,0:T(8,128)(2,1)}), bf16[32,128]{1,0:T(8,128)(2,1)}) %reduce-scatter.29.cloned.1.call-update) | async-done | bytes 8208 | tf_op jit(solution)/shard_map/reduce_scatter | solution.py:333
  1799.7 76.8 %all_gather.46 = bf16[1024,128]{1,0:T(8,128)(2,1)S(1)} all-gather(bf16[32,128]{1,0:T(8,128)(2,1)} %reduce-scatter.29.cloned.1.call-done), channel_id=1, replica_groups=mesh['ctx'=32,'tp'=4] {'ctx'}, dimensions={0}, use_global_device_ids=true | all-gather | bytes 270336 | tf_op jit(solution)/shard_map/all_gather | solution.py:356
  1878.4 80.9 %all-reduce.2 = (f32[1024]{0:T(1024)}, f32[64]{0:T(128)}, f32[64]{0:T(128)}, f32[1024]{0:T(1024)}) all-reduce(f32[1024]{0:T(1024)S(1)} %get-tuple-element.789, f32[64]{0:T(128)S(1)} %reduce_sum.204, f32[64]{0:T(128)S(1)} %reduce_sum.207, f32[1024]{0:T(1024)S(1)} %copy-done.50), channel_id=1, replica_groups=mesh['ctx'=32,'tp'=4] {'ctx','tp'}, use_global_device_ids=true, to_apply=%region_25.26 | all-reduce | flops 2176 | bytes 17408 | tf_op jit(solution)/shard_map/psum | solution.py:375
  1959.3 1.7 fusion.41
  1961.0 57.1 %all-gather.15.cloned.1.call-done = bf16[32,36,1024]{2,1,0:T(8,128)(2,1)} async-done(((bf16[1,36,1024]{2,1,0:T(8,128)(2,1)}), bf16[32,36,1024]{2,1,0:T(8,128)(2,1)}) %all-gather.15.cloned.1.call-update) | async-done | bytes 2359312 | tf_op jit(solution)/shard_map/all_gather | solution.py:371
  2018.1 4.5 reshape.566
  2022.6 151.5 %all-gather.11.cloned.1.call-done = bf16[1024,1152]{1,0:T(8,128)(2,1)} async-done(((bf16[32,1152]{1,0:T(8,128)(2,1)}), bf16[1024,1152]{1,0:T(8,128)(2,1)}) %all-gather.11.cloned.1.call-update) | async-done | bytes 2359312 | tf_op jit(solution)/shard_map/all_gather | solution.py:365
  2174.0 4.2 convert_element_type.217
  2178.2 151.6 %all-gather.13.cloned.1.call-done = bf16[1024,1152]{1,0:T(8,128)(2,1)} async-done(((bf16[32,1152]{1,0:T(8,128)(2,1)}), bf16[1024,1152]{1,0:T(8,128)(2,1)}) %all-gather.13.cloned.1.call-update) | async-done | bytes 2359312 | tf_op jit(solution)/shard_map/all_gather | solution.py:368
  2329.8 4.2 convert_element_type.219
  (680 shorter events, 160.3 us)
Async XLA Ops:
  7.2 392.0 %copy-start = (bf16[1152,1024]{1,0:T(8,128)(2,1)S(1)}, bf16[1152,1024]{1,0:T(8,128)(2,1)}, u32[]{:S(2)}) copy-start(bf16[1152,1024]{1,0:T(8,128)(2,1)} %param.30) | copy-start | bytes 7077892
  7.2 20.2 copy-start.55
  7.2 137.0 %all-gather.7.cloned.1.call-start = ((), (), s32[]{:S(2)}) async-start(), calls=%async_computation.12 | async-start | bytes 1081344 | tf_op jit(solution)/shard_map/all_gather | solution.py:192
  20.6 125.9 %copy-start.2 = (bf16[128,1024]{1,0:T(8,128)(2,1)}, bf16[128,1024]{1,0:T(8,128)(2,1)S(1)}, u32[]{:S(2)}) copy-start(bf16[128,1024]{1,0:T(8,128)(2,1)S(1)} %all_gather.39) | copy-start | bytes 786436
  22.1 124.4 %copy-start.39 = (f32[128,32]{0,1:T(8,128)}, f32[128,32]{0,1:T(8,128)S(1)}, u32[]{:S(2)}) copy-start(f32[128,32]{0,1:T(8,128)S(1)} %get-tuple-element.868) | copy-start | bytes 49156
  22.1 124.4 %copy-start.41 = (f32[128,32]{0,1:T(8,128)}, f32[128,32]{0,1:T(8,128)S(1)}, u32[]{:S(2)}) copy-start(f32[128,32]{0,1:T(8,128)S(1)} %get-tuple-element.869) | copy-start | bytes 49156
  24.0 263.2 %all-gather.9.cloned.1.call-start = ((), (), s32[]{:S(2)}) async-start(), calls=%async_computation.13 | async-start | bytes 1081344 | tf_op jit(solution)/shard_map/all_gather | solution.py:193
  25.8 361.1 %reduce-scatter.17.cloned.1.call-start = ((), (), s32[]{:S(2)}) async-start(), calls=%async_computation.14 | async-start | bytes 327680 | tf_op jit(solution)/shard_map/reduce_scatter | solution.py:91
  27.2 260.0 %copy-start.22 = (f32[128,256]{1,0:T(8,128)}, f32[128,256]{1,0:T(8,128)S(1)}, u32[]{:S(2)}) copy-start(f32[128,256]{1,0:T(8,128)S(1)} %fusion.67) | copy-start | bytes 393220
  27.3 259.9 %copy-start.16 = (f32[128,256]{0,1:T(8,128)}, f32[128,256]{0,1:T(8,128)S(1)}, u32[]{:S(2)}) copy-start(f32[128,256]{0,1:T(8,128)S(1)} %copy.128) | copy-start | bytes 393220
  28.3 258.9 %copy-start.31 = (bf16[2,64,2,2,64]{1,0,4,3,2:T(2,128)(2,1)}, bf16[2,64,2,2,64]{1,0,4,3,2:T(2,128)(2,1)S(1)}, u32[]{:S(2)}) copy-start(bf16[2,64,2,2,64]{1,0,4,3,2:T(2,128)(2,1)S(1)} %constant_dynamic-update-slice_fusion.2) | copy-start | bytes 196612
  345.1 43.0 %copy-start.11 = (bf16[32,1024]{1,0:T(8,128)(2,1)S(1)}, bf16[32,1024]{1,0:T(8,128)(2,1)}, u32[]{:S(2)}) copy-start(bf16[32,1024]{1,0:T(8,128)(2,1)} %param.18) | copy-start | bytes 196612
  345.1 43.0 %copy-start.45 = (f32[1024]{0:T(1024)S(1)}, f32[1024]{0:T(1024)}, u32[]{:S(2)}) copy-start(f32[1024]{0:T(1024)} %param.27) | copy-start | bytes 12292
  348.3 82.5 %reduce-scatter.21.cloned.1.call-start = ((), (), s32[]{:S(2)}) async-start(), calls=%async_computation.16 | async-start | bytes 327680 | tf_op jit(solution)/shard_map/reduce_scatter | solution.py:91
  355.9 43.3 %copy-start.27 = (bf16[128,1024]{1,0:T(8,128)(2,1)}, bf16[128,1024]{1,0:T(8,128)(2,1)S(1)}, u32[]{:S(2)}) copy-start(bf16[128,1024]{1,0:T(8,128)(2,1)S(1)} %all_gather.43) | copy-start | bytes 786436
  386.9 11.7 copy-start.5
  388.1 11.1 copy-start.53
  401.9 29.0 %copy-start.18 = (bf16[32,1024]{1,0:T(8,128)(2,1)S(1)}, bf16[32,1024]{1,0:T(8,128)(2,1)}, u32[]{:S(2)}) copy-start(bf16[32,1024]{1,0:T(8,128)(2,1)} %reduce-scatter.17.cloned.1.call-done) | copy-start | bytes 196612
  404.4 270.7 %reduce-scatter.39.cloned.1.call-start = ((), (), s32[]{:S(2)}) async-start(), calls=%async_computation.28 | async-start | bytes 1081344
  404.5 40.9 %copy-start.46 = (s32[64]{0:T(128)S(1)}, s32[64]{0:T(128)}, u32[]{:S(2)}) copy-start(s32[64]{0:T(128)} %get-tuple-element.1180) | copy-start | bytes 772
  432.4 10.3 copy-start.62
  461.7 4.8 copy-start.60
  472.4 4.8 copy-start.60
  483.0 4.8 copy-start.60
  493.6 4.8 copy-start.60
  532.7 302.1 %reduce-scatter.23.cloned.1.call-start = ((), (), s32[]{:S(2)}) async-start(), calls=%async_computation.17 | async-start | bytes 1081344 | tf_op jit(solution)/shard_map/reduce_scatter | solution.py:304
  533.3 466.0 %reduce-scatter.35.cloned.1.call-start = ((), (), s32[]{:S(2)}) async-start(), calls=%async_computation.23 | async-start | bytes 2433024 | tf_op jit(solution)/shard_map/reduce_scatter | solution.py:342
  535.8 5.4 copy-start.4
  535.8 628.1 %reduce-scatter.37.cloned.1.call-start = ((), (), s32[]{:S(2)}) async-start(), calls=%async_computation.25 | async-start | bytes 2433024 | tf_op jit(solution)/shard_map/reduce_scatter | solution.py:345
  538.0 5.2 copy-start.14
  538.0 5.2 copy-start.37
  538.0 6.4 copy-start.40
  538.0 6.4 copy-start.42
  538.0 6.4 copy-start.17
  538.1 8.0 copy-start.23
  538.1 9.1 copy-start.3
  538.1 785.5 %reduce-scatter.33.cloned.1.call-start = ((), (), s32[]{:S(2)}) async-start(), calls=%async_computation.22 | async-start | bytes 540672 | tf_op jit(solution)/shard_map/reduce_scatter | solution.py:339
  544.3 292.3 %copy-start.30 = (f32[128,128]{0,1:T(8,128)S(1)}, f32[128,128]{0,1:T(8,128)}, u32[]{:S(2)}) copy-start(f32[128,128]{0,1:T(8,128)} %copy-done.29) | copy-start | bytes 196612
  544.3 292.4 %copy-start.52 = (f32[128,2]{0,1:T(2,128)S(1)}, f32[128,2]{0,1:T(2,128)}, u32[]{:S(2)}) copy-start(f32[128,2]{0,1:T(2,128)} %copy-done.51) | copy-start | bytes 3076
  544.3 938.9 %reduce-scatter.27.cloned.1.call-start = ((), (), s32[]{:S(2)}) async-start(), calls=%async_computation.19 | async-start | bytes 540672 | tf_op jit(solution)/shard_map/reduce_scatter | solution.py:330
  545.3 293.3 %copy-start.15 = (bf16[1024,256]{1,0:T(8,128)(2,1)S(1)}, bf16[1024,256]{1,0:T(8,128)(2,1)}, u32[]{:S(2)}) copy-start(bf16[1024,256]{1,0:T(8,128)(2,1)} %param.21) | copy-start | bytes 1572868
  547.2 289.5 %copy-start.33 = (bf16[128,256]{1,0:T(8,128)(2,1)}, bf16[128,256]{1,0:T(8,128)(2,1)S(1)}, u32[]{:S(2)}) copy-start(bf16[128,256]{1,0:T(8,128)(2,1)S(1)} %get-tuple-element.851) | copy-start | bytes 196612
  548.3 1093.1 %reduce-scatter.31.cloned.1.call-start = ((), (), s32[]{:S(2)}) async-start(), calls=%async_computation.21 | async-start | bytes 270336 | tf_op jit(solution)/shard_map/reduce_scatter | solution.py:336
  836.5 963.2 %reduce-scatter.29.cloned.1.call-start = ((), (), s32[]{:S(2)}) async-start(), calls=%async_computation.20 | async-start | bytes 270336 | tf_op jit(solution)/shard_map/reduce_scatter | solution.py:333
  836.7 6.3 copy-start.24
  838.6 1038.7 %reduce-scatter.25.cloned.1.call-start = ((), (), s32[]{:S(2)}) async-start(), calls=%async_computation.18 | async-start | bytes 327680 | tf_op jit(solution)/shard_map/reduce_scatter | solution.py:91
  843.0 1116.3 %reduce-scatter.19.cloned.1.call-start = ((), (), s32[]{:S(2)}) async-start(), calls=%async_computation.15 | async-start | bytes 327680 | tf_op jit(solution)/shard_map/reduce_scatter | solution.py:91
  844.3 132.8 %copy-start.64 = (u32[128]{0:T(128)S(1)}, u32[128]{0:T(128)}, u32[]{:S(2)}) copy-start(u32[128]{0:T(128)} %constant.431) | copy-start | bytes 1540
  846.5 1171.6 %all-gather.15.cloned.1.call-start = ((), (), s32[]{:S(2)}) async-start(), calls=%async_computation.27 | async-start | bytes 2703360 | tf_op jit(solution)/shard_map/all_gather | solution.py:371
  955.1 23.3 collective-permute-start.2
  964.4 14.0 collective-permute-start.1
  967.4 11.0 collective-permute-start
  971.1 7.3 collective-permute-start.3
  979.8 1194.2 %all-gather.11.cloned.1.call-start = ((), (), s32[]{:S(2)}) async-start(), calls=%async_computation.24 | async-start | bytes 2433024 | tf_op jit(solution)/shard_map/all_gather | solution.py:365
  999.2 1330.5 %all-gather.13.cloned.1.call-start = ((), (), s32[]{:S(2)}) async-start(), calls=%async_computation.26 | async-start | bytes 2433024 | tf_op jit(solution)/shard_map/all_gather | solution.py:368
  1402.5 474.8 %copy-start.12 = (bf16[32,1024]{1,0:T(8,128)(2,1)S(1)}, bf16[32,1024]{1,0:T(8,128)(2,1)}, u32[]{:S(2)}) copy-start(bf16[32,1024]{1,0:T(8,128)(2,1)} %param.18) | copy-start | bytes 196612
  1402.5 474.8 %copy-start.47 = (f32[1024]{0:T(1024)S(1)}, f32[1024]{0:T(1024)}, u32[]{:S(2)}) copy-start(f32[1024]{0:T(1024)} %param.20) | copy-start | bytes 12292
  1402.5 474.8 %copy-start.58 = (f32[32]{0:T(128)S(1)}, f32[32]{0:T(128)}, u32[]{:S(2)}) copy-start(f32[32]{0:T(128)} %copy-done.57) | copy-start | bytes 388
  1402.5 475.9 %copy-start.50 = (f32[1024]{0:T(1024)S(1)}, f32[1024]{0:T(1024)}, u32[]{:S(2)}) copy-start(f32[1024]{0:T(1024)} %get-tuple-element.787) | copy-start | bytes 12292
  1402.5 556.8 %copy-start.19 = (bf16[32,1024]{1,0:T(8,128)(2,1)S(1)}, bf16[32,1024]{1,0:T(8,128)(2,1)}, u32[]{:S(2)}) copy-start(bf16[32,1024]{1,0:T(8,128)(2,1)} %reduce-scatter.17.cloned.1.call-done) | copy-start | bytes 196612
  1402.5 556.8 %copy-start.34 = (bf16[32,1024]{1,0:T(8,128)(2,1)S(1)}, bf16[32,1024]{1,0:T(8,128)(2,1)}, u32[]{:S(2)}) copy-start(bf16[32,1024]{1,0:T(8,128)(2,1)} %param.31) | copy-start | bytes 196612
  1402.5 556.8 %copy-start.35 = (bf16[32,1024]{1,0:T(8,128)(2,1)S(1)}, bf16[32,1024]{1,0:T(8,128)(2,1)}, u32[]{:S(2)}) copy-start(bf16[32,1024]{1,0:T(8,128)(2,1)} %reduce-scatter.21.cloned.1.call-done) | copy-start | bytes 196612
  1402.5 556.8 %copy-start.54 = (f32[32]{0:T(128)S(1)}, f32[32]{0:T(128)}, u32[]{:S(2)}) copy-start(f32[32]{0:T(128)} %copy-done.53) | copy-start | bytes 388
  1402.5 556.8 %copy-start.63 = (f32[32]{0:T(128)S(1)}, f32[32]{0:T(128)}, u32[]{:S(2)}) copy-start(f32[32]{0:T(128)} %copy-done.62) | copy-start | bytes 388
  (50 other events, 139.7 us)
Sparse Core Ops, SparseCore 0:
  24.1 120.0 all-gather.6
  146.4 140.7 all-gather.8
  348.4 38.4 reduce-scatter.16
  404.5 26.2 reduce-scatter.20
  532.8 142.2 reduce-scatter.38
  678.0 156.7 reduce-scatter.22
  837.7 161.4 reduce-scatter.34
  1002.2 161.6 reduce-scatter.36
  1166.8 156.7 reduce-scatter.32
  1326.5 156.7 reduce-scatter.26
  1485.6 155.8 reduce-scatter.30
  1643.8 155.8 reduce-scatter.28
  1802.3 41.5 reduce-scatter.24
  1846.4 26.2 reduce-scatter.18
  1874.7 143.3 all-gather.14
  2019.6 154.4 all-gather.10
  2175.5 154.1 all-gather.12
where the time goes:
time: 2350 us; the launch traced here: 2340 us
  waiting for transfers between devices  1540 us (66%)
  blocking collectives  529 us (23%)
  local copies, waits for them, and re-layouts  91.3 us (4%)
  other arithmetic  68.1 us (3%)
  matrix products  67.9 us (3%)
    reduce_scatter x1, waiting for transfers between devices, per_device(): lax.psum_scatter(grad_up.astype(jnp.bfloat16), 'ctx', scatter_dimension=0...  165 us
    reduce_scatter x1, waiting for transfers between devices, per_device(): lax.psum_scatter(grad_output.astype(jnp.bfloat16), 'ctx', scatter_dimensi...  160 us
    reduce_scatter x1, waiting for transfers between devices, per_device(): lax.psum_scatter(value_grad_all.astype(jnp.bfloat16), 'ctx', scatter_dime...  159 us
    all_gather x1, waiting for transfers between devices, per_device(): lax.all_gather(summed_up.astype(jnp.bfloat16), 'ctx', axis=0, tiled=True)  152 us
    all_gather x1, waiting for transfers between devices, per_device(): lax.all_gather(summed_gate.astype(jnp.bfloat16), 'ctx', axis=0, tiled=True)  151 us
    all_gather x1, waiting for transfers between devices, per_device(): lax.all_gather(values_own, 'ctx', axis=0, tiled=True)  141 us
    unnamed x22, waiting for transfers between devices  127 us
    all_gather x1, waiting for transfers between devices, per_device(): lax.all_gather(keys_own, 'ctx', axis=0, tiled=True)  116 us
  transfers between devices with their start and end apart: 21, of which 16 were waited for; matrix products, arithmetic and copies ran while one was open for 7% of the time, Pallas kernels for 0%

commit v1 on v0

--- a/solution.py
+++ b/solution.py
@@ -188,10 +188,10 @@
     )
     span_count = place_count // shard_span
     span_rows = shard_span * rows_total
-    whole_keys, whole_values = (
-        lax.all_gather(keys_own, "ctx", axis=0, tiled=True),
-        lax.all_gather(values_own, "ctx", axis=0, tiled=True),
-    )
+    whole_kv = lax.all_gather(
+        jnp.concatenate([keys_own, values_own], axis=1), "ctx", axis=0, tiled=True
+    )
+    whole_keys, whole_values = whole_kv[:, :kv_width], whole_kv[:, kv_width:]
 
     def whole_forward(span_index, softmax_state):
         first_anchor = span_index * shard_span
@@ -222,7 +222,7 @@
         jnp.dot(activated, down_weight, preferred_element_type=jnp.float32)
     )
     grad_rows = gather_rows(cotangent)
-    grad_down = jnp.dot(activated.T, grad_rows, preferred_element_type=jnp.float32)
+    grad_down_t = jnp.dot(grad_rows.T, activated, preferred_element_type=jnp.float32)
     grad_act = jnp.dot(grad_rows, down_weight.T, preferred_element_type=jnp.float32)
     grad_gate_pre = (grad_act * up_pre * gate_sig * (1.0 + gate_pre * (1.0 - gate_sig))).astype(
         jnp.bfloat16
@@ -237,7 +237,7 @@
     through_two, ffn_terms = rms_backward(residual_mid, inverse_two, ffn_gain, grad_normed_two)
     grad_mid = cotangent.astype(jnp.float32) + through_two
     grad_mid_rows = gather_rows(grad_mid.astype(jnp.bfloat16))
-    grad_output = jnp.dot(attn_low.T, grad_mid_rows, preferred_element_type=jnp.float32)
+    grad_output_t = jnp.dot(grad_mid_rows.T, attn_low, preferred_element_type=jnp.float32)
     grad_attn = jnp.dot(grad_mid_rows, output_weight.T, preferred_element_type=jnp.float32).astype(
         jnp.bfloat16
     )
@@ -297,14 +297,13 @@
     query_acc, key_grad_all, value_grad_all = lax.fori_loop(
         0, span_count, whole_backward, start_grads
     )
-    grad_keys_flat, grad_values_flat = (
-        lax.psum_scatter(
-            key_grad_all.astype(jnp.bfloat16), "ctx", scatter_dimension=0, tiled=True
-        ).astype(jnp.float32),
-        lax.psum_scatter(
-            value_grad_all.astype(jnp.bfloat16), "ctx", scatter_dimension=0, tiled=True
-        ).astype(jnp.float32),
-    )
+    grad_kv_flat = lax.psum_scatter(
+        jnp.concatenate([key_grad_all, value_grad_all], axis=1).astype(jnp.bfloat16),
+        "ctx",
+        scatter_dimension=0,
+        tiled=True,
+    ).astype(jnp.float32)
+    grad_keys_flat, grad_values_flat = grad_kv_flat[:, :kv_width], grad_kv_flat[:, kv_width:]
     grad_query_rot = query_acc.reshape(rows_total, query_heads, head_dim)
     grad_key_rot = grad_keys_flat.reshape(rows_total, kv_heads, head_dim)
     grad_query_raw, query_terms = rms_backward(
@@ -326,61 +325,29 @@
     )
     through_one, attn_terms = rms_backward(residual_in, inverse_one, attn_gain, grad_normed_one)
     input_grad = grad_mid + through_one
-    summed_query, summed_key, summed_value, summed_output, summed_gate, summed_up, summed_down = (
-        lax.psum_scatter(
-            grad_query.astype(jnp.bfloat16), "ctx", scatter_dimension=0, tiled=True
-        ).astype(jnp.float32),
-        lax.psum_scatter(
-            grad_key.astype(jnp.bfloat16), "ctx", scatter_dimension=0, tiled=True
-        ).astype(jnp.float32),
-        lax.psum_scatter(
-            grad_value.astype(jnp.bfloat16), "ctx", scatter_dimension=0, tiled=True
-        ).astype(jnp.float32),
-        lax.psum_scatter(
-            grad_output.astype(jnp.bfloat16), "ctx", scatter_dimension=0, tiled=True
-        ).astype(jnp.float32),
-        lax.psum_scatter(
-            grad_gate.astype(jnp.bfloat16), "ctx", scatter_dimension=0, tiled=True
-        ).astype(jnp.float32),
-        lax.psum_scatter(
-            grad_up.astype(jnp.bfloat16), "ctx", scatter_dimension=0, tiled=True
-        ).astype(jnp.float32),
-        lax.psum_scatter(
-            grad_down.astype(jnp.bfloat16), "ctx", scatter_dimension=0, tiled=True
-        ).astype(jnp.float32),
-    )
-    shared_query, shared_key, shared_value, shared_output, shared_gate, shared_up, shared_down = (
-        lax.all_gather(summed_query.astype(jnp.bfloat16), "ctx", axis=0, tiled=True).astype(
-            summed_query.dtype
-        ),
-        lax.all_gather(summed_key.astype(jnp.bfloat16), "ctx", axis=0, tiled=True).astype(
-            summed_key.dtype
-        ),
-        lax.all_gather(summed_value.astype(jnp.bfloat16), "ctx", axis=0, tiled=True).astype(
-            summed_value.dtype
-        ),
-        lax.all_gather(summed_output.astype(jnp.bfloat16), "ctx", axis=0, tiled=True).astype(
-            summed_output.dtype
-        ),
-        lax.all_gather(summed_gate.astype(jnp.bfloat16), "ctx", axis=0, tiled=True).astype(
-            summed_gate.dtype
-        ),
-        lax.all_gather(summed_up.astype(jnp.bfloat16), "ctx", axis=0, tiled=True).astype(
-            summed_up.dtype
-        ),
-        lax.all_gather(summed_down.astype(jnp.bfloat16), "ctx", axis=0, tiled=True).astype(
-            summed_down.dtype
-        ),
-    )
-    gain_attn, gain_query, gain_key, gain_ffn = lax.psum(
-        (
-            jnp.sum(attn_terms, axis=0),
-            jnp.sum(query_terms, axis=(0, 1)),
-            jnp.sum(key_terms, axis=(0, 1)),
-            jnp.sum(ffn_terms, axis=0),
-        ),
-        ("ctx", "tp"),
-    )
+    weight_parts = (grad_query, grad_key, grad_value, grad_output_t, grad_gate, grad_up, grad_down_t)
+    widths = [part.shape[1] for part in weight_parts]
+    summed = lax.psum(
+        jnp.concatenate([part.astype(jnp.bfloat16) for part in weight_parts], axis=1), "ctx"
+    ).astype(jnp.float32)
+    offsets = [sum(widths[:k]) for k in range(len(widths) + 1)]
+    shared_query, shared_key, shared_value, output_t, shared_gate, shared_up, down_t = (
+        summed[:, offsets[k] : offsets[k + 1]] for k in range(len(widths))
+    )
+    shared_output = output_t.T
+    shared_down = down_t.T
+    gain_parts = (
+        jnp.sum(attn_terms, axis=0),
+        jnp.sum(query_terms, axis=(0, 1)),
+        jnp.sum(key_terms, axis=(0, 1)),
+        jnp.sum(ffn_terms, axis=0),
+    )
+    gain_sizes = [part.shape[0] for part in gain_parts]
+    gains = lax.psum(jnp.concatenate(gain_parts), ("ctx", "tp"))
+    gain_attn = gains[: gain_sizes[0]]
+    gain_query = gains[gain_sizes[0] : gain_sizes[0] + gain_sizes[1]]
+    gain_key = gains[gain_sizes[0] + gain_sizes[1] : gain_sizes[0] + gain_sizes[1] + gain_sizes[2]]
+    gain_ffn = gains[gain_sizes[0] + gain_sizes[1] + gain_sizes[2] :]
     return (
         block_output,
         input_grad,

time: 2350 us -> 1110 us (0.47)
  waiting for transfers between devices: 1540 us -> 675 us
  blocking collectives: 529 us -> 97.3 us
  local copies, waits for them, and re-layouts: 91.3 us -> 142 us
  matrix products: 67.9 us -> 98.2 us
    reduce_scatter x7 -> x0, waiting for transfers between devices: 743 us -> none  [the longest x1 165 us: per_device(): lax.psum_scatter(grad_up.astype(jnp.bfloat16), 'ctx', scatter_dimension=0...]
    all_gather x5 -> x1, waiting for transfers between devices: 617 us -> 126 us  [per_device(): lax.all_gather(jnp.concatenate([keys_own, values_own], axis=1), 'ctx', ax...]
    psum x0 -> x1, waiting for transfers between devices: none -> 346 us  [per_device(): lax.psum(jnp.concatenate([part.astype(jnp.bfloat16) for part in weight_pa...]
    all_gather x4 -> x0, blocking collectives: 309 us -> none  [the longest x1 78 us: per_device(): lax.all_gather(summed_query.astype(jnp.bfloat16), 'ctx', axis=0, tiled=True)]
    unnamed x1 -> x0, blocking collectives: 109 us -> none
    unnamed x22 -> x8, waiting for transfers between devices: 127 us -> 131 us
  transfers between devices with their start and end apart: 21 -> 7, of which waited for: 16 -> 6; matrix products, arithmetic and copies ran while one was open for 7% -> 3% of each run, Pallas kernels for 0% -> 0%
where the time goes in v1:
time: 1110 us
  waiting for transfers between devices  675 us (61%)
  local copies, waits for them, and re-layouts  142 us (13%)
  matrix products  98.2 us (9%)
  blocking collectives  97.3 us (9%)
  other arithmetic  75.8 us (7%)
  between operations  15.6 us (1%)
    psum x1, waiting for transfers between devices, per_device(): lax.psum(jnp.concatenate([part.astype(jnp.bfloat16) for part in weight_pa...  346 us
    unnamed x8, waiting for transfers between devices  131 us
    all_gather x1, waiting for transfers between devices, per_device(): lax.all_gather(jnp.concatenate([keys_own, values_own], axis=1), 'ctx', ax...  126 us
    reduce_scatter x4, waiting for transfers between devices, reduce_rows(): lax.psum_scatter(partial_rows.astype(jnp.bfloat16), 'tp', scatter_dimensi...  72.1 us
    psum x1, blocking collectives, per_device(): gains = lax.psum(jnp.concatenate(gain_parts), ('ctx', 'tp'))  66.9 us
    all_gather x4, blocking collectives, gather_rows(): return lax.all_gather(rows_low, 'tp', axis=0, tiled=True)  30.4 us
    unnamed x130, local copies, waits for them, and re-layouts  23.1 us
  transfers between devices with their start and end apart: 7, of which 6 were waited for; matrix products, arithmetic and copies ran while one was open for 3% of the time, Pallas kernels for 0%

profile of v1, /device:TPU:28, one launch (start us, length us, event | category | flops | bytes accessed | tf_op | source)
XLA Modules:
  0.0 1106.3 jit_solution(10083355769534350955)
XLA Ops:
  9.3 8.1 all_gather.15
  28.1 125.8 %all-gather.2.cloned.1.call-done = bf16[4096,256]{0,1:T(8,128)(2,1)} async-done(((bf16[128,256]{0,1:T(8,128)(2,1)}), bf16[4096,256]{0,1:T(8,128)(2,1)}) %all-gather.2.cloned.1.call-update) | async-done | bytes 2097168 | tf_op jit(solution)/shard_map/all_gather | solution.py:191
  153.9 3.1 fusion.74
  156.9 2.3 copy.169
  159.2 2.3 copy.171
  161.5 67.0 %while.42 = (s32[]{:T(128)}, f32[2,2,2,64]{3,2,1,0:T(2,128)S(1)}, f32[2,2,2,64]{3,2,1,0:T(2,128)}, f32[2,2,2,64,64]{4,3,2,1,0:T(8,128)}, s32[32]{0:T(128)}, /*in...) while((s32[]{:T(128)}, f32[2,2,2,64]{3,2,1,0:T(2,128)S(1)}, ...), condition=%wide.region_8.9_spmd.clone, body=%wide.region_4.8_spmd.clone.sunk | while | flops 34854156 | bytes 4371807 | solution.py:207
  166.7 1.7 convolution_add_fusion.5
  174.9 2.0 convolution_add_fusion.5
  183.4 2.0 convolution_add_fusion.5
  191.9 2.0 convolution_add_fusion.5
  200.3 2.0 convolution_add_fusion.5
  208.8 2.0 convolution_add_fusion.5
  217.3 2.0 convolution_add_fusion.5
  225.8 2.0 convolution_add_fusion.5
  229.9 2.0 convolution_convert_fusion.8
  231.9 7.5 all_gather.18
  239.5 21.2 %reduce-scatter.8.cloned.1.call-done = bf16[32,1024]{1,0:T(8,128)(2,1)} async-done(((bf16[128,1024]{1,0:T(8,128)(2,1)}), bf16[32,1024]{1,0:T(8,128)(2,1)}) %reduce-scatter.8.cloned.1.call-update) | async-done | bytes 65552 | tf_op jit(solution)/shard_map/reduce_scatter | solution.py:91
  262.7 7.3 all_gather.17
  270.0 2.3 fusion.78
  272.3 2.3 fusion.79
  274.6 1.7 multiply_convert_fusion
  277.4 1.6 fusion.34
  280.4 25.0 %reduce-scatter.12.cloned.1.call-done = bf16[32,1024]{1,0:T(8,128)(2,1)} async-done(((bf16[128,1024]{1,0:T(8,128)(2,1)}), bf16[32,1024]{1,0:T(8,128)(2,1)}) %reduce-scatter.12.cloned.1.call-update) | async-done | bytes 65552 | tf_op jit(solution)/shard_map/reduce_scatter | solution.py:91
  305.4 1.5 fusion.49
  307.9 7.5 all_gather.19
  319.8 127.7 %while.43 = (s32[]{:T(128)}, f32[2,64,2,2,64]{1,4,3,2,0:T(8,128)}, bf16[4096,128]{0,1:T(8,128)(2,1)}, bf16[4096,128]{0,1:T(8,128)(2,1)}, bf16[4096,128]{1,0:T(8,...) while((s32[]{:T(128)}, f32[2,64,2,2,64]{1,4,3,2,0:T(8,128)}, ...), condition=%wide.region_17.18_spmd.clone, body=%wide.region_15.17_spmd.clone.sunk | while | flops 85019400 | bytes 8299901 | solution.py:297
  327.7 1.8 convolution_bitcast_fusion.7
  333.8 1.9 fusion.172
  343.5 1.8 convolution_bitcast_fusion.7
  349.7 2.0 fusion.172
  359.5 1.8 convolution_bitcast_fusion.7
  365.6 2.0 fusion.172
  375.5 1.8 convolution_bitcast_fusion.7
  381.6 2.0 fusion.172
  391.5 1.8 convolution_bitcast_fusion.7
  397.6 2.0 fusion.172
  407.4 1.8 convolution_bitcast_fusion.7
  413.6 2.0 fusion.172
  423.4 1.8 convolution_bitcast_fusion.7
  429.5 2.0 fusion.172
  439.4 1.8 convolution_bitcast_fusion.7
  445.5 2.0 fusion.172
  447.5 3.1 pad_maximum_fusion
  450.6 4.1 copy.208
  461.6 1.4 pad_maximum_fusion.1
  463.7 1.7 copy.179
  465.4 1.6 multiply_reduce_fusion
  468.8 130.8 %reduce-scatter.16.cloned.1.call-done = bf16[128,256]{1,0:T(8,128)(2,1)} async-done(((bf16[4096,256]{1,0:T(8,128)(2,1)}), bf16[128,256]{1,0:T(8,128)(2,1)}) %reduce-scatter.16.cloned.1.call-update) | async-done | bytes 65552
  603.2 1.4 convolution_add_fusion.2
  604.5 1.9 fusion.33
  606.5 2.2 convolution_convert_fusion.7
  614.1 2.2 fusion.30
  616.3 2.3 fusion.29
  618.6 2.3 fusion.32
  621.9 25.8 %reduce-scatter.14.cloned.1.call-done = bf16[32,1024]{1,0:T(8,128)(2,1)} async-done(((bf16[128,1024]{1,0:T(8,128)(2,1)}), bf16[32,1024]{1,0:T(8,128)(2,1)}) %reduce-scatter.14.cloned.1.call-update) | async-done | bytes 65552 | tf_op jit(solution)/shard_map/reduce_scatter | solution.py:91
  648.8 66.9 %psum.14 = f32[2176]{0:T(1024)S(1)} all-reduce(f32[2176]{0:T(1024)S(1)} %concatenate.46), channel_id=1, replica_groups=mesh['ctx'=32,'tp'=4] {'ctx','tp'}, use_global_device_ids=true, to_apply=%region_29.30 | all-reduce | flops 2176 | bytes 17408 | tf_op jit(solution)/shard_map/psum | solution.py:346
  716.9 1.7 fusion.44
  718.6 345.8 %all-reduce.2.cloned.1.call-done = bf16[1024,4224]{1,0:T(8,128)(2,1)} async-done(((bf16[1024,4224]{1,0:T(8,128)(2,1)}), bf16[1024,4224]{1,0:T(8,128)(2,1)}) %all-reduce.2.cloned.1.call-update) | async-done | bytes 8650768 | tf_op jit(solution)/shard_map/psum | solution.py:330
  1064.4 10.5 convert_element_type.179
  1074.9 4.8 slice_bitcast_fusion
  1081.1 6.0 copy.194
  1088.4 6.9 fusion.72
  1095.3 2.1 fusion.73
  1097.4 2.1 slice.111
  (620 shorter events, 194.1 us)
Async XLA Ops:
  7.2 267.4 %copy-start = (bf16[1152,1024]{1,0:T(8,128)(2,1)S(1)}, bf16[1152,1024]{1,0:T(8,128)(2,1)}, u32[]{:S(2)}) copy-start(bf16[1152,1024]{1,0:T(8,128)(2,1)} %param.30) | copy-start | bytes 7077892
  7.2 146.7 %all-gather.2.cloned.1.call-start = ((), (), s32[]{:S(2)}) async-start(), calls=%async_computation.5 | async-start | bytes 2162688 | tf_op jit(solution)/shard_map/all_gather | solution.py:191
  17.5 141.7 %copy-start.3 = (bf16[128,1024]{1,0:T(8,128)(2,1)}, bf16[128,1024]{1,0:T(8,128)(2,1)S(1)}, u32[]{:S(2)}) copy-start(bf16[128,1024]{1,0:T(8,128)(2,1)S(1)} %all_gather.15) | copy-start | bytes 786436
  18.8 6.1 copy-start.31
  18.8 5.3 copy-start.52
  23.3 4.4 copy-start.43
  23.3 4.4 copy-start.45
  24.8 235.9 %reduce-scatter.8.cloned.1.call-start = ((), (), s32[]{:S(2)}) async-start(), calls=%async_computation.6 | async-start | bytes 327680 | tf_op jit(solution)/shard_map/reduce_scatter | solution.py:91
  26.2 135.3 %copy-start.24 = (f32[128,256]{1,0:T(8,128)}, f32[128,256]{1,0:T(8,128)S(1)}, u32[]{:S(2)}) copy-start(f32[128,256]{1,0:T(8,128)S(1)} %fusion.77) | copy-start | bytes 393220
  26.3 135.2 %copy-start.17 = (f32[128,256]{0,1:T(8,128)}, f32[128,256]{0,1:T(8,128)S(1)}, u32[]{:S(2)}) copy-start(f32[128,256]{0,1:T(8,128)S(1)} %copy.168) | copy-start | bytes 393220
  28.0 133.5 %copy-start.32 = (bf16[2,64,2,2,64]{1,0,4,3,2:T(2,128)(2,1)}, bf16[2,64,2,2,64]{1,0,4,3,2:T(2,128)(2,1)S(1)}, u32[]{:S(2)}) copy-start(bf16[2,64,2,2,64]{1,0,4,3,2:T(2,128)(2,1)S(1)} %constant_dynamic-update-slice_fusion.2) | copy-start | bytes 196612
  228.4 46.2 %copy-start.41 = (f32[2,2,2,64]{3,2,1,0:T(2,128)}, f32[2,2,2,64]{3,2,1,0:T(2,128)S(1)}, u32[]{:S(2)}) copy-start(f32[2,2,2,64]{3,2,1,0:T(2,128)S(1)} %get-tuple-element.609) | copy-start | bytes 6148
  231.9 73.5 %reduce-scatter.12.cloned.1.call-start = ((), (), s32[]{:S(2)}) async-start(), calls=%async_computation.8 | async-start | bytes 327680 | tf_op jit(solution)/shard_map/reduce_scatter | solution.py:91
  239.4 35.2 %copy-start.29 = (bf16[128,1024]{1,0:T(8,128)(2,1)}, bf16[128,1024]{1,0:T(8,128)(2,1)S(1)}, u32[]{:S(2)}) copy-start(bf16[128,1024]{1,0:T(8,128)(2,1)S(1)} %all_gather.18) | copy-start | bytes 786436
  261.7 45.3 %copy-start.53 = (f32[32]{0:T(128)}, f32[32]{0:T(128)S(1)}, u32[]{:S(2)}) copy-start(f32[32]{0:T(128)S(1)} %add_rsqrt_fusion.2) | copy-start | bytes 388
  272.2 4.2 copy-start.7
  274.6 2.7 copy-start.8
  276.4 2.7 copy-start.33
  276.4 3.4 copy-start.42
  276.4 29.1 %copy-start.11 = (bf16[32,1024]{1,0:T(8,128)(2,1)S(1)}, bf16[32,1024]{1,0:T(8,128)(2,1)}, u32[]{:S(2)}) copy-start(bf16[32,1024]{1,0:T(8,128)(2,1)} %param.18) | copy-start | bytes 196612
  276.4 29.1 %copy-start.20 = (bf16[32,1024]{1,0:T(8,128)(2,1)S(1)}, bf16[32,1024]{1,0:T(8,128)(2,1)}, u32[]{:S(2)}) copy-start(bf16[32,1024]{1,0:T(8,128)(2,1)} %reduce-scatter.8.cloned.1.call-done) | copy-start | bytes 196612
  276.4 29.1 %copy-start.47 = (f32[1024]{0:T(1024)S(1)}, f32[1024]{0:T(1024)}, u32[]{:S(2)}) copy-start(f32[1024]{0:T(1024)} %param.27) | copy-start | bytes 12292
  276.4 30.6 %copy-start.36 = (bf16[32,1024]{1,0:T(8,128)(2,1)S(1)}, bf16[32,1024]{1,0:T(8,128)(2,1)}, u32[]{:S(2)}) copy-start(bf16[32,1024]{1,0:T(8,128)(2,1)} %param.31) | copy-start | bytes 196612
  276.4 39.7 %copy-start.19 = (bf16[256,1024]{1,0:T(8,128)(2,1)S(1)}, bf16[256,1024]{1,0:T(8,128)(2,1)}, u32[]{:S(2)}) copy-start(bf16[256,1024]{1,0:T(8,128)(2,1)} %param.26) | copy-start | bytes 1572868
  276.4 40.1 %copy-start.5 = (f32[2,2,2,64,64]{4,3,2,1,0:T(8,128)S(1)}, f32[2,2,2,64,64]{4,3,2,1,0:T(8,128)}, u32[]{:S(2)}) copy-start(f32[2,2,2,64,64]{4,3,2,1,0:T(8,128)} %get-tuple-element.607) | copy-start | bytes 393220
  279.0 320.6 %reduce-scatter.16.cloned.1.call-start = ((), (), s32[]{:S(2)}) async-start(), calls=%async_computation.11 | async-start | bytes 2162688
  307.0 12.8 %copy-start.58 = (f32[32]{0:T(128)}, f32[32]{0:T(128)S(1)}, u32[]{:S(2)}) copy-start(f32[32]{0:T(128)S(1)} %broadcast_multiply_fusion.3) | copy-start | bytes 388
  321.3 3.0 copy-start.2
  337.1 3.0 copy-start.2
  353.1 3.0 copy-start.2
  369.1 3.0 copy-start.2
  385.1 3.0 copy-start.2
  401.0 3.0 copy-start.2
  417.0 3.0 copy-start.2
  433.0 3.0 copy-start.2
  447.5 11.3 %copy-start.6 = (f32[2,64,2,2,64]{1,4,3,2,0:T(8,128)S(1)}, f32[2,64,2,2,64]{1,4,3,2,0:T(8,128)}, u32[]{:S(2)}) copy-start(f32[2,64,2,2,64]{1,4,3,2,0:T(8,128)} %get-tuple-element.610) | copy-start | bytes 393220
  450.6 10.2 copy-start.44
  450.6 11.0 copy-start.18
  450.6 14.8 %copy-start.25 = (f32[128,256]{1,0:T(8,128)S(1)}, f32[128,256]{1,0:T(8,128)}, u32[]{:S(2)}) copy-start(f32[128,256]{1,0:T(8,128)} %copy-done.24) | copy-start | bytes 393220
  450.6 17.1 %copy-start.16 = (bf16[1024,256]{1,0:T(8,128)(2,1)S(1)}, bf16[1024,256]{1,0:T(8,128)(2,1)}, u32[]{:S(2)}) copy-start(bf16[1024,256]{1,0:T(8,128)(2,1)} %param.21) | copy-start | bytes 1572868
  454.8 192.9 %reduce-scatter.14.cloned.1.call-start = ((), (), s32[]{:S(2)}) async-start(), calls=%async_computation.9 | async-start | bytes 327680 | tf_op jit(solution)/shard_map/reduce_scatter | solution.py:91
  461.6 147.2 %copy-start.4 = (bf16[128,1024]{1,0:T(8,128)(2,1)S(1)}, bf16[128,1024]{1,0:T(8,128)(2,1)}, u32[]{:S(2)}) copy-start(bf16[128,1024]{1,0:T(8,128)(2,1)} %copy-done.3) | copy-start | bytes 786436
  463.7 145.4 %copy-start.15 = (bf16[128,1024]{1,0:T(8,128)(2,1)S(1)}, bf16[128,1024]{1,0:T(8,128)(2,1)}, u32[]{:S(2)}) copy-start(bf16[128,1024]{1,0:T(8,128)(2,1)} %copy-done.14) | copy-start | bytes 786436
  467.1 142.1 %copy-start.40 = (bf16[128,256]{1,0:T(8,128)(2,1)S(1)}, bf16[128,256]{1,0:T(8,128)(2,1)}, u32[]{:S(2)}) copy-start(bf16[128,256]{1,0:T(8,128)(2,1)} %copy-done.39) | copy-start | bytes 196612
  468.8 140.0 %copy-start.35 = (bf16[128,256]{1,0:T(8,128)(2,1)S(1)}, bf16[128,256]{1,0:T(8,128)(2,1)}, u32[]{:S(2)}) copy-start(bf16[128,256]{1,0:T(8,128)(2,1)} %copy-done.34) | copy-start | bytes 196612
  606.4 4.8 copy-start.46
  606.5 110.4 %reduce-scatter.10.cloned.1.call-start = ((), (), s32[]{:S(2)}) async-start(), calls=%async_computation.7 | async-start | bytes 327680 | tf_op jit(solution)/shard_map/reduce_scatter | solution.py:91
  608.7 5.4 copy-start.10
  608.7 5.4 copy-start.23
  608.7 455.7 %all-reduce.2.cloned.1.call-start = ((), (), s32[]{:S(2)}) async-start(), calls=%async_computation.10 | async-start | bytes 17301504 | tf_op jit(solution)/shard_map/psum | solution.py:330
  609.7 6.6 copy-start.28
  611.1 7.6 copy-start.26
  611.1 7.6 copy-start.30
  621.0 26.7 %copy-start.12 = (bf16[32,1024]{1,0:T(8,128)(2,1)S(1)}, bf16[32,1024]{1,0:T(8,128)(2,1)}, u32[]{:S(2)}) copy-start(bf16[32,1024]{1,0:T(8,128)(2,1)} %param.18) | copy-start | bytes 196612
  621.0 26.7 %copy-start.49 = (f32[1024]{0:T(1024)S(1)}, f32[1024]{0:T(1024)}, u32[]{:S(2)}) copy-start(f32[1024]{0:T(1024)} %param.20) | copy-start | bytes 12292
  621.0 26.7 %copy-start.56 = (f32[32]{0:T(128)S(1)}, f32[32]{0:T(128)}, u32[]{:S(2)}) copy-start(f32[32]{0:T(128)} %copy-done.55) | copy-start | bytes 388
  621.0 27.7 %copy-start.51 = (f32[1024]{0:T(1024)S(1)}, f32[1024]{0:T(1024)}, u32[]{:S(2)}) copy-start(f32[1024]{0:T(1024)} %get-tuple-element.852) | copy-start | bytes 12292
  621.0 95.9 %copy-start.21 = (bf16[32,1024]{1,0:T(8,128)(2,1)S(1)}, bf16[32,1024]{1,0:T(8,128)(2,1)}, u32[]{:S(2)}) copy-start(bf16[32,1024]{1,0:T(8,128)(2,1)} %reduce-scatter.8.cloned.1.call-done) | copy-start | bytes 196612
  621.0 95.9 %copy-start.37 = (bf16[32,1024]{1,0:T(8,128)(2,1)S(1)}, bf16[32,1024]{1,0:T(8,128)(2,1)}, u32[]{:S(2)}) copy-start(bf16[32,1024]{1,0:T(8,128)(2,1)} %param.31) | copy-start | bytes 196612
  621.0 95.9 %copy-start.38 = (bf16[32,1024]{1,0:T(8,128)(2,1)S(1)}, bf16[32,1024]{1,0:T(8,128)(2,1)}, u32[]{:S(2)}) copy-start(bf16[32,1024]{1,0:T(8,128)(2,1)} %reduce-scatter.12.cloned.1.call-done) | copy-start | bytes 196612
  621.0 95.9 %copy-start.48 = (f32[1024]{0:T(1024)S(1)}, f32[1024]{0:T(1024)}, u32[]{:S(2)}) copy-start(f32[1024]{0:T(1024)} %param.27) | copy-start | bytes 12292
  621.0 95.8 %copy-start.54 = (f32[32]{0:T(128)S(1)}, f32[32]{0:T(128)}, u32[]{:S(2)}) copy-start(f32[32]{0:T(128)} %copy-done.53) | copy-start | bytes 388
  621.1 95.8 %copy-start.59 = (f32[32]{0:T(128)S(1)}, f32[32]{0:T(128)}, u32[]{:S(2)}) copy-start(f32[32]{0:T(128)} %copy-done.58) | copy-start | bytes 388
  1088.4 11.0 copy-start.1
  (17 other events, 23.0 us)
Sparse Core Ops, SparseCore 0:
  24.9 128.9 all-gather.1
  232.0 28.6 reduce-scatter.7
  279.1 26.2 reduce-scatter.11
  454.9 144.6 reduce-scatter.15
  606.6 41.0 reduce-scatter.13
  650.7 26.3 reduce-scatter.9
  679.8 384.6 all-reduce.1

commit v2 on v1

--- a/solution.py
+++ b/solution.py
@@ -1,9 +1,184 @@
+import functools
 import math
 
 import jax
 import jax.numpy as jnp
 from jax import lax
+from jax.experimental import pallas as pl
+from jax.experimental.pallas import tpu as pltpu
 from jax.sharding import PartitionSpec as P
+
+MESH = pl.DeviceIdType.MESH
+VMEM_LIMIT = 60 * 1024 * 1024
+
+
+def _enter(n, me, peer_axis):
+    barrier = pltpu.get_barrier_semaphore()
+    for k in range(1, n):
+        pl.semaphore_signal(
+            barrier, 1, device_id=(lax.rem(me + k, n), peer_axis), device_id_type=MESH
+        )
+    pl.semaphore_wait(barrier, n - 1)
+
+
+def _gather_kernel(n, part_ref, out_ref, send_sem, recv_sem):
+    me = lax.axis_index("ctx")
+    other = lax.axis_index("tp")
+    rows = part_ref.shape[0]
+    _enter(n, me, other)
+    copies = []
+    for k in range(1, n):
+        copy = pltpu.make_async_remote_copy(
+            src_ref=part_ref,
+            dst_ref=out_ref.at[pl.ds(pl.multiple_of(me * rows, rows), rows)],
+            send_sem=send_sem.at[k],
+            recv_sem=recv_sem.at[k],
+            device_id=(lax.rem(me + k, n), other),
+            device_id_type=MESH,
+        )
+        copy.start()
+        copies.append(copy)
+    out_ref[pl.ds(pl.multiple_of(me * rows, rows), rows), :] = part_ref[...]
+    for k in range(1, n):
+        source = lax.rem(me + n - k, n)
+        pltpu.make_async_remote_copy(
+            src_ref=part_ref,
+            dst_ref=out_ref.at[pl.ds(pl.multiple_of(source * rows, rows), rows)],
+            send_sem=send_sem.at[k],
+            recv_sem=recv_sem.at[k],
+            device_id=(source, other),
+            device_id_type=MESH,
+        ).wait_recv()
+    for copy in copies:
+        copy.wait_send()
+
+
+def ctx_gather(part, n, collective_id):
+    rows, cols = part.shape
+    return pl.pallas_call(
+        functools.partial(_gather_kernel, n),
+        out_shape=jax.ShapeDtypeStruct((n * rows, cols), part.dtype),
+        in_specs=[pl.BlockSpec(memory_space=pltpu.VMEM)],
+        out_specs=pl.BlockSpec(memory_space=pltpu.VMEM),
+        scratch_shapes=[pltpu.SemaphoreType.DMA((n,)), pltpu.SemaphoreType.DMA((n,))],
+        compiler_params=pltpu.CompilerParams(
+            collective_id=collective_id, has_side_effects=True, vmem_limit_bytes=VMEM_LIMIT
+        ),
+    )(part)
+
+
+def _scatter_sum(n, me, other, whole_ref, held, send_sem, recv_sem, rows):
+    copies = []
+    for k in range(1, n):
+        target = lax.rem(me + k, n)
+        copy = pltpu.make_async_remote_copy(
+            src_ref=whole_ref.at[pl.ds(pl.multiple_of(target * rows, rows), rows)],
+            dst_ref=held.at[k],
+            send_sem=send_sem.at[k],
+            recv_sem=recv_sem.at[k],
+            device_id=(target, other),
+            device_id_type=MESH,
+        )
+        copy.start()
+        copies.append(copy)
+    total = whole_ref[pl.ds(pl.multiple_of(me * rows, rows), rows), :].astype(jnp.float32)
+    for k in range(1, n):
+        source = lax.rem(me + n - k, n)
+        pltpu.make_async_remote_copy(
+            src_ref=whole_ref.at[pl.ds(0, rows)],
+            dst_ref=held.at[k],
+            send_sem=send_sem.at[k],
+            recv_sem=recv_sem.at[k],
+            device_id=(source, other),
+            device_id_type=MESH,
+        ).wait_recv()
+        total = total + held[k].astype(jnp.float32)
+    for copy in copies:
+        copy.wait_send()
+    return total
+
+
+def _scatter_kernel(n, whole_ref, out_ref, held, send_sem, recv_sem):
+    me = lax.axis_index("ctx")
+    other = lax.axis_index("tp")
+    rows = out_ref.shape[0]
+    _enter(n, me, other)
+    out_ref[...] = _scatter_sum(n, me, other, whole_ref, held, send_sem, recv_sem, rows)
+
+
+def ctx_scatter(whole, n, collective_id):
+    rows, cols = whole.shape[0] // n, whole.shape[1]
+    return pl.pallas_call(
+        functools.partial(_scatter_kernel, n),
+        out_shape=jax.ShapeDtypeStruct((rows, cols), jnp.float32),
+        in_specs=[pl.BlockSpec(memory_space=pltpu.VMEM)],
+        out_specs=pl.BlockSpec(memory_space=pltpu.VMEM),
+        scratch_shapes=[
+            pltpu.VMEM((n, rows, cols), whole.dtype),
+            pltpu.SemaphoreType.DMA((n,)),
+            pltpu.SemaphoreType.DMA((n,)),
+        ],
+        compiler_params=pltpu.CompilerParams(
+            collective_id=collective_id, has_side_effects=True, vmem_limit_bytes=VMEM_LIMIT
+        ),
+    )(whole)
+
+
+def _sum_kernel(n, whole_ref, out_ref, held, mine, send_sem, recv_sem, send_back, recv_back):
+    me = lax.axis_index("ctx")
+    other = lax.axis_index("tp")
+    rows = whole_ref.shape[0] // n
+    _enter(n, me, other)
+    mine[...] = _scatter_sum(n, me, other, whole_ref, held, send_sem, recv_sem, rows).astype(
+        mine.dtype
+    )
+    copies = []
+    for k in range(1, n):
+        copy = pltpu.make_async_remote_copy(
+            src_ref=mine,
+            dst_ref=out_ref.at[pl.ds(pl.multiple_of(me * rows, rows), rows)],
+            send_sem=send_back.at[k],
+            recv_sem=recv_back.at[k],
+            device_id=(lax.rem(me + k, n), other),
+            device_id_type=MESH,
+        )
+        copy.start()
+        copies.append(copy)
+    out_ref[pl.ds(pl.multiple_of(me * rows, rows), rows), :] = mine[...]
+    for k in range(1, n):
+        source = lax.rem(me + n - k, n)
+        pltpu.make_async_remote_copy(
+            src_ref=mine,
+            dst_ref=out_ref.at[pl.ds(pl.multiple_of(source * rows, rows), rows)],
+            send_sem=send_back.at[k],
+            recv_sem=recv_back.at[k],
+            device_id=(source, other),
+            device_id_type=MESH,
+        ).wait_recv()
+    for copy in copies:
+        copy.wait_send()
+
+
+def ctx_sum(whole, n, collective_id):
+    rows, cols = whole.shape[0] // n, whole.shape[1]
+    return pl.pallas_call(
+        functools.partial(_sum_kernel, n),
+        out_shape=jax.ShapeDtypeStruct(whole.shape, whole.dtype),
+        in_specs=[pl.BlockSpec(memory_space=pltpu.VMEM)],
+        out_specs=pl.BlockSpec(memory_space=pltpu.VMEM),
+        scratch_shapes=[
+            pltpu.VMEM((n, rows, cols), whole.dtype),
+            pltpu.VMEM((rows, cols), whole.dtype),
+            pltpu.SemaphoreType.DMA((n,)),
+            pltpu.SemaphoreType.DMA((n,)),
+            pltpu.SemaphoreType.DMA((n,)),
+            pltpu.SemaphoreType.DMA((n,)),
+        ],
+        compiler_params=pltpu.CompilerParams(
+            collective_id=collective_id, has_side_effects=True, vmem_limit_bytes=VMEM_LIMIT
+        ),
+    )(whole)
+
 
 EPS = 1e-05
 THETA = 1000000.0
@@ -188,9 +363,7 @@
     )
     span_count = place_count // shard_span
     span_rows = shard_span * rows_total
-    whole_kv = lax.all_gather(
-        jnp.concatenate([keys_own, values_own], axis=1), "ctx", axis=0, tiled=True
-    )
+    whole_kv = ctx_gather(jnp.concatenate([keys_own, values_own], axis=1), place_count, 0)
     whole_keys, whole_values = whole_kv[:, :kv_width], whole_kv[:, kv_width:]
 
     def whole_forward(span_index, softmax_state):
@@ -297,12 +470,11 @@
     query_acc, key_grad_all, value_grad_all = lax.fori_loop(
         0, span_count, whole_backward, start_grads
     )
-    grad_kv_flat = lax.psum_scatter(
+    grad_kv_flat = ctx_scatter(
         jnp.concatenate([key_grad_all, value_grad_all], axis=1).astype(jnp.bfloat16),
-        "ctx",
-        scatter_dimension=0,
-        tiled=True,
-    ).astype(jnp.float32)
+        place_count,
+        1,
+    )
     grad_keys_flat, grad_values_flat = grad_kv_flat[:, :kv_width], grad_kv_flat[:, kv_width:]
     grad_query_rot = query_acc.reshape(rows_total, query_heads, head_dim)
     grad_key_rot = grad_keys_flat.reshape(rows_total, kv_heads, head_dim)
@@ -327,8 +499,10 @@
     input_grad = grad_mid + through_one
     weight_parts = (grad_query, grad_key, grad_value, grad_output_t, grad_gate, grad_up, grad_down_t)
     widths = [part.shape[1] for part in weight_parts]
-    summed = lax.psum(
-        jnp.concatenate([part.astype(jnp.bfloat16) for part in weight_parts], axis=1), "ctx"
+    summed = ctx_sum(
+        jnp.concatenate([part.astype(jnp.bfloat16) for part in weight_parts], axis=1),
+        place_count,
+        2,
     ).astype(jnp.float32)
     offsets = [sum(widths[:k]) for k in range(len(widths) + 1)]
     shared_query, shared_key, shared_value, output_t, shared_gate, shared_up, down_t = (

time: 1110 us -> 1010 us (0.910)
  waiting for transfers between devices: 675 us -> 43.8 us
  Pallas kernels: 0 us -> 531 us
  local copies, waits for them, and re-layouts: 142 us -> 125 us
    pallas_call x0 -> x3, Pallas kernels: none -> 531 us  [the longest x1 419 us: ctx_sum(): pl.pallas_call(functools.partial(_sum_kernel, n), out_shape=jax.ShapeDtyp...]
    psum x1 -> x0, waiting for transfers between devices: 346 us -> none  [per_device(): lax.psum(jnp.concatenate([part.astype(jnp.bfloat16) for part in weight_pa...]
    unnamed x8 -> x4, waiting for transfers between devices: 131 us -> 0.07 us
    all_gather x1 -> x0, waiting for transfers between devices: 126 us -> none  [per_device(): lax.all_gather(jnp.concatenate([keys_own, values_own], axis=1), 'ctx', ax...]
    reduce_scatter x4, waiting for transfers between devices: 72.1 us -> 43.7 us  [reduce_rows(): lax.psum_scatter(partial_rows.astype(jnp.bfloat16), 'tp', scatter_dimensi...]
    unnamed x130 -> x122, local copies, waits for them, and re-layouts: 23.1 us -> 11 us
  transfers between devices with their start and end apart: 7 -> 4, of which waited for: 6 -> 2; matrix products, arithmetic and copies ran while one was open for 3% -> 5% of each run, Pallas kernels for 0% -> 42%
where the time goes in v2:
time: 1010 us; the launch traced here: 998 us
  Pallas kernels  531 us (53%)
  local copies, waits for them, and re-layouts  125 us (12%)
  matrix products  102 us (10%)
  blocking collectives  101 us (10%)
  other arithmetic  77.5 us (8%)
  waiting for transfers between devices  43.8 us (4%)
  between operations  15.3 us (2%)
    pallas_call x1, Pallas kernels, ctx_sum(): pl.pallas_call(functools.partial(_sum_kernel, n), out_shape=jax.ShapeDtyp...  419 us
    psum x1, blocking collectives, per_device(): gains = lax.psum(jnp.concatenate(gain_parts), ('ctx', 'tp'))  68.4 us
    pallas_call x1, Pallas kernels, ctx_scatter(): pl.pallas_call(functools.partial(_scatter_kernel, n), out_shape=jax.Shape...  59 us
    pallas_call x1, Pallas kernels, ctx_gather(): pl.pallas_call(functools.partial(_gather_kernel, n), out_shape=jax.ShapeD...  53.1 us
    reduce_scatter x4, waiting for transfers between devices, reduce_rows(): lax.psum_scatter(partial_rows.astype(jnp.bfloat16), 'tp', scatter_dimensi...  43.7 us
    all_gather x4, blocking collectives, gather_rows(): return lax.all_gather(rows_low, 'tp', axis=0, tiled=True)  32.4 us
  transfers between devices with their start and end apart: 4, of which 2 were waited for; matrix products, arithmetic and copies ran while one was open for 5% of the time, Pallas kernels for 42%

profile of v2, /device:TPU:28, one launch (start us, length us, event | category | flops | bytes accessed | tf_op | source)
XLA Modules:
  0.0 997.9 jit_solution(14684248704899410184)
XLA Ops:
  9.4 8.1 all_gather.12
  24.9 53.1 %shard_map.237 = bf16[4096,256]{1,0:T(8,128)(2,1)} custom-call(bf16[128,256]{1,0:T(8,128)(2,1)} %pad_maximum_fusion.2.part_ref), custom_call_target="tpu_custom_call" | custom-call | tf_op jit(solution)/shard_map/pallas_call | solution.py:58
  78.1 3.0 fusion.76
  83.1 76.6 %while.42 = (s32[]{:T(128)}, f32[2,2,2,64]{3,2,1,0:T(2,128)}, f32[2,2,2,64]{3,2,1,0:T(2,128)}, f32[2,2,2,64,64]{4,3,2,1,0:T(8,128)}, s32[32]{0:T(128)}, /*index=...) while((s32[]{:T(128)}, f32[2,2,2,64]{3,2,1,0:T(2,128)}, ...), condition=%wide.region_8.9_spmd.clone, body=%wide.region_4.8_spmd.clone.sunk | while | flops 34854156 | bytes 4371807 | solution.py:380
  88.3 1.7 convolution_add_fusion.5
  97.8 2.0 convolution_add_fusion.5
  107.6 2.0 convolution_add_fusion.5
  117.4 2.0 convolution_add_fusion.5
  127.1 2.0 convolution_add_fusion.5
  136.9 2.0 convolution_add_fusion.5
  146.7 2.0 convolution_add_fusion.5
  156.4 2.0 convolution_add_fusion.5
  161.1 2.0 convolution_convert_fusion.8
  163.2 9.5 all_gather.14
  172.7 20.6 %reduce-scatter.5.cloned.1.call-done = bf16[32,1024]{1,0:T(8,128)(2,1)} async-done(((bf16[128,1024]{1,0:T(8,128)(2,1)}), bf16[32,1024]{1,0:T(8,128)(2,1)}) %reduce-scatter.5.cloned.1.call-update) | async-done | bytes 65552 | tf_op jit(solution)/shard_map/reduce_scatter | solution.py:266
  195.3 7.3 all_gather.13
  202.6 2.3 fusion.80
  204.9 2.3 fusion.81
  207.2 1.7 multiply_convert_fusion
  210.0 1.6 fusion.38
  215.0 23.1 %reduce-scatter.9.cloned.1.call-done = bf16[32,1024]{1,0:T(8,128)(2,1)} async-done(((bf16[128,1024]{1,0:T(8,128)(2,1)}), bf16[32,1024]{1,0:T(8,128)(2,1)}) %reduce-scatter.9.cloned.1.call-update) | async-done | bytes 65552 | tf_op jit(solution)/shard_map/reduce_scatter | solution.py:266
  240.6 7.5 all_gather.15
  252.3 125.7 %while.43 = (s32[]{:T(128)}, f32[2,64,2,2,64]{1,4,3,2,0:T(8,128)}, bf16[4096,128]{1,0:T(8,128)(2,1)}, bf16[4096,128]{1,0:T(8,128)(2,1)}, bf16[4096,128]{1,0:T(8,...) while((s32[]{:T(128)}, f32[2,64,2,2,64]{1,4,3,2,0:T(8,128)}, ...), condition=%wide.region_17.18_spmd.clone, body=%wide.region_15.17_spmd.clone.sunk | while | flops 85019400 | bytes 7775613 | solution.py:470
  260.2 1.8 convolution_bitcast_fusion.7
  264.4 1.6 constant_dynamic-update-slice_fusion.5
  266.1 1.9 fusion.174
  275.8 1.8 convolution_bitcast_fusion.7
  280.0 1.6 constant_dynamic-update-slice_fusion.5
  281.7 2.0 fusion.174
  291.5 1.8 convolution_bitcast_fusion.7
  295.8 1.6 constant_dynamic-update-slice_fusion.5
  297.4 2.0 fusion.174
  307.2 1.8 convolution_bitcast_fusion.7
  311.5 1.6 constant_dynamic-update-slice_fusion.5
  313.1 2.0 fusion.174
  323.0 1.8 convolution_bitcast_fusion.7
  327.2 1.6 constant_dynamic-update-slice_fusion.5
  328.9 2.0 fusion.174
  338.7 1.8 convolution_bitcast_fusion.7
  343.0 1.6 constant_dynamic-update-slice_fusion.5
  344.6 2.0 fusion.174
  354.4 1.8 convolution_bitcast_fusion.7
  358.7 1.6 constant_dynamic-update-slice_fusion.5
  360.3 2.0 fusion.174
  370.2 1.8 convolution_bitcast_fusion.7
  374.4 1.6 constant_dynamic-update-slice_fusion.5
  376.0 2.0 fusion.174
  381.4 3.1 pad_maximum_fusion.whole_ref
  384.5 59.0 %shard_map.238 = f32[128,256]{1,0:T(8,128)} custom-call(bf16[4096,256]{1,0:T(8,128)(2,1)} %pad_maximum_fusion.whole_ref), custom_call_target="tpu_custom_call" | custom-call | tf_op jit(solution)/shard_map/pallas_call | solution.py:111
  449.9 1.9 fusion.35
  452.1 2.2 convolution_convert_fusion.7
  456.5 1.8 fusion.36
  458.3 2.0 fusion.33
  460.4 2.3 fusion.30
  462.7 2.3 fusion.29
  465.0 2.3 fusion.32.whole_ref
  467.3 418.8 %shard_map.239 = bf16[1024,4224]{1,0:T(8,128)(2,1)} custom-call(bf16[1024,4224]{1,0:T(8,128)(2,1)} %fusion.32.whole_ref), custom_call_target="tpu_custom_call" | custom-call | tf_op jit(solution)/shard_map/pallas_call | solution.py:164
  886.1 10.5 %convert_element_type.178 = f32[1024,4224]{1,0:T(8,128)} convert(bf16[1024,4224]{1,0:T(8,128)(2,1)} %shard_map.239) | non-fusion elementwise | flops 4325376 | bytes 25952256 | tf_op jit(solution)/shard_map/convert_element_type | solution.py:506
  896.6 5.2 slice_bitcast_fusion
  901.8 1.7 slice_bitcast_fusion.1
  903.5 4.3 fusion.74
  910.0 6.1 copy.146
  920.1 68.4 %psum.7 = f32[2176]{0:T(1024)S(1)} all-reduce(f32[2176]{0:T(1024)S(1)} %concatenate.46), channel_id=1, replica_groups=mesh['ctx'=32,'tp'=4] {'ctx','tp'}, use_global_device_ids=true, to_apply=%region_28.29 | all-reduce | flops 2176 | bytes 17408 | tf_op jit(solution)/shard_map/psum | solution.py:520
  989.7 1.7 fusion.48
  (587 shorter events, 186.6 us)
Async XLA Ops:
  7.2 200.0 %copy-start = (bf16[1152,1024]{1,0:T(8,128)(2,1)S(1)}, bf16[1152,1024]{1,0:T(8,128)(2,1)}, u32[]{:S(2)}) copy-start(bf16[1152,1024]{1,0:T(8,128)(2,1)} %param.30) | copy-start | bytes 7077892
  7.2 73.9 %copy-start.15 = (bf16[1024,256]{1,0:T(8,128)(2,1)S(1)}, bf16[1024,256]{1,0:T(8,128)(2,1)}, u32[]{:S(2)}) copy-start(bf16[1024,256]{1,0:T(8,128)(2,1)} %param.21) | copy-start | bytes 1572868
  7.2 186.1 %reduce-scatter.5.cloned.1.call-start = ((), (), s32[]{:S(2)}) async-start(), calls=%async_computation.4 | async-start | bytes 327680 | tf_op jit(solution)/shard_map/reduce_scatter | solution.py:266
  17.6 64.5 %copy-start.4 = (bf16[128,1024]{1,0:T(8,128)(2,1)}, bf16[128,1024]{1,0:T(8,128)(2,1)S(1)}, u32[]{:S(2)}) copy-start(bf16[128,1024]{1,0:T(8,128)(2,1)S(1)} %all_gather.12) | copy-start | bytes 786436
  17.6 64.4 %copy-start.53 = (f32[64]{0:T(128)S(1)}, f32[64]{0:T(128)}, u32[]{:S(2)}) copy-start(f32[64]{0:T(128)} %param.24) | copy-start | bytes 772
  18.9 59.2 %copy-start.29 = (f32[128,128]{0,1:T(8,128)}, f32[128,128]{0,1:T(8,128)S(1)}, u32[]{:S(2)}) copy-start(f32[128,128]{0,1:T(8,128)S(1)} %get-tuple-element.908) | copy-start | bytes 196612
  18.9 63.2 %copy-start.50 = (f32[128,2]{0,1:T(2,128)}, f32[128,2]{0,1:T(2,128)S(1)}, u32[]{:S(2)}) copy-start(f32[128,2]{0,1:T(2,128)S(1)} %add_rsqrt_fusion.1) | copy-start | bytes 3076
  22.2 59.9 %copy-start.37 = (f32[128,32]{0,1:T(8,128)}, f32[128,32]{0,1:T(8,128)S(1)}, u32[]{:S(2)}) copy-start(f32[128,32]{0,1:T(8,128)S(1)} %get-tuple-element.905) | copy-start | bytes 49156
  22.2 59.9 %copy-start.39 = (f32[128,32]{0,1:T(8,128)}, f32[128,32]{0,1:T(8,128)S(1)}, u32[]{:S(2)}) copy-start(f32[128,32]{0,1:T(8,128)S(1)} %get-tuple-element.906) | copy-start | bytes 49156
  95.6 1.7 copy-start.12
  105.4 1.7 copy-start.12
  144.5 1.7 copy-start.12
  161.1 2.0 copy-start.34
  163.1 75.0 %reduce-scatter.9.cloned.1.call-start = ((), (), s32[]{:S(2)}) async-start(), calls=%async_computation.6 | async-start | bytes 327680 | tf_op jit(solution)/shard_map/reduce_scatter | solution.py:266
  172.7 36.2 %copy-start.27 = (bf16[128,1024]{1,0:T(8,128)(2,1)}, bf16[128,1024]{1,0:T(8,128)(2,1)S(1)}, u32[]{:S(2)}) copy-start(bf16[128,1024]{1,0:T(8,128)(2,1)S(1)} %all_gather.14) | copy-start | bytes 786436
  194.3 45.3 %copy-start.51 = (f32[32]{0:T(128)}, f32[32]{0:T(128)S(1)}, u32[]{:S(2)}) copy-start(f32[32]{0:T(128)S(1)} %add_rsqrt_fusion.2) | copy-start | bytes 388
  202.6 2.3 copy-start.8
  204.8 4.2 copy-start.6
  207.2 2.8 copy-start.7
  208.9 2.7 copy-start.32
  208.9 3.4 copy-start.48
  209.0 4.2 copy-start.54
  209.0 4.8 copy-start.57
  209.0 5.4 copy-start.36
  209.0 5.4 copy-start.41
  209.0 29.1 %copy-start.10 = (bf16[32,1024]{1,0:T(8,128)(2,1)S(1)}, bf16[32,1024]{1,0:T(8,128)(2,1)}, u32[]{:S(2)}) copy-start(bf16[32,1024]{1,0:T(8,128)(2,1)} %param.18) | copy-start | bytes 196612
  209.0 29.1 %copy-start.18 = (bf16[32,1024]{1,0:T(8,128)(2,1)S(1)}, bf16[32,1024]{1,0:T(8,128)(2,1)}, u32[]{:S(2)}) copy-start(bf16[32,1024]{1,0:T(8,128)(2,1)} %reduce-scatter.5.cloned.1.call-done) | copy-start | bytes 196612
  209.0 29.1 %copy-start.44 = (f32[1024]{0:T(1024)S(1)}, f32[1024]{0:T(1024)}, u32[]{:S(2)}) copy-start(f32[1024]{0:T(1024)} %param.27) | copy-start | bytes 12292
  209.0 30.6 %copy-start.33 = (bf16[32,1024]{1,0:T(8,128)(2,1)S(1)}, bf16[32,1024]{1,0:T(8,128)(2,1)}, u32[]{:S(2)}) copy-start(bf16[32,1024]{1,0:T(8,128)(2,1)} %param.31) | copy-start | bytes 196612
  209.0 39.7 %copy-start.17 = (bf16[256,1024]{1,0:T(8,128)(2,1)S(1)}, bf16[256,1024]{1,0:T(8,128)(2,1)}, u32[]{:S(2)}) copy-start(bf16[256,1024]{1,0:T(8,128)(2,1)} %param.26) | copy-start | bytes 1572868
  209.1 40.1 %copy-start.3 = (f32[2,2,2,64,64]{4,3,2,1,0:T(8,128)S(1)}, f32[2,2,2,64,64]{4,3,2,1,0:T(8,128)}, u32[]{:S(2)}) copy-start(f32[2,2,2,64,64]{4,3,2,1,0:T(8,128)} %get-tuple-element.607) | copy-start | bytes 393220
  211.6 707.3 %reduce-scatter.11.cloned.1.call-start = ((), (), s32[]{:S(2)}) async-start(), calls=%async_computation.7 | async-start | bytes 327680 | tf_op jit(solution)/shard_map/reduce_scatter | solution.py:266
  239.6 12.6 %copy-start.59 = (f32[32]{0:T(128)}, f32[32]{0:T(128)S(1)}, u32[]{:S(2)}) copy-start(f32[32]{0:T(128)S(1)} %broadcast_multiply_fusion.3) | copy-start | bytes 388
  252.3 127.2 %copy-start.38 = (f32[128,32]{0,1:T(8,128)S(1)}, f32[128,32]{0,1:T(8,128)}, u32[]{:S(2)}) copy-start(f32[128,32]{0,1:T(8,128)} %copy-done.37) | copy-start | bytes 49156
  253.8 3.0 copy-start.2
  269.4 3.0 copy-start.2
  285.1 3.0 copy-start.2
  300.9 3.0 copy-start.2
  316.6 3.0 copy-start.2
  332.3 3.0 copy-start.2
  348.0 3.0 copy-start.2
  363.8 3.0 copy-start.2
  378.0 66.6 %copy-start.40 = (f32[128,32]{0,1:T(8,128)S(1)}, f32[128,32]{0,1:T(8,128)}, u32[]{:S(2)}) copy-start(f32[128,32]{0,1:T(8,128)} %copy-done.39) | copy-start | bytes 49156
  378.0 66.6 %copy-start.30 = (f32[128,128]{0,1:T(8,128)S(1)}, f32[128,128]{0,1:T(8,128)}, u32[]{:S(2)}) copy-start(f32[128,128]{0,1:T(8,128)} %copy-done.29) | copy-start | bytes 196612
  378.0 66.6 %copy-start.58 = (f32[64]{0:T(128)S(1)}, f32[64]{0:T(128)}, u32[]{:S(2)}) copy-start(f32[64]{0:T(128)} %param.25) | copy-start | bytes 772
  378.0 66.7 %copy-start.23 = (f32[128,256]{1,0:T(8,128)S(1)}, f32[128,256]{1,0:T(8,128)}, u32[]{:S(2)}) copy-start(f32[128,256]{1,0:T(8,128)} %copy-done.22) | copy-start | bytes 393220
  378.0 66.7 %copy-start.35 = (f32[128,256]{1,0:T(8,128)S(1)}, f32[128,256]{1,0:T(8,128)}, u32[]{:S(2)}) copy-start(f32[128,256]{1,0:T(8,128)} %copy.136) | copy-start | bytes 393220
  378.0 66.7 %copy-start.56 = (f32[256]{0:T(256)S(1)}, f32[256]{0:T(256)}, u32[]{:S(2)}) copy-start(f32[256]{0:T(256)} %mul.674) | copy-start | bytes 3076
  443.6 10.7 %copy-start.5 = (bf16[128,1024]{1,0:T(8,128)(2,1)S(1)}, bf16[128,1024]{1,0:T(8,128)(2,1)}, u32[]{:S(2)}) copy-start(bf16[128,1024]{1,0:T(8,128)(2,1)} %copy-done.4) | copy-start | bytes 786436
  445.4 13.0 %copy-start.14 = (bf16[128,1024]{1,0:T(8,128)(2,1)S(1)}, bf16[128,1024]{1,0:T(8,128)(2,1)}, u32[]{:S(2)}) copy-start(bf16[128,1024]{1,0:T(8,128)(2,1)} %copy-done.13) | copy-start | bytes 786436
  447.3 13.0 %copy-start.9 = (bf16[128,1024]{1,0:T(8,128)(2,1)S(1)}, bf16[128,1024]{1,0:T(8,128)(2,1)}, u32[]{:S(2)}) copy-start(bf16[128,1024]{1,0:T(8,128)(2,1)} %copy-done.8) | copy-start | bytes 786436
  447.4 13.0 %copy-start.21 = (bf16[128,1152]{1,0:T(8,128)(2,1)S(1)}, bf16[128,1152]{1,0:T(8,128)(2,1)}, u32[]{:S(2)}) copy-start(bf16[128,1152]{1,0:T(8,128)(2,1)} %copy-done.20) | copy-start | bytes 884740
  448.7 5.6 copy-start.43
  451.8 537.8 %reduce-scatter.7.cloned.1.call-start = ((), (), s32[]{:S(2)}) async-start(), calls=%async_computation.5 | async-start | bytes 327680 | tf_op jit(solution)/shard_map/reduce_scatter | solution.py:266
  454.3 8.3 copy-start.26
  454.3 10.6 %copy-start.24 = (bf16[128,1152]{1,0:T(8,128)(2,1)S(1)}, bf16[128,1152]{1,0:T(8,128)(2,1)}, u32[]{:S(2)}) copy-start(bf16[128,1152]{1,0:T(8,128)(2,1)} %get-tuple-element.882) | copy-start | bytes 884740
  454.4 10.6 %copy-start.28 = (bf16[128,1024]{1,0:T(8,128)(2,1)S(1)}, bf16[128,1024]{1,0:T(8,128)(2,1)}, u32[]{:S(2)}) copy-start(bf16[128,1024]{1,0:T(8,128)(2,1)} %copy-done.27) | copy-start | bytes 786436
  896.6 6.9 copy-start.1
  909.9 9.0 copy-start.11
  909.9 9.0 copy-start.46
  909.9 10.1 %copy-start.49 = (f32[1024]{0:T(1024)S(1)}, f32[1024]{0:T(1024)}, u32[]{:S(2)}) copy-start(f32[1024]{0:T(1024)} %get-tuple-element.818) | copy-start | bytes 12292
  909.9 79.7 %copy-start.19 = (bf16[32,1024]{1,0:T(8,128)(2,1)S(1)}, bf16[32,1024]{1,0:T(8,128)(2,1)}, u32[]{:S(2)}) copy-start(bf16[32,1024]{1,0:T(8,128)(2,1)} %reduce-scatter.5.cloned.1.call-done) | copy-start | bytes 196612
  909.9 79.7 %copy-start.45 = (f32[1024]{0:T(1024)S(1)}, f32[1024]{0:T(1024)}, u32[]{:S(2)}) copy-start(f32[1024]{0:T(1024)} %param.27) | copy-start | bytes 12292
  910.0 79.7 %copy-start.52 = (f32[32]{0:T(128)S(1)}, f32[32]{0:T(128)}, u32[]{:S(2)}) copy-start(f32[32]{0:T(128)} %copy-done.51) | copy-start | bytes 388
  (14 other events, 16.1 us)
Sparse Core Ops, SparseCore 0:
  163.2 29.9 reduce-scatter.4
  211.7 26.3 reduce-scatter.8
  452.0 27.6 reduce-scatter.10
  482.3 95.7 reduce-scatter.6

commit v3 on v2

--- a/solution.py
+++ b/solution.py
@@ -320,67 +320,31 @@
     query_blocks = query_rot.reshape(2, seq_rows, kv_heads, group_size, head_dim)
     query_places = own_places[:seq_rows]
 
-    def span_heads(flat_rows):
-        return jnp.transpose(
-            flat_rows.reshape(shard_span, 2, seq_rows, kv_heads, head_dim), (1, 0, 2, 3, 4)
-        ).reshape(2, shard_span * seq_rows, kv_heads, head_dim)
-
-    def span_flat(head_rows):
-        return jnp.transpose(
-            head_rows.reshape(2, shard_span, seq_rows, kv_width), (1, 0, 2, 3)
-        ).reshape(shard_span * rows_total, kv_width)
-
-    def scores_for(key_heads, key_places):
-        scores = (
-            jnp.einsum(
-                "sqhgd,skhd->shgqk", query_blocks, key_heads, preferred_element_type=jnp.float32
-            )
-            * score_scale
+    whole_kv = ctx_gather(jnp.concatenate([keys_own, values_own], axis=1), place_count, 0)
+    seq_kv = jnp.transpose(
+        whole_kv.reshape(place_count, 2, seq_rows, 2 * kv_width), (1, 0, 2, 3)
+    ).reshape(2, place_count * seq_rows, 2 * kv_width)
+    key_heads = seq_kv[..., :kv_width].reshape(2, place_count * seq_rows, kv_heads, head_dim)
+    value_heads = seq_kv[..., kv_width:].reshape(2, place_count * seq_rows, kv_heads, head_dim)
+    key_places = span_places(block_map, 0, place_count, seq_rows, place_count)
+    allowed = key_places[None, :] <= query_places[:, None]
+    scores = (
+        jnp.einsum(
+            "sqhgd,skhd->shgqk", query_blocks, key_heads, preferred_element_type=jnp.float32
         )
-        allowed = key_places[None, :] <= query_places[:, None]
-        return (scores, allowed)
-
-    def forward_step(softmax_state, key_heads, value_heads, key_places):
-        running_top, running_total, running_acc = softmax_state
-        scores, allowed = scores_for(key_heads, key_places)
-        scores = jnp.where(allowed, scores, NEGATIVE)
-        new_top = jnp.maximum(running_top, jnp.max(scores, axis=-1))
-        weights = jnp.where(allowed, jnp.exp(scores - new_top[..., None]), 0.0)
-        fading = jnp.exp(running_top - new_top)
-        running_total = running_total * fading + jnp.sum(weights, axis=-1)
-        running_acc = running_acc * fading[..., None] + jnp.einsum(
-            "shgqk,skhd->shgqd",
-            weights.astype(jnp.bfloat16),
-            value_heads,
-            preferred_element_type=jnp.float32,
-        )
-        return (new_top, running_total, running_acc)
-
-    start_state = (
-        jnp.full((2, kv_heads, group_size, seq_rows), NEGATIVE, jnp.float32),
-        jnp.zeros((2, kv_heads, group_size, seq_rows), jnp.float32),
-        jnp.zeros((2, kv_heads, group_size, seq_rows, head_dim), jnp.float32),
-    )
-    span_count = place_count // shard_span
-    span_rows = shard_span * rows_total
-    whole_kv = ctx_gather(jnp.concatenate([keys_own, values_own], axis=1), place_count, 0)
-    whole_keys, whole_values = whole_kv[:, :kv_width], whole_kv[:, kv_width:]
-
-    def whole_forward(span_index, softmax_state):
-        first_anchor = span_index * shard_span
-        keys_flat = lax.dynamic_slice_in_dim(whole_keys, first_anchor * rows_total, span_rows, 0)
-        values_flat = lax.dynamic_slice_in_dim(
-            whole_values, first_anchor * rows_total, span_rows, 0
-        )
-        key_places = span_places(block_map, first_anchor, shard_span, seq_rows, place_count)
-        return forward_step(
-            softmax_state, span_heads(keys_flat), span_heads(values_flat), key_places
-        )
-
-    softmax_state = lax.fori_loop(0, span_count, whole_forward, start_state)
-    running_top, running_total, running_acc = softmax_state
-    log_total = running_top + jnp.log(running_total)
-    attn_rows = jnp.transpose(running_acc / running_total[..., None], (0, 3, 1, 2, 4))
+        * score_scale
+    )
+    top = jnp.max(jnp.where(allowed, scores, NEGATIVE), axis=-1)
+    weights = jnp.where(allowed, jnp.exp(scores - top[..., None]), 0.0)
+    weight_total = jnp.sum(weights, axis=-1)
+    weighted = jnp.einsum(
+        "shgqk,skhd->shgqd",
+        weights.astype(jnp.bfloat16),
+        value_heads,
+        preferred_element_type=jnp.float32,
+    )
+    log_total = top + jnp.log(weight_total)
+    attn_rows = jnp.transpose(weighted / weight_total[..., None], (0, 3, 1, 2, 4))
     attn_low = attn_rows.reshape(rows_total, query_heads * head_dim).astype(jnp.bfloat16)
     residual_mid = residual_in + reduce_rows(
         jnp.dot(attn_low, output_weight, preferred_element_type=jnp.float32)
@@ -418,60 +382,35 @@
     delta_rows = jnp.sum(grad_attn_blocks.astype(jnp.float32) * attn_rows, axis=-1)
     delta_rows = jnp.transpose(delta_rows, (0, 2, 3, 1))
 
-    def backward_step(key_heads, value_heads, key_places):
-        scores, allowed = scores_for(key_heads, key_places)
-        probs = jnp.where(allowed, jnp.exp(scores - log_total[..., None]), 0.0)
-        grad_value_block = jnp.einsum(
-            "shgqk,sqhgd->skhd",
-            probs.astype(jnp.bfloat16),
-            grad_attn_blocks,
-            preferred_element_type=jnp.float32,
-        )
-        grad_probs = jnp.einsum(
-            "sqhgd,skhd->shgqk", grad_attn_blocks, value_heads, preferred_element_type=jnp.float32
-        )
-        grad_scores = (score_scale * probs * (grad_probs - delta_rows[..., None])).astype(
-            jnp.bfloat16
-        )
-        grad_query_block = jnp.einsum(
-            "shgqk,skhd->sqhgd", grad_scores, key_heads, preferred_element_type=jnp.float32
-        )
-        grad_key_block = jnp.einsum(
-            "shgqk,sqhgd->skhd", grad_scores, query_blocks, preferred_element_type=jnp.float32
-        )
-        return (grad_query_block, grad_key_block, grad_value_block)
-
-    key_grad_whole = jnp.zeros((place_count * rows_total, kv_width), jnp.float32)
-    start_grads = (
-        jnp.zeros((2, seq_rows, kv_heads, group_size, head_dim), jnp.float32),
-        key_grad_whole,
-        key_grad_whole,
-    )
-
-    def whole_backward(span_index, grad_carry):
-        query_acc, key_grad_all, value_grad_all = grad_carry
-        first_anchor = span_index * shard_span
-        keys_flat = lax.dynamic_slice_in_dim(whole_keys, first_anchor * rows_total, span_rows, 0)
-        values_flat = lax.dynamic_slice_in_dim(
-            whole_values, first_anchor * rows_total, span_rows, 0
-        )
-        key_places = span_places(block_map, first_anchor, shard_span, seq_rows, place_count)
-        add_query, add_key, add_value = backward_step(
-            span_heads(keys_flat), span_heads(values_flat), key_places
-        )
-        key_grad_all = lax.dynamic_update_slice_in_dim(
-            key_grad_all, span_flat(add_key), first_anchor * rows_total, 0
-        )
-        value_grad_all = lax.dynamic_update_slice_in_dim(
-            value_grad_all, span_flat(add_value), first_anchor * rows_total, 0
-        )
-        return (query_acc + add_query, key_grad_all, value_grad_all)
-
-    query_acc, key_grad_all, value_grad_all = lax.fori_loop(
-        0, span_count, whole_backward, start_grads
+    probs = jnp.where(allowed, jnp.exp(scores - log_total[..., None]), 0.0)
+    grad_value_seq = jnp.einsum(
+        "shgqk,sqhgd->skhd",
+        probs.astype(jnp.bfloat16),
+        grad_attn_blocks,
+        preferred_element_type=jnp.float32,
+    )
+    grad_probs = jnp.einsum(
+        "sqhgd,skhd->shgqk", grad_attn_blocks, value_heads, preferred_element_type=jnp.float32
+    )
+    grad_scores = (score_scale * probs * (grad_probs - delta_rows[..., None])).astype(jnp.bfloat16)
+    query_acc = jnp.einsum(
+        "shgqk,skhd->sqhgd", grad_scores, key_heads, preferred_element_type=jnp.float32
+    )
+    grad_key_seq = jnp.einsum(
+        "shgqk,sqhgd->skhd", grad_scores, query_blocks, preferred_element_type=jnp.float32
+    )
+    grad_kv_seq = jnp.concatenate(
+        [
+            grad_key_seq.reshape(2, place_count, seq_rows, kv_width),
+            grad_value_seq.reshape(2, place_count, seq_rows, kv_width),
+        ],
+        axis=-1,
+    )
+    grad_kv_all = jnp.transpose(grad_kv_seq, (1, 0, 2, 3)).reshape(
+        place_count * rows_total, 2 * kv_width
     )
     grad_kv_flat = ctx_scatter(
-        jnp.concatenate([key_grad_all, value_grad_all], axis=1).astype(jnp.bfloat16),
+        grad_kv_all.astype(jnp.bfloat16),
         place_count,
         1,
     )

time: 1010 us -> 864 us (0.86)
  matrix products: 102 us -> 50.7 us
  local copies, waits for them, and re-layouts: 125 us -> 78 us
  other arithmetic: 77.5 us -> 44.8 us
    dot_general x56 -> x6, matrix products: 68.7 us -> 14 us  [the longest x1 4.91 us: per_device(): jnp.einsum('shgqk,sqhgd->skhd', probs.astype(jnp.bfloat16), grad_attn_blo...]
    dynamic_slice x24 -> x0, local copies, waits for them, and re-layouts: 22.6 us -> none  [the longest x8 7.88 us: whole_forward(): lax.dynamic_slice_in_dim(whole_values, first_anchor * rows_total, span_ro...]
    reshape x80 -> x3, local copies, waits for them, and re-layouts: 26.1 us -> 10.5 us  [the longest x1 4.39 us: per_device(): grad_key_seq.reshape(2, place_count, seq_rows, kv_width)]
    dynamic_update_slice x8 -> x0, local copies, waits for them, and re-layouts: 13 us -> none  [whole_backward(): lax.dynamic_update_slice_in_dim(value_grad_all, span_flat(add_value), fir...]
    transpose x48 -> x1, local copies, waits for them, and re-layouts: 14.5 us -> 1.85 us  [per_device(): jnp.einsum('shgqk,skhd->sqhgd', grad_scores, key_heads, preferred_element...]
    reduce_sum x16 -> x1, other arithmetic: 13.7 us -> 1.3 us  [span_places(): jnp.sum(jnp.where(jnp.arange(place_count, dtype=jnp.int32)[None, :] == an...]
    while x41 -> x0, local copies, waits for them, and re-layouts: 11.5 us -> none
    le x16 -> x1, other arithmetic: 11.7 us -> 0.84 us  [per_device(): allowed = key_places[None, :] <= query_places[:, None]]
  transfers between devices with their start and end apart: 4 -> 4, of which waited for: 2 -> 2; matrix products, arithmetic and copies ran while one was open for 5% -> 7% of each run, Pallas kernels for 42% -> 48%
where the time goes in v3:
time: 864 us; the launch traced here: 858 us
  Pallas kernels  524 us (61%)
  blocking collectives  108 us (12%)
  local copies, waits for them, and re-layouts  78 us (9%)
  matrix products  50.7 us (6%)
  other arithmetic  44.8 us (5%)
  waiting for transfers between devices  37.6 us (4%)
  between operations  15.1 us (2%)
    pallas_call x1, Pallas kernels, ctx_sum(): pl.pallas_call(functools.partial(_sum_kernel, n), out_shape=jax.ShapeDtyp...  411 us
    psum x1, blocking collectives, per_device(): gains = lax.psum(jnp.concatenate(gain_parts), ('ctx', 'tp'))  74.5 us
    pallas_call x1, Pallas kernels, ctx_scatter(): pl.pallas_call(functools.partial(_scatter_kernel, n), out_shape=jax.Shape...  59.1 us
    pallas_call x1, Pallas kernels, ctx_gather(): pl.pallas_call(functools.partial(_gather_kernel, n), out_shape=jax.ShapeD...  53.2 us
    reduce_scatter x4, waiting for transfers between devices, reduce_rows(): lax.psum_scatter(partial_rows.astype(jnp.bfloat16), 'tp', scatter_dimensi...  37.5 us
    all_gather x4, blocking collectives, gather_rows(): return lax.all_gather(rows_low, 'tp', axis=0, tiled=True)  33.2 us
  transfers between devices with their start and end apart: 4, of which 2 were waited for; matrix products, arithmetic and copies ran while one was open for 7% of the time, Pallas kernels for 48%

profile of v3, /device:TPU:28, one launch (start us, length us, event | category | flops | bytes accessed | tf_op | source)
XLA Modules:
  0.0 857.9 jit_solution(13989462701571220189)
XLA Ops:
  10.2 8.1 all_gather.12
  27.0 53.2 %shard_map.237 = bf16[4096,256]{1,0:T(8,128)(2,1)} custom-call(bf16[128,256]{1,0:T(8,128)(2,1)} %pad_maximum_fusion.2.part_ref), custom_call_target="tpu_custom_call" | custom-call | tf_op jit(solution)/shard_map/pallas_call | solution.py:58
  80.2 1.7 copy.76
  81.9 1.7 fusion.82
  83.6 1.5 copy.77
  85.1 2.0 fusion.86
  88.9 1.4 subtract_convert_fusion
  90.3 1.5 concatenate.38
  91.7 1.6 copy.79
  93.4 1.5 concatenate.39
  94.8 1.6 copy.80
  97.1 1.4 multiply_add_fusion.2
  98.5 1.4 add.166
  99.9 2.3 copy.81
  103.0 2.0 fusion.2
  106.2 2.0 fusion.85
  108.2 1.7 copy.82
  109.9 1.7 convert_element_type.132
  111.6 2.0 convolution_convert_fusion.8
  113.7 10.3 %all_gather.14 = bf16[128,1024]{1,0:T(8,128)(2,1)} all-gather(bf16[32,1024]{1,0:T(8,128)(2,1)S(1)} %copy-done.33), channel_id=1, replica_groups=mesh['ctx'=32,'tp'=4] {'tp'}, dimensions={0}, use_global_device_ids=true | all-gather | bytes 327680 | tf_op jit(solution)/shard_map/all_gather | solution.py:262
  124.0 20.3 %reduce-scatter.5.cloned.1.call-done = bf16[32,1024]{1,0:T(8,128)(2,1)} async-done(((bf16[128,1024]{1,0:T(8,128)(2,1)}), bf16[32,1024]{1,0:T(8,128)(2,1)}) %reduce-scatter.5.cloned.1.call-update) | async-done | bytes 65552 | tf_op jit(solution)/shard_map/reduce_scatter | solution.py:266
  146.4 7.3 all_gather.13
  153.7 2.3 fusion.87
  156.6 1.7 multiply_convert_fusion
  159.2 1.6 fusion.31
  164.6 1.6 copy.90
  167.5 1.3 mul.534
  170.2 17.1 %reduce-scatter.9.cloned.1.call-done = bf16[32,1024]{1,0:T(8,128)(2,1)} async-done(((bf16[128,1024]{1,0:T(8,128)(2,1)}), bf16[32,1024]{1,0:T(8,128)(2,1)}) %reduce-scatter.9.cloned.1.call-update) | async-done | bytes 65552 | tf_op jit(solution)/shard_map/reduce_scatter | solution.py:266
  187.3 1.5 fusion.51
  190.4 7.5 all_gather.15
  198.6 2.0 convolution_convert_fusion.9
  200.6 1.6 reshape.322
  202.2 1.7 copy.84
  205.1 4.9 fusion.16
  210.1 1.7 fusion.1
  211.8 1.5 fusion.17
  213.3 1.8 convolution_bitcast_fusion.2
  215.2 4.4 reshape.324
  219.6 4.4 reshape.325
  224.0 5.0 maximum_bitcast_fusion
  229.0 5.5 copy.93
  234.6 59.1 %shard_map.238 = f32[128,256]{1,0:T(8,128)} custom-call(bf16[4096,256]{1,0:T(8,128)(2,1)} %bitcast.191), custom_call_target="tpu_custom_call" | custom-call | tf_op jit(solution)/shard_map/pallas_call | solution.py:111
  295.9 1.9 copy.85
  300.3 1.7 copy.89
  302.0 1.7 copy.86
  303.6 1.6 multiply_reduce_fusion.1
  305.9 1.5 fusion.63
  308.7 1.9 fusion.28
  310.9 2.2 convolution_convert_fusion.7
  313.1 2.1 fusion.27
  315.2 1.8 fusion.30
  317.0 1.8 fusion.29
  318.8 2.0 fusion.26
  320.8 3.3 fusion.8
  324.1 2.3 fusion.7
  326.4 2.3 fusion.10.whole_ref
  328.7 411.3 %shard_map.239 = bf16[1024,4224]{1,0:T(8,128)(2,1)} custom-call(bf16[1024,4224]{1,0:T(8,128)(2,1)} %fusion.10.whole_ref), custom_call_target="tpu_custom_call" | custom-call | tf_op jit(solution)/shard_map/pallas_call | solution.py:164
  740.0 10.5 %convert_element_type.163 = f32[1024,4224]{1,0:T(8,128)} convert(bf16[1024,4224]{1,0:T(8,128)(2,1)} %shard_map.239) | non-fusion elementwise | flops 4325376 | bytes 25952256 | tf_op jit(solution)/shard_map/convert_element_type | solution.py:445
  750.5 5.2 slice_bitcast_fusion
  755.7 1.7 slice_bitcast_fusion.1
  757.4 4.3 fusion.80
  763.8 6.1 copy.103
  773.9 74.5 %psum.7 = f32[2176]{0:T(1024)S(1)} all-reduce(f32[2176]{0:T(1024)S(1)} %concatenate.46), channel_id=1, replica_groups=mesh['ctx'=32,'tp'=4] {'ctx','tp'}, use_global_device_ids=true, to_apply=%region_23.24 | all-reduce | flops 2176 | bytes 17408 | tf_op jit(solution)/shard_map/psum | solution.py:459
  849.6 1.7 fusion.46
  (178 shorter events, 42.9 us)
Async XLA Ops:
  7.2 149.4 %copy-start = (bf16[1152,1024]{1,0:T(8,128)(2,1)S(1)}, bf16[1152,1024]{1,0:T(8,128)(2,1)}, u32[]{:S(2)}) copy-start(bf16[1152,1024]{1,0:T(8,128)(2,1)} %param.26) | copy-start | bytes 7077892
  7.2 137.1 %reduce-scatter.5.cloned.1.call-start = ((), (), s32[]{:S(2)}) async-start(), calls=%async_computation.4 | async-start | bytes 327680 | tf_op jit(solution)/shard_map/reduce_scatter | solution.py:266
  9.3 0.9 copy-start.49
  18.3 65.2 %copy-start.5 = (bf16[128,1024]{1,0:T(8,128)(2,1)}, bf16[128,1024]{1,0:T(8,128)(2,1)S(1)}, u32[]{:S(2)}) copy-start(bf16[128,1024]{1,0:T(8,128)(2,1)S(1)} %all_gather.12) | copy-start | bytes 786436
  19.7 63.9 %copy-start.29 = (f32[128,128]{0,1:T(8,128)}, f32[128,128]{0,1:T(8,128)S(1)}, u32[]{:S(2)}) copy-start(f32[128,128]{0,1:T(8,128)S(1)} %get-tuple-element.92) | copy-start | bytes 196612
  19.7 5.3 copy-start.45
  24.3 59.3 %copy-start.35 = (f32[128,32]{0,1:T(8,128)}, f32[128,32]{0,1:T(8,128)S(1)}, u32[]{:S(2)}) copy-start(f32[128,32]{0,1:T(8,128)S(1)} %get-tuple-element.90) | copy-start | bytes 49156
  88.1 16.9 %copy-start.17 = (f32[128,256]{0,1:T(8,128)}, f32[128,256]{0,1:T(8,128)S(1)}, u32[]{:S(2)}) copy-start(f32[128,256]{0,1:T(8,128)S(1)} %copy.78) | copy-start | bytes 393220
  88.1 2.1 copy-start.42
  103.0 3.2 copy-start.14
  103.0 3.2 copy-start.31
  105.0 3.2 copy-start.3
  105.0 3.2 copy-start.41
  106.2 2.0 copy-start.44
  106.2 7.5 copy-start.33
  106.2 38.1 %copy-start.11 = (bf16[32,1024]{1,0:T(8,128)(2,1)S(1)}, bf16[32,1024]{1,0:T(8,128)(2,1)}, u32[]{:S(2)}) copy-start(bf16[32,1024]{1,0:T(8,128)(2,1)} %param.14) | copy-start | bytes 196612
  113.6 73.7 %reduce-scatter.9.cloned.1.call-start = ((), (), s32[]{:S(2)}) async-start(), calls=%async_computation.6 | async-start | bytes 327680 | tf_op jit(solution)/shard_map/reduce_scatter | solution.py:266
  144.3 11.7 %copy-start.8 = (bf16[1024,1152]{1,0:T(8,128)(2,1)S(1)}, bf16[1024,1152]{1,0:T(8,128)(2,1)}, u32[]{:S(2)}) copy-start(bf16[1024,1152]{1,0:T(8,128)(2,1)} %param.25) | copy-start | bytes 7077892
  144.3 12.2 %copy-start.27 = (bf16[128,1024]{1,0:T(8,128)(2,1)S(1)}, bf16[128,1024]{1,0:T(8,128)(2,1)}, u32[]{:S(2)}) copy-start(bf16[128,1024]{1,0:T(8,128)(2,1)} %all_gather.14) | copy-start | bytes 786436
  145.5 10.5 %copy-start.46 = (f32[32]{0:T(128)}, f32[32]{0:T(128)S(1)}, u32[]{:S(2)}) copy-start(f32[32]{0:T(128)S(1)} %add_rsqrt_fusion.2) | copy-start | bytes 388
  153.7 2.3 copy-start.9
  156.0 2.3 copy-start.7
  158.3 0.9 copy-start.20
  158.3 0.9 copy-start.23
  158.3 29.0 %copy-start.19 = (bf16[32,1024]{1,0:T(8,128)(2,1)S(1)}, bf16[32,1024]{1,0:T(8,128)(2,1)}, u32[]{:S(2)}) copy-start(bf16[32,1024]{1,0:T(8,128)(2,1)} %reduce-scatter.5.cloned.1.call-done) | copy-start | bytes 196612
  160.8 612.0 %reduce-scatter.11.cloned.1.call-start = ((), (), s32[]{:S(2)}) async-start(), calls=%async_computation.7 | async-start | bytes 327680 | tf_op jit(solution)/shard_map/reduce_scatter | solution.py:266
  188.8 0.6 copy-start.52
  197.9 0.7 copy-start.12
  203.9 6.1 copy-start.4
  203.9 6.1 copy-start.15
  203.9 6.1 copy-start.32
  203.9 6.1 copy-start.34
  203.9 6.1 copy-start.50
  210.0 1.8 copy-start.25
  210.0 1.8 copy-start.26
  229.0 65.7 %copy-start.36 = (f32[128,32]{0,1:T(8,128)S(1)}, f32[128,32]{0,1:T(8,128)}, u32[]{:S(2)}) copy-start(f32[128,32]{0,1:T(8,128)} %copy-done.35) | copy-start | bytes 49156
  229.0 65.7 %copy-start.30 = (f32[128,128]{0,1:T(8,128)S(1)}, f32[128,128]{0,1:T(8,128)}, u32[]{:S(2)}) copy-start(f32[128,128]{0,1:T(8,128)} %copy-done.29) | copy-start | bytes 196612
  229.0 65.7 %copy-start.51 = (f32[64]{0:T(128)S(1)}, f32[64]{0:T(128)}, u32[]{:S(2)}) copy-start(f32[64]{0:T(128)} %param.21) | copy-start | bytes 772
  229.0 69.9 %copy-start.18 = (f32[128,256]{0,1:T(8,128)S(1)}, f32[128,256]{0,1:T(8,128)}, u32[]{:S(2)}) copy-start(f32[128,256]{0,1:T(8,128)} %copy-done.17) | copy-start | bytes 393220
  229.0 69.9 %copy-start.48 = (f32[64]{0:T(128)S(1)}, f32[64]{0:T(128)}, u32[]{:S(2)}) copy-start(f32[64]{0:T(128)} %param.20) | copy-start | bytes 772
  229.0 74.6 %copy-start.21 = (f32[128,256]{1,0:T(8,128)S(1)}, f32[128,256]{1,0:T(8,128)}, u32[]{:S(2)}) copy-start(f32[128,256]{1,0:T(8,128)} %fusion.86) | copy-start | bytes 393220
  234.6 70.7 %copy-start.16 = (bf16[1024,256]{1,0:T(8,128)(2,1)S(1)}, bf16[1024,256]{1,0:T(8,128)(2,1)}, u32[]{:S(2)}) copy-start(bf16[1024,256]{1,0:T(8,128)(2,1)} %param.17) | copy-start | bytes 1572868
  299.6 13.5 %copy-start.6 = (bf16[128,1024]{1,0:T(8,128)(2,1)S(1)}, bf16[128,1024]{1,0:T(8,128)(2,1)}, u32[]{:S(2)}) copy-start(bf16[128,1024]{1,0:T(8,128)(2,1)} %copy-done.5) | copy-start | bytes 786436
  305.3 0.6 copy-start.38
  305.9 12.9 %copy-start.13 = (bf16[128,1024]{1,0:T(8,128)(2,1)S(1)}, bf16[128,1024]{1,0:T(8,128)(2,1)}, u32[]{:S(2)}) copy-start(bf16[128,1024]{1,0:T(8,128)(2,1)} %copy-done.12) | copy-start | bytes 786436
  307.4 5.7 copy-start.37
  307.4 13.4 %copy-start.10 = (bf16[128,1024]{1,0:T(8,128)(2,1)S(1)}, bf16[128,1024]{1,0:T(8,128)(2,1)}, u32[]{:S(2)}) copy-start(bf16[128,1024]{1,0:T(8,128)(2,1)} %copy-done.9) | copy-start | bytes 786436
  310.6 539.0 %reduce-scatter.7.cloned.1.call-start = ((), (), s32[]{:S(2)}) async-start(), calls=%async_computation.5 | async-start | bytes 327680 | tf_op jit(solution)/shard_map/reduce_scatter | solution.py:266
  313.1 11.1 %copy-start.24 = (bf16[128,1152]{1,0:T(8,128)(2,1)S(1)}, bf16[128,1152]{1,0:T(8,128)(2,1)}, u32[]{:S(2)}) copy-start(bf16[128,1152]{1,0:T(8,128)(2,1)} %copy-done.23) | copy-start | bytes 884740
  313.1 13.3 %copy-start.22 = (bf16[128,1152]{1,0:T(8,128)(2,1)S(1)}, bf16[128,1152]{1,0:T(8,128)(2,1)}, u32[]{:S(2)}) copy-start(bf16[128,1152]{1,0:T(8,128)(2,1)} %get-tuple-element.66) | copy-start | bytes 884740
  313.1 13.3 %copy-start.28 = (bf16[128,1024]{1,0:T(8,128)(2,1)S(1)}, bf16[128,1024]{1,0:T(8,128)(2,1)}, u32[]{:S(2)}) copy-start(bf16[128,1024]{1,0:T(8,128)(2,1)} %all_gather.14) | copy-start | bytes 786436
  750.5 6.9 copy-start.2
  762.8 88.6 %copy-start.1 = (bf16[1152,1024]{1,0:T(8,128)(2,1)S(1)}, bf16[1152,1024]{1,0:T(8,128)(2,1)}, u32[]{:S(2)}) copy-start(bf16[1152,1024]{1,0:T(8,128)(2,1)} %param.26) | copy-start | bytes 7077892
  763.8 9.0 %copy-start.40 = (f32[1024]{0:T(1024)S(1)}, f32[1024]{0:T(1024)}, u32[]{:S(2)}) copy-start(f32[1024]{0:T(1024)} %param.16) | copy-start | bytes 12292
  763.8 10.0 %copy-start.43 = (f32[1024]{0:T(1024)S(1)}, f32[1024]{0:T(1024)}, u32[]{:S(2)}) copy-start(f32[1024]{0:T(1024)} %get-tuple-element.52) | copy-start | bytes 12292
  763.8 85.8 %copy-start.39 = (f32[1024]{0:T(1024)S(1)}, f32[1024]{0:T(1024)}, u32[]{:S(2)}) copy-start(f32[1024]{0:T(1024)} %param.23) | copy-start | bytes 12292
  763.8 85.8 %copy-start.47 = (f32[32]{0:T(128)S(1)}, f32[32]{0:T(128)}, u32[]{:S(2)}) copy-start(f32[32]{0:T(128)} %copy-done.46) | copy-start | bytes 388
Sparse Core Ops, SparseCore 0:
  113.7 30.5 reduce-scatter.4
  160.9 26.3 reduce-scatter.8
  310.7 27.3 reduce-scatter.10
  340.7 47.4 reduce-scatter.6

commit v4 on v3

--- a/solution.py
+++ b/solution.py
@@ -124,11 +124,38 @@
     )(whole)
 
 
-def _sum_kernel(n, whole_ref, out_ref, held, mine, send_sem, recv_sem, send_back, recv_back):
+def _sum_kernel(
+    n,
+    whole_ref,
+    extra_ref,
+    out_ref,
+    extra_out,
+    held,
+    mine,
+    extra_held,
+    send_sem,
+    recv_sem,
+    send_back,
+    recv_back,
+    send_extra,
+    recv_extra,
+):
     me = lax.axis_index("ctx")
     other = lax.axis_index("tp")
     rows = whole_ref.shape[0] // n
     _enter(n, me, other)
+    extra_copies = []
+    for k in range(1, n):
+        copy = pltpu.make_async_remote_copy(
+            src_ref=extra_ref,
+            dst_ref=extra_held.at[k],
+            send_sem=send_extra.at[k],
+            recv_sem=recv_extra.at[k],
+            device_id=(lax.rem(me + k, n), other),
+            device_id_type=MESH,
+        )
+        copy.start()
+        extra_copies.append(copy)
     mine[...] = _scatter_sum(n, me, other, whole_ref, held, send_sem, recv_sem, rows).astype(
         mine.dtype
     )
@@ -145,6 +172,19 @@
         copy.start()
         copies.append(copy)
     out_ref[pl.ds(pl.multiple_of(me * rows, rows), rows), :] = mine[...]
+    extra_total = extra_ref[...]
+    for k in range(1, n):
+        source = lax.rem(me + n - k, n)
+        pltpu.make_async_remote_copy(
+            src_ref=extra_ref,
+            dst_ref=extra_held.at[k],
+            send_sem=send_extra.at[k],
+            recv_sem=recv_extra.at[k],
+            device_id=(source, other),
+            device_id_type=MESH,
+        ).wait_recv()
+        extra_total = extra_total + extra_held[k]
+    extra_out[...] = extra_total
     for k in range(1, n):
         source = lax.rem(me + n - k, n)
         pltpu.make_async_remote_copy(
@@ -155,29 +195,30 @@
             device_id=(source, other),
             device_id_type=MESH,
         ).wait_recv()
-    for copy in copies:
+    for copy in copies + extra_copies:
         copy.wait_send()
 
 
-def ctx_sum(whole, n, collective_id):
+def ctx_sum(whole, extra, n, collective_id):
     rows, cols = whole.shape[0] // n, whole.shape[1]
     return pl.pallas_call(
         functools.partial(_sum_kernel, n),
-        out_shape=jax.ShapeDtypeStruct(whole.shape, whole.dtype),
-        in_specs=[pl.BlockSpec(memory_space=pltpu.VMEM)],
-        out_specs=pl.BlockSpec(memory_space=pltpu.VMEM),
+        out_shape=(
+            jax.ShapeDtypeStruct(whole.shape, whole.dtype),
+            jax.ShapeDtypeStruct(extra.shape, extra.dtype),
+        ),
+        in_specs=[pl.BlockSpec(memory_space=pltpu.VMEM)] * 2,
+        out_specs=(pl.BlockSpec(memory_space=pltpu.VMEM),) * 2,
         scratch_shapes=[
             pltpu.VMEM((n, rows, cols), whole.dtype),
             pltpu.VMEM((rows, cols), whole.dtype),
-            pltpu.SemaphoreType.DMA((n,)),
-            pltpu.SemaphoreType.DMA((n,)),
-            pltpu.SemaphoreType.DMA((n,)),
-            pltpu.SemaphoreType.DMA((n,)),
-        ],
+            pltpu.VMEM((n,) + extra.shape, extra.dtype),
+        ]
+        + [pltpu.SemaphoreType.DMA((n,))] * 6,
         compiler_params=pltpu.CompilerParams(
             collective_id=collective_id, has_side_effects=True, vmem_limit_bytes=VMEM_LIMIT
         ),
-    )(whole)
+    )(whole, extra)
 
 
 EPS = 1e-05
@@ -438,17 +479,6 @@
     input_grad = grad_mid + through_one
     weight_parts = (grad_query, grad_key, grad_value, grad_output_t, grad_gate, grad_up, grad_down_t)
     widths = [part.shape[1] for part in weight_parts]
-    summed = ctx_sum(
-        jnp.concatenate([part.astype(jnp.bfloat16) for part in weight_parts], axis=1),
-        place_count,
-        2,
-    ).astype(jnp.float32)
-    offsets = [sum(widths[:k]) for k in range(len(widths) + 1)]
-    shared_query, shared_key, shared_value, output_t, shared_gate, shared_up, down_t = (
-        summed[:, offsets[k] : offsets[k + 1]] for k in range(len(widths))
-    )
-    shared_output = output_t.T
-    shared_down = down_t.T
     gain_parts = (
         jnp.sum(attn_terms, axis=0),
         jnp.sum(query_terms, axis=(0, 1)),
@@ -456,11 +486,26 @@
         jnp.sum(ffn_terms, axis=0),
     )
     gain_sizes = [part.shape[0] for part in gain_parts]
-    gains = lax.psum(jnp.concatenate(gain_parts), ("ctx", "tp"))
+    gain_flat = lax.psum(jnp.concatenate(gain_parts), "tp")
+    gain_pad = -gain_flat.shape[0] % 1024
+    summed, gains = ctx_sum(
+        jnp.concatenate([part.astype(jnp.bfloat16) for part in weight_parts], axis=1),
+        jnp.pad(gain_flat, (0, gain_pad)).reshape(8, -1),
+        place_count,
+        2,
+    )
+    summed = summed.astype(jnp.float32)
+    gains = gains.reshape(-1)
+    offsets = [sum(widths[:k]) for k in range(len(widths) + 1)]
+    shared_query, shared_key, shared_value, output_t, shared_gate, shared_up, down_t = (
+        summed[:, offsets[k] : offsets[k + 1]] for k in range(len(widths))
+    )
+    shared_output = output_t.T
+    shared_down = down_t.T
     gain_attn = gains[: gain_sizes[0]]
     gain_query = gains[gain_sizes[0] : gain_sizes[0] + gain_sizes[1]]
     gain_key = gains[gain_sizes[0] + gain_sizes[1] : gain_sizes[0] + gain_sizes[1] + gain_sizes[2]]
-    gain_ffn = gains[gain_sizes[0] + gain_sizes[1] + gain_sizes[2] :]
+    gain_ffn = gains[gain_sizes[0] + gain_sizes[1] + gain_sizes[2] : sum(gain_sizes)]
     return (
         block_output,
         input_grad,

time: 864 us -> 783 us (0.906)
  blocking collectives: 108 us -> 46.3 us
  Pallas kernels: 524 us -> 490 us
    psum x1, blocking collectives: 74.5 us -> 13.1 us  [per_device(): gain_flat = lax.psum(jnp.concatenate(gain_parts), 'tp')]
    pallas_call x1, Pallas kernels: 411 us -> 377 us  [ctx_sum(): pl.pallas_call(functools.partial(_sum_kernel, n), out_shape=(jax.ShapeDty...]
  transfers between devices with their start and end apart: 4 -> 4, of which waited for: 2 -> 3; matrix products, arithmetic and copies ran while one was open for 7% -> 8% of each run, Pallas kernels for 48% -> 49%
where the time goes in v4:
time: 783 us; the launch traced here: 772 us
  Pallas kernels  490 us (63%)
  local copies, waits for them, and re-layouts  79.4 us (10%)
  matrix products  50.9 us (7%)
  blocking collectives  46.3 us (6%)
  waiting for transfers between devices  45.6 us (6%)
  other arithmetic  44.3 us (6%)
  between operations  15.1 us (2%)
    pallas_call x1, Pallas kernels, ctx_sum(): pl.pallas_call(functools.partial(_sum_kernel, n), out_shape=(jax.ShapeDty...  377 us
    pallas_call x1, Pallas kernels, ctx_scatter(): pl.pallas_call(functools.partial(_scatter_kernel, n), out_shape=jax.Shape...  59.1 us
    pallas_call x1, Pallas kernels, ctx_gather(): pl.pallas_call(functools.partial(_gather_kernel, n), out_shape=jax.ShapeD...  53.2 us
    reduce_scatter x4, waiting for transfers between devices, reduce_rows(): lax.psum_scatter(partial_rows.astype(jnp.bfloat16), 'tp', scatter_dimensi...  45.5 us
    all_gather x4, blocking collectives, gather_rows(): return lax.all_gather(rows_low, 'tp', axis=0, tiled=True)  33.2 us
  transfers between devices with their start and end apart: 4, of which 3 were waited for; matrix products, arithmetic and copies ran while one was open for 8% of the time, Pallas kernels for 49%

profile of v4, /device:TPU:28, one launch (start us, length us, event | category | flops | bytes accessed | tf_op | source)
XLA Modules:
  0.0 771.6 jit_solution(12995376711367219683)
XLA Ops:
  10.2 8.1 %all_gather.12 = bf16[128,1024]{1,0:T(8,128)(2,1)S(1)} all-gather(bf16[32,1024]{1,0:T(8,128)(2,1)S(1)} %fusion.43), channel_id=1, replica_groups=mesh['ctx'=32,'tp'=4] {'tp'}, dimensions={0}, use_global_device_ids=true | all-gather | bytes 327680 | tf_op jit(solution)/shard_map/all_gather | solution.py:303
  27.0 53.2 %shard_map.237 = bf16[4096,256]{1,0:T(8,128)(2,1)} custom-call(bf16[128,256]{1,0:T(8,128)(2,1)} %pad_maximum_fusion.2.part_ref), custom_call_target="tpu_custom_call" | custom-call | tf_op jit(solution)/shard_map/pallas_call | solution.py:58
  80.2 1.7 copy.76
  81.9 1.7 fusion.82
  83.6 1.5 copy.77
  85.1 2.0 fusion.86
  88.9 1.4 subtract_convert_fusion
  90.3 1.5 concatenate.38
  91.7 1.6 copy.79
  93.4 1.5 concatenate.39
  94.8 1.6 copy.80
  97.1 1.4 multiply_add_fusion.2
  98.5 1.4 add.168
  99.9 2.3 copy.81
  103.0 2.0 fusion.2
  106.2 2.0 fusion.85
  108.2 1.7 copy.82
  109.9 1.7 convert_element_type.134
  111.6 2.0 convolution_convert_fusion.8
  113.7 10.3 %all_gather.14 = bf16[128,1024]{1,0:T(8,128)(2,1)} all-gather(bf16[32,1024]{1,0:T(8,128)(2,1)S(1)} %copy-done.33), channel_id=1, replica_groups=mesh['ctx'=32,'tp'=4] {'tp'}, dimensions={0}, use_global_device_ids=true | all-gather | bytes 327680 | tf_op jit(solution)/shard_map/all_gather | solution.py:303
  124.0 20.3 %reduce-scatter.5.cloned.1.call-done = bf16[32,1024]{1,0:T(8,128)(2,1)} async-done(((bf16[128,1024]{1,0:T(8,128)(2,1)}), bf16[32,1024]{1,0:T(8,128)(2,1)}) %reduce-scatter.5.cloned.1.call-update) | async-done | bytes 65552 | tf_op jit(solution)/shard_map/reduce_scatter | solution.py:307
  146.4 7.3 all_gather.13
  153.7 2.3 fusion.87
  156.6 1.7 multiply_convert_fusion
  159.2 1.6 fusion.31
  164.7 1.6 copy.90
  170.2 17.1 %reduce-scatter.9.cloned.1.call-done = bf16[32,1024]{1,0:T(8,128)(2,1)} async-done(((bf16[128,1024]{1,0:T(8,128)(2,1)}), bf16[32,1024]{1,0:T(8,128)(2,1)}) %reduce-scatter.9.cloned.1.call-update) | async-done | bytes 65552 | tf_op jit(solution)/shard_map/reduce_scatter | solution.py:307
  187.3 1.5 fusion.51
  190.4 7.5 all_gather.15
  198.6 2.0 convolution_convert_fusion.9
  200.5 1.6 reshape.328
  202.2 1.7 copy.84
  205.0 4.9 fusion.16
  210.0 1.7 fusion.1
  211.8 1.5 fusion.17
  213.3 1.8 convolution_bitcast_fusion.2
  215.1 4.4 reshape.330
  219.5 4.4 reshape.331
  223.9 5.0 maximum_bitcast_fusion
  229.0 5.5 copy.93
  234.5 59.1 %shard_map.238 = f32[128,256]{1,0:T(8,128)} custom-call(bf16[4096,256]{1,0:T(8,128)(2,1)} %bitcast.191), custom_call_target="tpu_custom_call" | custom-call | tf_op jit(solution)/shard_map/pallas_call | solution.py:111
  295.8 1.9 copy.85
  300.2 1.7 copy.89
  301.8 1.7 copy.86
  307.5 1.9 fusion.28
  309.7 2.2 convolution_convert_fusion.7
  312.0 2.1 fusion.27
  314.3 1.8 fusion.30
  316.0 1.9 fusion.29
  317.9 2.0 fusion.26
  319.9 3.3 fusion.8
  323.2 2.3 fusion.7
  325.5 2.4 fusion.10.whole_ref
  327.9 8.1 %reduce-scatter.11.cloned.1.call-done = bf16[32,1024]{1,0:T(8,128)(2,1)} async-done(((bf16[128,1024]{1,0:T(8,128)(2,1)}), bf16[32,1024]{1,0:T(8,128)(2,1)}) %reduce-scatter.11.cloned.1.call-update) | async-done | bytes 65552 | tf_op jit(solution)/shard_map/reduce_scatter | solution.py:307
  337.1 13.1 %psum.7 = f32[2176]{0:T(1024)S(1)} all-reduce(f32[2176]{0:T(1024)S(1)} %concatenate.47), channel_id=1, replica_groups=mesh['ctx'=32,'tp'=4] {'tp'}, use_global_device_ids=true, to_apply=%region_23.24 | all-reduce | flops 2176 | bytes 17408 | tf_op jit(solution)/shard_map/psum | solution.py:489
  350.8 377.4 %shard_map.239 = (bf16[1024,4224]{1,0:T(8,128)(2,1)}, f32[8,384]{1,0:T(8,128)}) custom-call(bf16[1024,4224]{1,0:T(8,128)(2,1)} %fusion.10.whole_ref, f32[8,384]{1,0:T(8,128)} %reshape.333.extra_ref), custom_call_target="tpu_custom_call" | custom-call | tf_op jit(solution)/shard_map/pallas_call | solution.py:204
  728.2 10.5 %convert_element_type.165 = f32[1024,4224]{1,0:T(8,128)} convert(bf16[1024,4224]{1,0:T(8,128)(2,1)} %get-tuple-element.16) | non-fusion elementwise | flops 4325376 | bytes 25952256 | tf_op jit(solution)/shard_map/convert_element_type | solution.py:497
  738.7 5.2 slice_bitcast_fusion
  743.9 1.7 slice_bitcast_fusion.1
  745.6 4.3 fusion.80
  751.0 2.1 slice.109
  753.1 6.2 copy.103
  761.2 2.1 fusion.81
  763.3 1.8 fusion.46
  (183 shorter events, 44.0 us)
Async XLA Ops:
  7.2 149.4 %copy-start = (bf16[1152,1024]{1,0:T(8,128)(2,1)S(1)}, bf16[1152,1024]{1,0:T(8,128)(2,1)}, u32[]{:S(2)}) copy-start(bf16[1152,1024]{1,0:T(8,128)(2,1)} %param.26) | copy-start | bytes 7077892
  7.2 137.1 %reduce-scatter.5.cloned.1.call-start = ((), (), s32[]{:S(2)}) async-start(), calls=%async_computation.4 | async-start | bytes 327680 | tf_op jit(solution)/shard_map/reduce_scatter | solution.py:307
  9.3 0.9 copy-start.49
  18.3 65.2 %copy-start.5 = (bf16[128,1024]{1,0:T(8,128)(2,1)}, bf16[128,1024]{1,0:T(8,128)(2,1)S(1)}, u32[]{:S(2)}) copy-start(bf16[128,1024]{1,0:T(8,128)(2,1)S(1)} %all_gather.12) | copy-start | bytes 786436
  19.7 63.9 %copy-start.29 = (f32[128,128]{0,1:T(8,128)}, f32[128,128]{0,1:T(8,128)S(1)}, u32[]{:S(2)}) copy-start(f32[128,128]{0,1:T(8,128)S(1)} %get-tuple-element.96) | copy-start | bytes 196612
  19.7 5.3 copy-start.46
  24.3 59.3 %copy-start.35 = (f32[128,32]{0,1:T(8,128)}, f32[128,32]{0,1:T(8,128)S(1)}, u32[]{:S(2)}) copy-start(f32[128,32]{0,1:T(8,128)S(1)} %get-tuple-element.94) | copy-start | bytes 49156
  88.1 16.9 %copy-start.17 = (f32[128,256]{0,1:T(8,128)}, f32[128,256]{0,1:T(8,128)S(1)}, u32[]{:S(2)}) copy-start(f32[128,256]{0,1:T(8,128)S(1)} %copy.78) | copy-start | bytes 393220
  88.1 2.1 copy-start.42
  103.0 3.2 copy-start.14
  103.0 3.2 copy-start.31
  105.0 3.2 copy-start.3
  105.1 3.2 copy-start.41
  106.2 2.0 copy-start.44
  106.2 7.5 copy-start.33
  106.2 38.1 %copy-start.11 = (bf16[32,1024]{1,0:T(8,128)(2,1)S(1)}, bf16[32,1024]{1,0:T(8,128)(2,1)}, u32[]{:S(2)}) copy-start(bf16[32,1024]{1,0:T(8,128)(2,1)} %param.14) | copy-start | bytes 196612
  113.6 73.7 %reduce-scatter.9.cloned.1.call-start = ((), (), s32[]{:S(2)}) async-start(), calls=%async_computation.6 | async-start | bytes 327680 | tf_op jit(solution)/shard_map/reduce_scatter | solution.py:307
  144.3 11.7 %copy-start.8 = (bf16[1024,1152]{1,0:T(8,128)(2,1)S(1)}, bf16[1024,1152]{1,0:T(8,128)(2,1)}, u32[]{:S(2)}) copy-start(bf16[1024,1152]{1,0:T(8,128)(2,1)} %param.25) | copy-start | bytes 7077892
  144.3 12.2 %copy-start.27 = (bf16[128,1024]{1,0:T(8,128)(2,1)S(1)}, bf16[128,1024]{1,0:T(8,128)(2,1)}, u32[]{:S(2)}) copy-start(bf16[128,1024]{1,0:T(8,128)(2,1)} %all_gather.14) | copy-start | bytes 786436
  145.5 10.5 %copy-start.47 = (f32[32]{0:T(128)}, f32[32]{0:T(128)S(1)}, u32[]{:S(2)}) copy-start(f32[32]{0:T(128)S(1)} %add_rsqrt_fusion.2) | copy-start | bytes 388
  153.7 2.3 copy-start.9
  156.0 2.3 copy-start.7
  158.3 0.9 copy-start.20
  158.3 0.9 copy-start.23
  158.3 29.0 %copy-start.19 = (bf16[32,1024]{1,0:T(8,128)(2,1)S(1)}, bf16[32,1024]{1,0:T(8,128)(2,1)}, u32[]{:S(2)}) copy-start(bf16[32,1024]{1,0:T(8,128)(2,1)} %reduce-scatter.5.cloned.1.call-done) | copy-start | bytes 196612
  160.8 175.1 %reduce-scatter.11.cloned.1.call-start = ((), (), s32[]{:S(2)}) async-start(), calls=%async_computation.7 | async-start | bytes 327680 | tf_op jit(solution)/shard_map/reduce_scatter | solution.py:307
  188.8 0.6 copy-start.53
  197.9 0.7 copy-start.12
  203.8 6.1 copy-start.4
  203.8 6.1 copy-start.15
  203.8 6.1 copy-start.32
  203.8 6.1 copy-start.34
  203.8 6.1 copy-start.51
  210.0 1.8 copy-start.25
  210.0 1.8 copy-start.26
  229.0 65.6 %copy-start.36 = (f32[128,32]{0,1:T(8,128)S(1)}, f32[128,32]{0,1:T(8,128)}, u32[]{:S(2)}) copy-start(f32[128,32]{0,1:T(8,128)} %copy-done.35) | copy-start | bytes 49156
  229.0 65.6 %copy-start.30 = (f32[128,128]{0,1:T(8,128)S(1)}, f32[128,128]{0,1:T(8,128)}, u32[]{:S(2)}) copy-start(f32[128,128]{0,1:T(8,128)} %copy-done.29) | copy-start | bytes 196612
  229.0 65.6 %copy-start.52 = (f32[64]{0:T(128)S(1)}, f32[64]{0:T(128)}, u32[]{:S(2)}) copy-start(f32[64]{0:T(128)} %param.21) | copy-start | bytes 772
  229.0 69.8 %copy-start.18 = (f32[128,256]{0,1:T(8,128)S(1)}, f32[128,256]{0,1:T(8,128)}, u32[]{:S(2)}) copy-start(f32[128,256]{0,1:T(8,128)} %copy-done.17) | copy-start | bytes 393220
  229.0 69.8 %copy-start.48 = (f32[64]{0:T(128)S(1)}, f32[64]{0:T(128)}, u32[]{:S(2)}) copy-start(f32[64]{0:T(128)} %param.20) | copy-start | bytes 772
  229.0 74.5 %copy-start.21 = (f32[128,256]{1,0:T(8,128)S(1)}, f32[128,256]{1,0:T(8,128)}, u32[]{:S(2)}) copy-start(f32[128,256]{1,0:T(8,128)} %fusion.86) | copy-start | bytes 393220
  234.5 70.1 %copy-start.16 = (bf16[1024,256]{1,0:T(8,128)(2,1)S(1)}, bf16[1024,256]{1,0:T(8,128)(2,1)}, u32[]{:S(2)}) copy-start(bf16[1024,256]{1,0:T(8,128)(2,1)} %param.17) | copy-start | bytes 1572868
  299.5 12.4 %copy-start.6 = (bf16[128,1024]{1,0:T(8,128)(2,1)S(1)}, bf16[128,1024]{1,0:T(8,128)(2,1)}, u32[]{:S(2)}) copy-start(bf16[128,1024]{1,0:T(8,128)(2,1)} %copy-done.5) | copy-start | bytes 786436
  304.6 0.6 copy-start.38
  305.2 12.7 %copy-start.13 = (bf16[128,1024]{1,0:T(8,128)(2,1)S(1)}, bf16[128,1024]{1,0:T(8,128)(2,1)}, u32[]{:S(2)}) copy-start(bf16[128,1024]{1,0:T(8,128)(2,1)} %copy-done.12) | copy-start | bytes 786436
  306.2 5.7 copy-start.37
  306.2 13.7 %copy-start.10 = (bf16[128,1024]{1,0:T(8,128)(2,1)S(1)}, bf16[128,1024]{1,0:T(8,128)(2,1)}, u32[]{:S(2)}) copy-start(bf16[128,1024]{1,0:T(8,128)(2,1)} %copy-done.9) | copy-start | bytes 786436
  309.4 453.9 %reduce-scatter.7.cloned.1.call-start = ((), (), s32[]{:S(2)}) async-start(), calls=%async_computation.5 | async-start | bytes 327680 | tf_op jit(solution)/shard_map/reduce_scatter | solution.py:307
  311.9 11.3 %copy-start.24 = (bf16[128,1152]{1,0:T(8,128)(2,1)S(1)}, bf16[128,1152]{1,0:T(8,128)(2,1)}, u32[]{:S(2)}) copy-start(bf16[128,1152]{1,0:T(8,128)(2,1)} %copy-done.23) | copy-start | bytes 884740
  311.9 13.6 %copy-start.22 = (bf16[128,1152]{1,0:T(8,128)(2,1)S(1)}, bf16[128,1152]{1,0:T(8,128)(2,1)}, u32[]{:S(2)}) copy-start(bf16[128,1152]{1,0:T(8,128)(2,1)} %get-tuple-element.70) | copy-start | bytes 884740
  311.9 13.5 %copy-start.28 = (bf16[128,1024]{1,0:T(8,128)(2,1)S(1)}, bf16[128,1024]{1,0:T(8,128)(2,1)}, u32[]{:S(2)}) copy-start(bf16[128,1024]{1,0:T(8,128)(2,1)} %all_gather.14) | copy-start | bytes 786436
  319.9 16.0 %copy-start.40 = (f32[1024]{0:T(1024)S(1)}, f32[1024]{0:T(1024)}, u32[]{:S(2)}) copy-start(f32[1024]{0:T(1024)} %param.16) | copy-start | bytes 12292
  319.9 16.0 %copy-start.50 = (f32[32]{0:T(128)S(1)}, f32[32]{0:T(128)}, u32[]{:S(2)}) copy-start(f32[32]{0:T(128)} %copy-done.49) | copy-start | bytes 388
  319.9 17.0 %copy-start.43 = (f32[1024]{0:T(1024)S(1)}, f32[1024]{0:T(1024)}, u32[]{:S(2)}) copy-start(f32[1024]{0:T(1024)} %get-tuple-element.56) | copy-start | bytes 12292
  738.7 6.9 copy-start.2
  745.6 4.4 copy-start.45
  753.1 11.9 %copy-start.1 = (bf16[1152,1024]{1,0:T(8,128)(2,1)S(1)}, bf16[1152,1024]{1,0:T(8,128)(2,1)}, u32[]{:S(2)}) copy-start(bf16[1152,1024]{1,0:T(8,128)(2,1)} %param.26) | copy-start | bytes 7077892
  759.3 4.0 copy-start.39
Sparse Core Ops, SparseCore 0:
  113.7 30.5 reduce-scatter.4
  160.9 26.2 reduce-scatter.8
  309.6 26.3 reduce-scatter.10
  338.5 28.5 reduce-scatter.6

commit v5 on v4

--- a/solution.py
+++ b/solution.py
@@ -12,9 +12,18 @@
 VMEM_LIMIT = 60 * 1024 * 1024
 
 
+def _shifts(n):
+    order = []
+    for k in range(1, n // 2 + 1):
+        order.append(k)
+        if n - k != k:
+            order.append(n - k)
+    return order
+
+
 def _enter(n, me, peer_axis):
     barrier = pltpu.get_barrier_semaphore()
-    for k in range(1, n):
+    for k in _shifts(n):
         pl.semaphore_signal(
             barrier, 1, device_id=(lax.rem(me + k, n), peer_axis), device_id_type=MESH
         )
@@ -27,7 +36,7 @@
     rows = part_ref.shape[0]
     _enter(n, me, other)
     copies = []
-    for k in range(1, n):
+    for k in _shifts(n):
         copy = pltpu.make_async_remote_copy(
             src_ref=part_ref,
             dst_ref=out_ref.at[pl.ds(pl.multiple_of(me * rows, rows), rows)],
@@ -39,7 +48,7 @@
         copy.start()
         copies.append(copy)
     out_ref[pl.ds(pl.multiple_of(me * rows, rows), rows), :] = part_ref[...]
-    for k in range(1, n):
+    for k in _shifts(n):
         source = lax.rem(me + n - k, n)
         pltpu.make_async_remote_copy(
             src_ref=part_ref,
@@ -69,7 +78,7 @@
 
 def _scatter_sum(n, me, other, whole_ref, held, send_sem, recv_sem, rows):
     copies = []
-    for k in range(1, n):
+    for k in _shifts(n):
         target = lax.rem(me + k, n)
         copy = pltpu.make_async_remote_copy(
             src_ref=whole_ref.at[pl.ds(pl.multiple_of(target * rows, rows), rows)],
@@ -82,7 +91,7 @@
         copy.start()
         copies.append(copy)
     total = whole_ref[pl.ds(pl.multiple_of(me * rows, rows), rows), :].astype(jnp.float32)
-    for k in range(1, n):
+    for k in _shifts(n):
         source = lax.rem(me + n - k, n)
         pltpu.make_async_remote_copy(
             src_ref=whole_ref.at[pl.ds(0, rows)],
@@ -145,7 +154,7 @@
     rows = whole_ref.shape[0] // n
     _enter(n, me, other)
     extra_copies = []
-    for k in range(1, n):
+    for k in _shifts(n):
         copy = pltpu.make_async_remote_copy(
             src_ref=extra_ref,
             dst_ref=extra_held.at[k],
@@ -160,7 +169,7 @@
         mine.dtype
     )
     copies = []
-    for k in range(1, n):
+    for k in _shifts(n):
         copy = pltpu.make_async_remote_copy(
             src_ref=mine,
             dst_ref=out_ref.at[pl.ds(pl.multiple_of(me * rows, rows), rows)],
@@ -173,7 +182,7 @@
         copies.append(copy)
     out_ref[pl.ds(pl.multiple_of(me * rows, rows), rows), :] = mine[...]
     extra_total = extra_ref[...]
-    for k in range(1, n):
+    for k in _shifts(n):
         source = lax.rem(me + n - k, n)
         pltpu.make_async_remote_copy(
             src_ref=extra_ref,
@@ -185,7 +194,7 @@
         ).wait_recv()
         extra_total = extra_total + extra_held[k]
     extra_out[...] = extra_total
-    for k in range(1, n):
+    for k in _shifts(n):
         source = lax.rem(me + n - k, n)
         pltpu.make_async_remote_copy(
             src_ref=mine,

time: 783 us -> 710 us (0.907); the launches traced: 772 us -> 708 us
  Pallas kernels: 490 us -> 428 us
    pallas_call x1, Pallas kernels: 377 us -> 343 us  [ctx_sum(): pl.pallas_call(functools.partial(_sum_kernel, n), out_shape=(jax.ShapeDty...]
    pallas_call x1, Pallas kernels: 59.1 us -> 42.9 us  [ctx_scatter(): pl.pallas_call(functools.partial(_scatter_kernel, n), out_shape=jax.Shape...]
    pallas_call x1, Pallas kernels: 53.2 us -> 42.1 us  [ctx_gather(): pl.pallas_call(functools.partial(_gather_kernel, n), out_shape=jax.ShapeD...]
  transfers between devices with their start and end apart: 4 -> 4, of which waited for: 3 -> 3; matrix products, arithmetic and copies ran while one was open for 8% -> 9% of each run, Pallas kernels for 49% -> 48%
where the time goes in v5:
time: 710 us; the launch traced here: 708 us
  Pallas kernels  428 us (60%)
  local copies, waits for them, and re-layouts  79.4 us (11%)
  matrix products  50.9 us (7%)
  waiting for transfers between devices  45.6 us (6%)
  other arithmetic  44.3 us (6%)
  blocking collectives  44 us (6%)
  between operations  15.1 us (2%)
    pallas_call x1, Pallas kernels, ctx_sum(): pl.pallas_call(functools.partial(_sum_kernel, n), out_shape=(jax.ShapeDty...  343 us
    reduce_scatter x4, waiting for transfers between devices, reduce_rows(): lax.psum_scatter(partial_rows.astype(jnp.bfloat16), 'tp', scatter_dimensi...  45.5 us
    pallas_call x1, Pallas kernels, ctx_scatter(): pl.pallas_call(functools.partial(_scatter_kernel, n), out_shape=jax.Shape...  42.9 us
    pallas_call x1, Pallas kernels, ctx_gather(): pl.pallas_call(functools.partial(_gather_kernel, n), out_shape=jax.ShapeD...  42.1 us
    all_gather x4, blocking collectives, gather_rows(): return lax.all_gather(rows_low, 'tp', axis=0, tiled=True)  30.9 us
  transfers between devices with their start and end apart: 4, of which 3 were waited for; matrix products, arithmetic and copies ran while one was open for 9% of the time, Pallas kernels for 48%

profile of v5, /device:TPU:28, one launch (start us, length us, event | category | flops | bytes accessed | tf_op | source)
XLA Modules:
  0.0 707.8 jit_solution(7528856298684981173)
XLA Ops:
  10.2 8.1 %all_gather.12 = bf16[128,1024]{1,0:T(8,128)(2,1)S(1)} all-gather(bf16[32,1024]{1,0:T(8,128)(2,1)S(1)} %fusion.43), channel_id=1, replica_groups=mesh['ctx'=32,'tp'=4] {'tp'}, dimensions={0}, use_global_device_ids=true | all-gather | bytes 327680 | tf_op jit(solution)/shard_map/all_gather | solution.py:312
  27.0 42.1 %shard_map.237 = bf16[4096,256]{1,0:T(8,128)(2,1)} custom-call(bf16[128,256]{1,0:T(8,128)(2,1)} %pad_maximum_fusion.2.part_ref), custom_call_target="tpu_custom_call" | custom-call | tf_op jit(solution)/shard_map/pallas_call | solution.py:67
  69.1 1.7 copy.76
  70.8 1.7 fusion.82
  72.5 1.5 copy.77
  74.0 2.0 fusion.86
  77.8 1.4 subtract_convert_fusion
  79.2 1.5 concatenate.38
  80.7 1.6 copy.79
  82.3 1.5 concatenate.39
  83.8 1.6 copy.80
  86.0 1.4 multiply_add_fusion.2
  87.4 1.4 add.168
  88.8 2.3 copy.81
  91.9 2.0 fusion.2
  95.2 2.0 fusion.85
  97.2 1.7 copy.82
  98.9 1.7 convert_element_type.134
  100.5 2.0 convolution_convert_fusion.8
  102.6 8.0 %all_gather.14 = bf16[128,1024]{1,0:T(8,128)(2,1)} all-gather(bf16[32,1024]{1,0:T(8,128)(2,1)S(1)} %copy-done.33), channel_id=1, replica_groups=mesh['ctx'=32,'tp'=4] {'tp'}, dimensions={0}, use_global_device_ids=true | all-gather | bytes 327680 | tf_op jit(solution)/shard_map/all_gather | solution.py:312
  110.6 20.3 %reduce-scatter.5.cloned.1.call-done = bf16[32,1024]{1,0:T(8,128)(2,1)} async-done(((bf16[128,1024]{1,0:T(8,128)(2,1)}), bf16[32,1024]{1,0:T(8,128)(2,1)}) %reduce-scatter.5.cloned.1.call-update) | async-done | bytes 65552 | tf_op jit(solution)/shard_map/reduce_scatter | solution.py:316
  133.0 7.3 %all_gather.13 = bf16[128,1024]{1,0:T(8,128)(2,1)S(1)} all-gather(bf16[32,1024]{1,0:T(8,128)(2,1)S(1)} %multiply_convert_fusion.3), channel_id=1, replica_groups=mesh['ctx'=32,'tp'=4] {'tp'}, dimensions={0}, use_global_device_ids=true | all-gather | bytes 327680 | tf_op jit(solution)/shard_map/all_gather | solution.py:312
  140.3 2.3 fusion.87
  143.2 1.7 multiply_convert_fusion
  145.8 1.6 fusion.31
  151.3 1.6 copy.90
  156.8 17.1 %reduce-scatter.9.cloned.1.call-done = bf16[32,1024]{1,0:T(8,128)(2,1)} async-done(((bf16[128,1024]{1,0:T(8,128)(2,1)}), bf16[32,1024]{1,0:T(8,128)(2,1)}) %reduce-scatter.9.cloned.1.call-update) | async-done | bytes 65552 | tf_op jit(solution)/shard_map/reduce_scatter | solution.py:316
  173.9 1.5 fusion.51
  177.0 7.5 %all_gather.15 = bf16[128,1024]{1,0:T(8,128)(2,1)S(1)} all-gather(bf16[32,1024]{1,0:T(8,128)(2,1)S(1)} %fusion.77), channel_id=1, replica_groups=mesh['ctx'=32,'tp'=4] {'tp'}, dimensions={0}, use_global_device_ids=true | all-gather | bytes 327680 | tf_op jit(solution)/shard_map/all_gather | solution.py:312
  185.2 2.0 convolution_convert_fusion.9
  187.2 1.6 reshape.328
  188.8 1.7 copy.84
  191.7 4.9 fusion.16
  196.7 1.7 fusion.1
  198.4 1.5 fusion.17
  200.0 1.8 convolution_bitcast_fusion.2
  201.8 4.4 reshape.330
  206.2 4.4 reshape.331
  210.6 5.0 maximum_bitcast_fusion
  215.6 5.5 copy.93
  221.2 42.9 %shard_map.238 = f32[128,256]{1,0:T(8,128)} custom-call(bf16[4096,256]{1,0:T(8,128)(2,1)} %bitcast.191), custom_call_target="tpu_custom_call" | custom-call | tf_op jit(solution)/shard_map/pallas_call | solution.py:120
  266.3 1.9 copy.85
  270.7 1.7 copy.89
  272.3 1.7 copy.86
  278.0 1.9 fusion.28
  280.2 2.2 convolution_convert_fusion.7
  282.4 2.1 fusion.27
  284.7 1.8 fusion.30
  286.5 1.9 fusion.29
  288.4 2.0 fusion.26
  290.4 3.3 fusion.8
  293.7 2.3 fusion.7
  296.0 2.4 fusion.10.whole_ref
  298.3 8.0 %reduce-scatter.11.cloned.1.call-done = bf16[32,1024]{1,0:T(8,128)(2,1)} async-done(((bf16[128,1024]{1,0:T(8,128)(2,1)}), bf16[32,1024]{1,0:T(8,128)(2,1)}) %reduce-scatter.11.cloned.1.call-update) | async-done | bytes 65552 | tf_op jit(solution)/shard_map/reduce_scatter | solution.py:316
  307.5 13.1 %psum.7 = f32[2176]{0:T(1024)S(1)} all-reduce(f32[2176]{0:T(1024)S(1)} %concatenate.47), channel_id=1, replica_groups=mesh['ctx'=32,'tp'=4] {'tp'}, use_global_device_ids=true, to_apply=%region_23.24 | all-reduce | flops 2176 | bytes 17408 | tf_op jit(solution)/shard_map/psum | solution.py:498
  321.2 343.2 %shard_map.239 = (bf16[1024,4224]{1,0:T(8,128)(2,1)}, f32[8,384]{1,0:T(8,128)}) custom-call(bf16[1024,4224]{1,0:T(8,128)(2,1)} %fusion.10.whole_ref, f32[8,384]{1,0:T(8,128)} %reshape.333.extra_ref), custom_call_target="tpu_custom_call" | custom-call | tf_op jit(solution)/shard_map/pallas_call | solution.py:213
  664.4 10.5 %convert_element_type.165 = f32[1024,4224]{1,0:T(8,128)} convert(bf16[1024,4224]{1,0:T(8,128)(2,1)} %get-tuple-element.16) | non-fusion elementwise | flops 4325376 | bytes 25952256 | tf_op jit(solution)/shard_map/convert_element_type | solution.py:506
  674.9 5.2 slice_bitcast_fusion
  680.1 1.7 slice_bitcast_fusion.1
  681.8 4.3 fusion.80
  687.3 2.1 slice.109
  689.4 6.2 copy.103
  697.5 2.1 fusion.81
  699.6 1.8 fusion.46
  (183 shorter events, 44.0 us)
Async XLA Ops:
  7.2 136.0 %copy-start = (bf16[1152,1024]{1,0:T(8,128)(2,1)S(1)}, bf16[1152,1024]{1,0:T(8,128)(2,1)}, u32[]{:S(2)}) copy-start(bf16[1152,1024]{1,0:T(8,128)(2,1)} %param.26) | copy-start | bytes 7077892
  7.2 123.7 %reduce-scatter.5.cloned.1.call-start = ((), (), s32[]{:S(2)}) async-start(), calls=%async_computation.4 | async-start | bytes 327680 | tf_op jit(solution)/shard_map/reduce_scatter | solution.py:316
  9.3 0.9 copy-start.49
  18.3 54.2 %copy-start.5 = (bf16[128,1024]{1,0:T(8,128)(2,1)}, bf16[128,1024]{1,0:T(8,128)(2,1)S(1)}, u32[]{:S(2)}) copy-start(bf16[128,1024]{1,0:T(8,128)(2,1)S(1)} %all_gather.12) | copy-start | bytes 786436
  19.7 52.8 %copy-start.29 = (f32[128,128]{0,1:T(8,128)}, f32[128,128]{0,1:T(8,128)S(1)}, u32[]{:S(2)}) copy-start(f32[128,128]{0,1:T(8,128)S(1)} %get-tuple-element.96) | copy-start | bytes 196612
  19.7 5.3 copy-start.46
  24.3 48.3 %copy-start.35 = (f32[128,32]{0,1:T(8,128)}, f32[128,32]{0,1:T(8,128)S(1)}, u32[]{:S(2)}) copy-start(f32[128,32]{0,1:T(8,128)S(1)} %get-tuple-element.94) | copy-start | bytes 49156
  77.0 16.9 %copy-start.17 = (f32[128,256]{0,1:T(8,128)}, f32[128,256]{0,1:T(8,128)S(1)}, u32[]{:S(2)}) copy-start(f32[128,256]{0,1:T(8,128)S(1)} %copy.78) | copy-start | bytes 393220
  77.1 2.1 copy-start.42
  91.9 3.2 copy-start.14
  91.9 3.2 copy-start.31
  94.0 3.2 copy-start.3
  94.0 3.2 copy-start.41
  95.1 2.0 copy-start.44
  95.1 7.5 %copy-start.33 = (bf16[32,1024]{1,0:T(8,128)(2,1)S(1)}, bf16[32,1024]{1,0:T(8,128)(2,1)}, u32[]{:S(2)}) copy-start(bf16[32,1024]{1,0:T(8,128)(2,1)} %param.27) | copy-start | bytes 196612
  95.1 35.8 %copy-start.11 = (bf16[32,1024]{1,0:T(8,128)(2,1)S(1)}, bf16[32,1024]{1,0:T(8,128)(2,1)}, u32[]{:S(2)}) copy-start(bf16[32,1024]{1,0:T(8,128)(2,1)} %param.14) | copy-start | bytes 196612
  102.6 71.4 %reduce-scatter.9.cloned.1.call-start = ((), (), s32[]{:S(2)}) async-start(), calls=%async_computation.6 | async-start | bytes 327680 | tf_op jit(solution)/shard_map/reduce_scatter | solution.py:316
  130.9 11.7 %copy-start.8 = (bf16[1024,1152]{1,0:T(8,128)(2,1)S(1)}, bf16[1024,1152]{1,0:T(8,128)(2,1)}, u32[]{:S(2)}) copy-start(bf16[1024,1152]{1,0:T(8,128)(2,1)} %param.25) | copy-start | bytes 7077892
  130.9 12.2 %copy-start.27 = (bf16[128,1024]{1,0:T(8,128)(2,1)S(1)}, bf16[128,1024]{1,0:T(8,128)(2,1)}, u32[]{:S(2)}) copy-start(bf16[128,1024]{1,0:T(8,128)(2,1)} %all_gather.14) | copy-start | bytes 786436
  132.1 10.5 %copy-start.47 = (f32[32]{0:T(128)}, f32[32]{0:T(128)S(1)}, u32[]{:S(2)}) copy-start(f32[32]{0:T(128)S(1)} %add_rsqrt_fusion.2) | copy-start | bytes 388
  140.3 2.3 copy-start.9
  142.6 2.3 copy-start.7
  144.9 0.9 copy-start.20
  144.9 0.9 copy-start.23
  144.9 29.0 %copy-start.19 = (bf16[32,1024]{1,0:T(8,128)(2,1)S(1)}, bf16[32,1024]{1,0:T(8,128)(2,1)}, u32[]{:S(2)}) copy-start(bf16[32,1024]{1,0:T(8,128)(2,1)} %reduce-scatter.5.cloned.1.call-done) | copy-start | bytes 196612
  147.4 158.9 %reduce-scatter.11.cloned.1.call-start = ((), (), s32[]{:S(2)}) async-start(), calls=%async_computation.7 | async-start | bytes 327680 | tf_op jit(solution)/shard_map/reduce_scatter | solution.py:316
  175.5 0.6 copy-start.53
  184.5 0.7 copy-start.12
  190.5 6.1 copy-start.4
  190.5 6.1 copy-start.15
  190.5 6.1 copy-start.32
  190.5 6.1 copy-start.34
  190.5 6.1 copy-start.51
  196.6 1.8 copy-start.25
  196.6 1.8 copy-start.26
  215.6 49.4 %copy-start.36 = (f32[128,32]{0,1:T(8,128)S(1)}, f32[128,32]{0,1:T(8,128)}, u32[]{:S(2)}) copy-start(f32[128,32]{0,1:T(8,128)} %copy-done.35) | copy-start | bytes 49156
  215.6 49.4 %copy-start.30 = (f32[128,128]{0,1:T(8,128)S(1)}, f32[128,128]{0,1:T(8,128)}, u32[]{:S(2)}) copy-start(f32[128,128]{0,1:T(8,128)} %copy-done.29) | copy-start | bytes 196612
  215.6 49.5 %copy-start.52 = (f32[64]{0:T(128)S(1)}, f32[64]{0:T(128)}, u32[]{:S(2)}) copy-start(f32[64]{0:T(128)} %param.21) | copy-start | bytes 772
  215.6 53.7 %copy-start.18 = (f32[128,256]{0,1:T(8,128)S(1)}, f32[128,256]{0,1:T(8,128)}, u32[]{:S(2)}) copy-start(f32[128,256]{0,1:T(8,128)} %copy-done.17) | copy-start | bytes 393220
  215.6 53.7 %copy-start.48 = (f32[64]{0:T(128)S(1)}, f32[64]{0:T(128)}, u32[]{:S(2)}) copy-start(f32[64]{0:T(128)} %param.20) | copy-start | bytes 772
  215.6 58.3 %copy-start.21 = (f32[128,256]{1,0:T(8,128)S(1)}, f32[128,256]{1,0:T(8,128)}, u32[]{:S(2)}) copy-start(f32[128,256]{1,0:T(8,128)} %fusion.86) | copy-start | bytes 393220
  221.2 53.9 %copy-start.16 = (bf16[1024,256]{1,0:T(8,128)(2,1)S(1)}, bf16[1024,256]{1,0:T(8,128)(2,1)}, u32[]{:S(2)}) copy-start(bf16[1024,256]{1,0:T(8,128)(2,1)} %param.17) | copy-start | bytes 1572868
  270.0 12.4 %copy-start.6 = (bf16[128,1024]{1,0:T(8,128)(2,1)S(1)}, bf16[128,1024]{1,0:T(8,128)(2,1)}, u32[]{:S(2)}) copy-start(bf16[128,1024]{1,0:T(8,128)(2,1)} %copy-done.5) | copy-start | bytes 786436
  275.1 0.6 copy-start.38
  275.7 12.7 %copy-start.13 = (bf16[128,1024]{1,0:T(8,128)(2,1)S(1)}, bf16[128,1024]{1,0:T(8,128)(2,1)}, u32[]{:S(2)}) copy-start(bf16[128,1024]{1,0:T(8,128)(2,1)} %copy-done.12) | copy-start | bytes 786436
  276.7 5.7 copy-start.37
  276.7 13.7 %copy-start.10 = (bf16[128,1024]{1,0:T(8,128)(2,1)S(1)}, bf16[128,1024]{1,0:T(8,128)(2,1)}, u32[]{:S(2)}) copy-start(bf16[128,1024]{1,0:T(8,128)(2,1)} %copy-done.9) | copy-start | bytes 786436
  279.9 419.6 %reduce-scatter.7.cloned.1.call-start = ((), (), s32[]{:S(2)}) async-start(), calls=%async_computation.5 | async-start | bytes 327680 | tf_op jit(solution)/shard_map/reduce_scatter | solution.py:316
  282.4 11.3 %copy-start.24 = (bf16[128,1152]{1,0:T(8,128)(2,1)S(1)}, bf16[128,1152]{1,0:T(8,128)(2,1)}, u32[]{:S(2)}) copy-start(bf16[128,1152]{1,0:T(8,128)(2,1)} %copy-done.23) | copy-start | bytes 884740
  282.4 13.6 %copy-start.22 = (bf16[128,1152]{1,0:T(8,128)(2,1)S(1)}, bf16[128,1152]{1,0:T(8,128)(2,1)}, u32[]{:S(2)}) copy-start(bf16[128,1152]{1,0:T(8,128)(2,1)} %get-tuple-element.70) | copy-start | bytes 884740
  282.4 13.5 %copy-start.28 = (bf16[128,1024]{1,0:T(8,128)(2,1)S(1)}, bf16[128,1024]{1,0:T(8,128)(2,1)}, u32[]{:S(2)}) copy-start(bf16[128,1024]{1,0:T(8,128)(2,1)} %all_gather.14) | copy-start | bytes 786436
  290.4 16.0 %copy-start.40 = (f32[1024]{0:T(1024)S(1)}, f32[1024]{0:T(1024)}, u32[]{:S(2)}) copy-start(f32[1024]{0:T(1024)} %param.16) | copy-start | bytes 12292
  290.4 16.0 %copy-start.50 = (f32[32]{0:T(128)S(1)}, f32[32]{0:T(128)}, u32[]{:S(2)}) copy-start(f32[32]{0:T(128)} %copy-done.49) | copy-start | bytes 388
  290.4 17.0 %copy-start.43 = (f32[1024]{0:T(1024)S(1)}, f32[1024]{0:T(1024)}, u32[]{:S(2)}) copy-start(f32[1024]{0:T(1024)} %get-tuple-element.56) | copy-start | bytes 12292
  674.9 6.9 copy-start.2
  681.8 4.4 copy-start.45
  689.4 11.9 %copy-start.1 = (bf16[1152,1024]{1,0:T(8,128)(2,1)S(1)}, bf16[1152,1024]{1,0:T(8,128)(2,1)}, u32[]{:S(2)}) copy-start(bf16[1152,1024]{1,0:T(8,128)(2,1)} %param.26) | copy-start | bytes 7077892
  695.6 4.0 copy-start.39
Sparse Core Ops, SparseCore 0:
  102.7 28.2 reduce-scatter.4
  147.6 26.3 reduce-scatter.8
  280.0 26.2 reduce-scatter.10
  309.0 63.4 reduce-scatter.6

commit v6 on v5

--- a/solution.py
+++ b/solution.py
@@ -133,27 +133,17 @@
     )(whole)
 
 
-def _sum_kernel(
-    n,
-    whole_ref,
-    extra_ref,
-    out_ref,
-    extra_out,
-    held,
-    mine,
-    extra_held,
-    send_sem,
-    recv_sem,
-    send_back,
-    recv_back,
-    send_extra,
-    recv_extra,
-):
+def _sum_kernel(n, spans, whole_ref, extra_ref, out_ref, extra_out, *scratch):
+    pieces = len(spans)
+    helds, mines, extra_held = scratch[:pieces], scratch[pieces : 2 * pieces], scratch[2 * pieces]
+    sems = scratch[2 * pieces + 1 :]
+    send_extra, recv_extra = sems[4 * pieces], sems[4 * pieces + 1]
     me = lax.axis_index("ctx")
     other = lax.axis_index("tp")
     rows = whole_ref.shape[0] // n
+    own_rows = pl.ds(pl.multiple_of(me * rows, rows), rows)
     _enter(n, me, other)
-    extra_copies = []
+    sent = []
     for k in _shifts(n):
         copy = pltpu.make_async_remote_copy(
             src_ref=extra_ref,
@@ -164,66 +154,93 @@
             device_id_type=MESH,
         )
         copy.start()
-        extra_copies.append(copy)
-    mine[...] = _scatter_sum(n, me, other, whole_ref, held, send_sem, recv_sem, rows).astype(
-        mine.dtype
-    )
-    copies = []
-    for k in _shifts(n):
-        copy = pltpu.make_async_remote_copy(
-            src_ref=mine,
-            dst_ref=out_ref.at[pl.ds(pl.multiple_of(me * rows, rows), rows)],
-            send_sem=send_back.at[k],
-            recv_sem=recv_back.at[k],
-            device_id=(lax.rem(me + k, n), other),
-            device_id_type=MESH,
-        )
-        copy.start()
-        copies.append(copy)
-    out_ref[pl.ds(pl.multiple_of(me * rows, rows), rows), :] = mine[...]
+        sent.append(copy)
+    for piece, (first, width) in enumerate(spans):
+        for k in _shifts(n):
+            target = lax.rem(me + k, n)
+            copy = pltpu.make_async_remote_copy(
+                src_ref=whole_ref.at[
+                    pl.ds(pl.multiple_of(target * rows, rows), rows), pl.ds(first, width)
+                ],
+                dst_ref=helds[piece].at[k],
+                send_sem=sems[4 * piece].at[k],
+                recv_sem=sems[4 * piece + 1].at[k],
+                device_id=(target, other),
+                device_id_type=MESH,
+            )
+            copy.start()
+            sent.append(copy)
+    for piece, (first, width) in enumerate(spans):
+        total = whole_ref[own_rows, pl.ds(first, width)].astype(jnp.float32)
+        for k in _shifts(n):
+            pltpu.make_async_remote_copy(
+                src_ref=whole_ref.at[pl.ds(0, rows), pl.ds(first, width)],
+                dst_ref=helds[piece].at[k],
+                send_sem=sems[4 * piece].at[k],
+                recv_sem=sems[4 * piece + 1].at[k],
+                device_id=(lax.rem(me + n - k, n), other),
+                device_id_type=MESH,
+            ).wait_recv()
+            total = total + helds[piece][k].astype(jnp.float32)
+        mines[piece][...] = total.astype(mines[piece].dtype)
+        for k in _shifts(n):
+            copy = pltpu.make_async_remote_copy(
+                src_ref=mines[piece],
+                dst_ref=out_ref.at[own_rows, pl.ds(first, width)],
+                send_sem=sems[4 * piece + 2].at[k],
+                recv_sem=sems[4 * piece + 3].at[k],
+                device_id=(lax.rem(me + k, n), other),
+                device_id_type=MESH,
+            )
+            copy.start()
+            sent.append(copy)
+        out_ref[own_rows, pl.ds(first, width)] = mines[piece][...]
     extra_total = extra_ref[...]
     for k in _shifts(n):
-        source = lax.rem(me + n - k, n)
         pltpu.make_async_remote_copy(
             src_ref=extra_ref,
             dst_ref=extra_held.at[k],
             send_sem=send_extra.at[k],
             recv_sem=recv_extra.at[k],
-            device_id=(source, other),
+            device_id=(lax.rem(me + n - k, n), other),
             device_id_type=MESH,
         ).wait_recv()
         extra_total = extra_total + extra_held[k]
     extra_out[...] = extra_total
-    for k in _shifts(n):
-        source = lax.rem(me + n - k, n)
-        pltpu.make_async_remote_copy(
-            src_ref=mine,
-            dst_ref=out_ref.at[pl.ds(pl.multiple_of(source * rows, rows), rows)],
-            send_sem=send_back.at[k],
-            recv_sem=recv_back.at[k],
-            device_id=(source, other),
-            device_id_type=MESH,
-        ).wait_recv()
-    for copy in copies + extra_copies:
+    for piece, (first, width) in enumerate(spans):
+        for k in _shifts(n):
+            source = lax.rem(me + n - k, n)
+            pltpu.make_async_remote_copy(
+                src_ref=mines[piece],
+                dst_ref=out_ref.at[
+                    pl.ds(pl.multiple_of(source * rows, rows), rows), pl.ds(first, width)
+                ],
+                send_sem=sems[4 * piece + 2].at[k],
+                recv_sem=sems[4 * piece + 3].at[k],
+                device_id=(source, other),
+                device_id_type=MESH,
+            ).wait_recv()
+    for copy in sent:
         copy.wait_send()
 
 
-def ctx_sum(whole, extra, n, collective_id):
+def ctx_sum(whole, extra, n, collective_id, pieces=2):
     rows, cols = whole.shape[0] // n, whole.shape[1]
+    lanes = cols // 128
+    edges = [128 * (lanes * p // pieces) for p in range(pieces + 1)]
+    spans = tuple((edges[p], edges[p + 1] - edges[p]) for p in range(pieces))
     return pl.pallas_call(
-        functools.partial(_sum_kernel, n),
+        functools.partial(_sum_kernel, n, spans),
         out_shape=(
             jax.ShapeDtypeStruct(whole.shape, whole.dtype),
             jax.ShapeDtypeStruct(extra.shape, extra.dtype),
         ),
         in_specs=[pl.BlockSpec(memory_space=pltpu.VMEM)] * 2,
         out_specs=(pl.BlockSpec(memory_space=pltpu.VMEM),) * 2,
-        scratch_shapes=[
-            pltpu.VMEM((n, rows, cols), whole.dtype),
-            pltpu.VMEM((rows, cols), whole.dtype),
-            pltpu.VMEM((n,) + extra.shape, extra.dtype),
-        ]
-        + [pltpu.SemaphoreType.DMA((n,))] * 6,
+        scratch_shapes=[pltpu.VMEM((n, rows, width), whole.dtype) for _, width in spans]
+        + [pltpu.VMEM((rows, width), whole.dtype) for _, width in spans]
+        + [pltpu.VMEM((n,) + extra.shape, extra.dtype)]
+        + [pltpu.SemaphoreType.DMA((n,))] * (4 * pieces + 2),
         compiler_params=pltpu.CompilerParams(
             collective_id=collective_id, has_side_effects=True, vmem_limit_bytes=VMEM_LIMIT
         ),

time: 710 us -> 656 us (0.924)
  Pallas kernels: 428 us -> 370 us
    pallas_call x1, Pallas kernels: 343 us -> 285 us  [ctx_sum(): pl.pallas_call(functools.partial(_sum_kernel, n, spans), out_shape=(jax.S...]
  transfers between devices with their start and end apart: 4 -> 4, of which waited for: 3 -> 3; matrix products, arithmetic and copies ran while one was open for 9% -> 10% of each run, Pallas kernels for 48% -> 44%
where the time goes in v6:
time: 656 us; the launch traced here: 650 us
  Pallas kernels  370 us (56%)
  local copies, waits for them, and re-layouts  79.4 us (12%)
  matrix products  50.9 us (8%)
  waiting for transfers between devices  45.6 us (7%)
  other arithmetic  44.3 us (7%)
  blocking collectives  44 us (7%)
  between operations  15.1 us (2%)
    pallas_call x1, Pallas kernels, ctx_sum(): pl.pallas_call(functools.partial(_sum_kernel, n, spans), out_shape=(jax.S...  285 us
    reduce_scatter x4, waiting for transfers between devices, reduce_rows(): lax.psum_scatter(partial_rows.astype(jnp.bfloat16), 'tp', scatter_dimensi...  45.5 us
    pallas_call x1, Pallas kernels, ctx_scatter(): pl.pallas_call(functools.partial(_scatter_kernel, n), out_shape=jax.Shape...  42.9 us
    pallas_call x1, Pallas kernels, ctx_gather(): pl.pallas_call(functools.partial(_gather_kernel, n), out_shape=jax.ShapeD...  42.1 us
    all_gather x4, blocking collectives, gather_rows(): return lax.all_gather(rows_low, 'tp', axis=0, tiled=True)  30.9 us
    psum x1, blocking collectives, per_device(): gain_flat = lax.psum(jnp.concatenate(gain_parts), 'tp')  13.1 us
  transfers between devices with their start and end apart: 4, of which 3 were waited for; matrix products, arithmetic and copies ran while one was open for 10% of the time, Pallas kernels for 44%

profile of v6, /device:TPU:28, one launch (start us, length us, event | category | flops | bytes accessed | tf_op | source)
XLA Modules:
  0.0 650.0 jit_solution(10888320704321061381)
XLA Ops:
  10.2 8.1 %all_gather.12 = bf16[128,1024]{1,0:T(8,128)(2,1)S(1)} all-gather(bf16[32,1024]{1,0:T(8,128)(2,1)S(1)} %fusion.43), channel_id=1, replica_groups=mesh['ctx'=32,'tp'=4] {'tp'}, dimensions={0}, use_global_device_ids=true | all-gather | bytes 327680 | tf_op jit(solution)/shard_map/all_gather | solution.py:329
  27.0 42.1 %shard_map.237 = bf16[4096,256]{1,0:T(8,128)(2,1)} custom-call(bf16[128,256]{1,0:T(8,128)(2,1)} %pad_maximum_fusion.2.part_ref), custom_call_target="tpu_custom_call" | custom-call | tf_op jit(solution)/shard_map/pallas_call | solution.py:67
  69.1 1.7 copy.76
  70.8 1.7 fusion.82
  72.5 1.5 copy.77
  74.0 2.0 fusion.86
  77.8 1.4 subtract_convert_fusion
  79.2 1.5 concatenate.38
  80.7 1.6 copy.79
  82.3 1.5 concatenate.39
  83.8 1.6 copy.80
  86.0 1.4 multiply_add_fusion.2
  87.4 1.4 add.168
  88.8 2.3 copy.81
  91.9 2.0 fusion.2
  95.2 2.0 fusion.85
  97.2 1.7 copy.82
  98.9 1.7 convert_element_type.134
  100.5 2.0 convolution_convert_fusion.8
  102.6 8.0 %all_gather.14 = bf16[128,1024]{1,0:T(8,128)(2,1)} all-gather(bf16[32,1024]{1,0:T(8,128)(2,1)S(1)} %copy-done.33), channel_id=1, replica_groups=mesh['ctx'=32,'tp'=4] {'tp'}, dimensions={0}, use_global_device_ids=true | all-gather | bytes 327680 | tf_op jit(solution)/shard_map/all_gather | solution.py:329
  110.6 20.3 %reduce-scatter.5.cloned.1.call-done = bf16[32,1024]{1,0:T(8,128)(2,1)} async-done(((bf16[128,1024]{1,0:T(8,128)(2,1)}), bf16[32,1024]{1,0:T(8,128)(2,1)}) %reduce-scatter.5.cloned.1.call-update) | async-done | bytes 65552 | tf_op jit(solution)/shard_map/reduce_scatter | solution.py:333
  133.0 7.3 %all_gather.13 = bf16[128,1024]{1,0:T(8,128)(2,1)S(1)} all-gather(bf16[32,1024]{1,0:T(8,128)(2,1)S(1)} %multiply_convert_fusion.3), channel_id=1, replica_groups=mesh['ctx'=32,'tp'=4] {'tp'}, dimensions={0}, use_global_device_ids=true | all-gather | bytes 327680 | tf_op jit(solution)/shard_map/all_gather | solution.py:329
  140.3 2.3 fusion.87
  143.2 1.7 multiply_convert_fusion
  145.8 1.6 fusion.31
  151.3 1.6 copy.90
  156.8 17.1 %reduce-scatter.9.cloned.1.call-done = bf16[32,1024]{1,0:T(8,128)(2,1)} async-done(((bf16[128,1024]{1,0:T(8,128)(2,1)}), bf16[32,1024]{1,0:T(8,128)(2,1)}) %reduce-scatter.9.cloned.1.call-update) | async-done | bytes 65552 | tf_op jit(solution)/shard_map/reduce_scatter | solution.py:333
  173.9 1.5 fusion.51
  177.0 7.5 %all_gather.15 = bf16[128,1024]{1,0:T(8,128)(2,1)S(1)} all-gather(bf16[32,1024]{1,0:T(8,128)(2,1)S(1)} %fusion.77), channel_id=1, replica_groups=mesh['ctx'=32,'tp'=4] {'tp'}, dimensions={0}, use_global_device_ids=true | all-gather | bytes 327680 | tf_op jit(solution)/shard_map/all_gather | solution.py:329
  185.2 2.0 convolution_convert_fusion.9
  187.2 1.6 reshape.328
  188.8 1.7 copy.84
  191.7 4.9 fusion.16
  196.7 1.7 fusion.1
  198.4 1.5 fusion.17
  200.0 1.8 convolution_bitcast_fusion.2
  201.8 4.4 reshape.330
  206.2 4.4 reshape.331
  210.6 5.0 maximum_bitcast_fusion
  215.6 5.5 copy.93
  221.2 42.9 %shard_map.238 = f32[128,256]{1,0:T(8,128)} custom-call(bf16[4096,256]{1,0:T(8,128)(2,1)} %bitcast.191), custom_call_target="tpu_custom_call" | custom-call | tf_op jit(solution)/shard_map/pallas_call | solution.py:120
  266.3 1.9 copy.85
  270.7 1.7 copy.89
  272.3 1.7 copy.86
  278.0 1.9 fusion.28
  280.2 2.2 convolution_convert_fusion.7
  282.4 2.1 fusion.27
  284.7 1.8 fusion.30
  286.5 1.9 fusion.29
  288.4 2.0 fusion.26
  290.4 3.3 fusion.8
  293.7 2.3 fusion.7
  296.0 2.4 fusion.10.whole_ref
  298.3 8.0 %reduce-scatter.11.cloned.1.call-done = bf16[32,1024]{1,0:T(8,128)(2,1)} async-done(((bf16[128,1024]{1,0:T(8,128)(2,1)}), bf16[32,1024]{1,0:T(8,128)(2,1)}) %reduce-scatter.11.cloned.1.call-update) | async-done | bytes 65552 | tf_op jit(solution)/shard_map/reduce_scatter | solution.py:333
  307.5 13.1 %psum.7 = f32[2176]{0:T(1024)S(1)} all-reduce(f32[2176]{0:T(1024)S(1)} %concatenate.47), channel_id=1, replica_groups=mesh['ctx'=32,'tp'=4] {'tp'}, use_global_device_ids=true, to_apply=%region_23.24 | all-reduce | flops 2176 | bytes 17408 | tf_op jit(solution)/shard_map/psum | solution.py:515
  321.2 285.3 %shard_map.239 = (bf16[1024,4224]{1,0:T(8,128)(2,1)}, f32[8,384]{1,0:T(8,128)}) custom-call(bf16[1024,4224]{1,0:T(8,128)(2,1)} %fusion.10.whole_ref, f32[8,384]{1,0:T(8,128)} %reshape.333.extra_ref), custom_call_target="tpu_custom_call" | custom-call | tf_op jit(solution)/shard_map/pallas_call | solution.py:232
  606.5 10.5 %convert_element_type.165 = f32[1024,4224]{1,0:T(8,128)} convert(bf16[1024,4224]{1,0:T(8,128)(2,1)} %get-tuple-element.16) | non-fusion elementwise | flops 4325376 | bytes 25952256 | tf_op jit(solution)/shard_map/convert_element_type | solution.py:523
  617.0 5.2 slice_bitcast_fusion
  622.2 1.7 slice_bitcast_fusion.1
  623.9 4.3 fusion.80
  629.4 2.1 slice.109
  631.5 6.2 copy.103
  639.6 2.1 fusion.81
  641.7 1.8 fusion.46
  (183 shorter events, 44.0 us)
Async XLA Ops:
  7.2 136.0 %copy-start = (bf16[1152,1024]{1,0:T(8,128)(2,1)S(1)}, bf16[1152,1024]{1,0:T(8,128)(2,1)}, u32[]{:S(2)}) copy-start(bf16[1152,1024]{1,0:T(8,128)(2,1)} %param.26) | copy-start | bytes 7077892
  7.2 123.7 %reduce-scatter.5.cloned.1.call-start = ((), (), s32[]{:S(2)}) async-start(), calls=%async_computation.4 | async-start | bytes 327680 | tf_op jit(solution)/shard_map/reduce_scatter | solution.py:333
  9.3 0.9 copy-start.49
  18.3 54.2 %copy-start.5 = (bf16[128,1024]{1,0:T(8,128)(2,1)}, bf16[128,1024]{1,0:T(8,128)(2,1)S(1)}, u32[]{:S(2)}) copy-start(bf16[128,1024]{1,0:T(8,128)(2,1)S(1)} %all_gather.12) | copy-start | bytes 786436
  19.7 52.8 %copy-start.29 = (f32[128,128]{0,1:T(8,128)}, f32[128,128]{0,1:T(8,128)S(1)}, u32[]{:S(2)}) copy-start(f32[128,128]{0,1:T(8,128)S(1)} %get-tuple-element.96) | copy-start | bytes 196612
  19.7 5.3 copy-start.46
  24.3 48.3 %copy-start.35 = (f32[128,32]{0,1:T(8,128)}, f32[128,32]{0,1:T(8,128)S(1)}, u32[]{:S(2)}) copy-start(f32[128,32]{0,1:T(8,128)S(1)} %get-tuple-element.94) | copy-start | bytes 49156
  77.0 16.9 %copy-start.17 = (f32[128,256]{0,1:T(8,128)}, f32[128,256]{0,1:T(8,128)S(1)}, u32[]{:S(2)}) copy-start(f32[128,256]{0,1:T(8,128)S(1)} %copy.78) | copy-start | bytes 393220
  77.1 2.1 copy-start.42
  91.9 3.2 copy-start.14
  91.9 3.2 copy-start.31
  94.0 3.2 copy-start.3
  94.0 3.2 copy-start.41
  95.1 2.0 copy-start.44
  95.1 7.5 %copy-start.33 = (bf16[32,1024]{1,0:T(8,128)(2,1)S(1)}, bf16[32,1024]{1,0:T(8,128)(2,1)}, u32[]{:S(2)}) copy-start(bf16[32,1024]{1,0:T(8,128)(2,1)} %param.27) | copy-start | bytes 196612
  95.1 35.8 %copy-start.11 = (bf16[32,1024]{1,0:T(8,128)(2,1)S(1)}, bf16[32,1024]{1,0:T(8,128)(2,1)}, u32[]{:S(2)}) copy-start(bf16[32,1024]{1,0:T(8,128)(2,1)} %param.14) | copy-start | bytes 196612
  102.6 71.4 %reduce-scatter.9.cloned.1.call-start = ((), (), s32[]{:S(2)}) async-start(), calls=%async_computation.6 | async-start | bytes 327680 | tf_op jit(solution)/shard_map/reduce_scatter | solution.py:333
  130.9 11.7 %copy-start.8 = (bf16[1024,1152]{1,0:T(8,128)(2,1)S(1)}, bf16[1024,1152]{1,0:T(8,128)(2,1)}, u32[]{:S(2)}) copy-start(bf16[1024,1152]{1,0:T(8,128)(2,1)} %param.25) | copy-start | bytes 7077892
  130.9 12.2 %copy-start.27 = (bf16[128,1024]{1,0:T(8,128)(2,1)S(1)}, bf16[128,1024]{1,0:T(8,128)(2,1)}, u32[]{:S(2)}) copy-start(bf16[128,1024]{1,0:T(8,128)(2,1)} %all_gather.14) | copy-start | bytes 786436
  132.1 10.5 %copy-start.47 = (f32[32]{0:T(128)}, f32[32]{0:T(128)S(1)}, u32[]{:S(2)}) copy-start(f32[32]{0:T(128)S(1)} %add_rsqrt_fusion.2) | copy-start | bytes 388
  140.3 2.3 copy-start.9
  142.6 2.3 copy-start.7
  144.9 0.9 copy-start.20
  144.9 0.9 copy-start.23
  144.9 29.0 %copy-start.19 = (bf16[32,1024]{1,0:T(8,128)(2,1)S(1)}, bf16[32,1024]{1,0:T(8,128)(2,1)}, u32[]{:S(2)}) copy-start(bf16[32,1024]{1,0:T(8,128)(2,1)} %reduce-scatter.5.cloned.1.call-done) | copy-start | bytes 196612
  147.4 158.9 %reduce-scatter.11.cloned.1.call-start = ((), (), s32[]{:S(2)}) async-start(), calls=%async_computation.7 | async-start | bytes 327680 | tf_op jit(solution)/shard_map/reduce_scatter | solution.py:333
  175.5 0.6 copy-start.53
  184.5 0.7 copy-start.12
  190.5 6.1 copy-start.4
  190.5 6.1 copy-start.15
  190.5 6.1 copy-start.32
  190.5 6.1 copy-start.34
  190.5 6.1 copy-start.51
  196.6 1.8 copy-start.25
  196.6 1.8 copy-start.26
  215.6 49.4 %copy-start.36 = (f32[128,32]{0,1:T(8,128)S(1)}, f32[128,32]{0,1:T(8,128)}, u32[]{:S(2)}) copy-start(f32[128,32]{0,1:T(8,128)} %copy-done.35) | copy-start | bytes 49156
  215.6 49.4 %copy-start.30 = (f32[128,128]{0,1:T(8,128)S(1)}, f32[128,128]{0,1:T(8,128)}, u32[]{:S(2)}) copy-start(f32[128,128]{0,1:T(8,128)} %copy-done.29) | copy-start | bytes 196612
  215.6 49.5 %copy-start.52 = (f32[64]{0:T(128)S(1)}, f32[64]{0:T(128)}, u32[]{:S(2)}) copy-start(f32[64]{0:T(128)} %param.21) | copy-start | bytes 772
  215.6 53.7 %copy-start.18 = (f32[128,256]{0,1:T(8,128)S(1)}, f32[128,256]{0,1:T(8,128)}, u32[]{:S(2)}) copy-start(f32[128,256]{0,1:T(8,128)} %copy-done.17) | copy-start | bytes 393220
  215.6 53.7 %copy-start.48 = (f32[64]{0:T(128)S(1)}, f32[64]{0:T(128)}, u32[]{:S(2)}) copy-start(f32[64]{0:T(128)} %param.20) | copy-start | bytes 772
  215.6 58.3 %copy-start.21 = (f32[128,256]{1,0:T(8,128)S(1)}, f32[128,256]{1,0:T(8,128)}, u32[]{:S(2)}) copy-start(f32[128,256]{1,0:T(8,128)} %fusion.86) | copy-start | bytes 393220
  221.2 53.9 %copy-start.16 = (bf16[1024,256]{1,0:T(8,128)(2,1)S(1)}, bf16[1024,256]{1,0:T(8,128)(2,1)}, u32[]{:S(2)}) copy-start(bf16[1024,256]{1,0:T(8,128)(2,1)} %param.17) | copy-start | bytes 1572868
  270.0 12.4 %copy-start.6 = (bf16[128,1024]{1,0:T(8,128)(2,1)S(1)}, bf16[128,1024]{1,0:T(8,128)(2,1)}, u32[]{:S(2)}) copy-start(bf16[128,1024]{1,0:T(8,128)(2,1)} %copy-done.5) | copy-start | bytes 786436
  275.1 0.6 copy-start.38
  275.7 12.7 %copy-start.13 = (bf16[128,1024]{1,0:T(8,128)(2,1)S(1)}, bf16[128,1024]{1,0:T(8,128)(2,1)}, u32[]{:S(2)}) copy-start(bf16[128,1024]{1,0:T(8,128)(2,1)} %copy-done.12) | copy-start | bytes 786436
  276.7 5.7 copy-start.37
  276.7 13.7 %copy-start.10 = (bf16[128,1024]{1,0:T(8,128)(2,1)S(1)}, bf16[128,1024]{1,0:T(8,128)(2,1)}, u32[]{:S(2)}) copy-start(bf16[128,1024]{1,0:T(8,128)(2,1)} %copy-done.9) | copy-start | bytes 786436
  279.9 361.7 %reduce-scatter.7.cloned.1.call-start = ((), (), s32[]{:S(2)}) async-start(), calls=%async_computation.5 | async-start | bytes 327680 | tf_op jit(solution)/shard_map/reduce_scatter | solution.py:333
  282.4 11.3 %copy-start.24 = (bf16[128,1152]{1,0:T(8,128)(2,1)S(1)}, bf16[128,1152]{1,0:T(8,128)(2,1)}, u32[]{:S(2)}) copy-start(bf16[128,1152]{1,0:T(8,128)(2,1)} %copy-done.23) | copy-start | bytes 884740
  282.4 13.6 %copy-start.22 = (bf16[128,1152]{1,0:T(8,128)(2,1)S(1)}, bf16[128,1152]{1,0:T(8,128)(2,1)}, u32[]{:S(2)}) copy-start(bf16[128,1152]{1,0:T(8,128)(2,1)} %get-tuple-element.70) | copy-start | bytes 884740
  282.4 13.5 %copy-start.28 = (bf16[128,1024]{1,0:T(8,128)(2,1)S(1)}, bf16[128,1024]{1,0:T(8,128)(2,1)}, u32[]{:S(2)}) copy-start(bf16[128,1024]{1,0:T(8,128)(2,1)} %all_gather.14) | copy-start | bytes 786436
  290.4 16.0 %copy-start.40 = (f32[1024]{0:T(1024)S(1)}, f32[1024]{0:T(1024)}, u32[]{:S(2)}) copy-start(f32[1024]{0:T(1024)} %param.16) | copy-start | bytes 12292
  290.4 16.0 %copy-start.50 = (f32[32]{0:T(128)S(1)}, f32[32]{0:T(128)}, u32[]{:S(2)}) copy-start(f32[32]{0:T(128)} %copy-done.49) | copy-start | bytes 388
  290.4 17.0 %copy-start.43 = (f32[1024]{0:T(1024)S(1)}, f32[1024]{0:T(1024)}, u32[]{:S(2)}) copy-start(f32[1024]{0:T(1024)} %get-tuple-element.56) | copy-start | bytes 12292
  617.0 6.9 %copy-start.2 = (bf16[1024,4224]{1,0:T(8,128)(2,1)S(1)}, bf16[1024,4224]{1,0:T(8,128)(2,1)}, u32[]{:S(2)}) copy-start(bf16[1024,4224]{1,0:T(8,128)(2,1)} %get-tuple-element.16) | copy-start | bytes 25952260
  623.9 4.4 copy-start.45
  631.5 11.9 %copy-start.1 = (bf16[1152,1024]{1,0:T(8,128)(2,1)S(1)}, bf16[1152,1024]{1,0:T(8,128)(2,1)}, u32[]{:S(2)}) copy-start(bf16[1152,1024]{1,0:T(8,128)(2,1)} %param.26) | copy-start | bytes 7077892
  637.7 4.0 copy-start.39
Sparse Core Ops, SparseCore 0:
  102.7 28.2 reduce-scatter.4
  147.6 26.3 reduce-scatter.8
  280.0 26.2 reduce-scatter.10
  309.0 48.6 reduce-scatter.6

commit v7 on v6

--- a/solution.py
+++ b/solution.py
@@ -224,7 +224,7 @@
         copy.wait_send()
 
 
-def ctx_sum(whole, extra, n, collective_id, pieces=2):
+def ctx_sum(whole, extra, n, collective_id, pieces=4):
     rows, cols = whole.shape[0] // n, whole.shape[1]
     lanes = cols // 128
     edges = [128 * (lanes * p // pieces) for p in range(pieces + 1)]

time: 656 us -> 600 us (0.915)
  Pallas kernels: 370 us -> 318 us
    pallas_call x1, Pallas kernels: 285 us -> 233 us  [ctx_sum(): pl.pallas_call(functools.partial(_sum_kernel, n, spans), out_shape=(jax.S...]
  transfers between devices with their start and end apart: 4 -> 4, of which waited for: 3 -> 3; matrix products, arithmetic and copies ran while one was open for 10% -> 11% of each run, Pallas kernels for 44% -> 39%
where the time goes in v7:
time: 600 us; the launch traced here: 597 us
  Pallas kernels  318 us (53%)
  local copies, waits for them, and re-layouts  79.4 us (13%)
  matrix products  50.9 us (8%)
  waiting for transfers between devices  45.6 us (8%)
  other arithmetic  44.3 us (7%)
  blocking collectives  44 us (7%)
  between operations  15.1 us (3%)
    pallas_call x1, Pallas kernels, ctx_sum(): pl.pallas_call(functools.partial(_sum_kernel, n, spans), out_shape=(jax.S...  233 us
    reduce_scatter x4, waiting for transfers between devices, reduce_rows(): lax.psum_scatter(partial_rows.astype(jnp.bfloat16), 'tp', scatter_dimensi...  45.5 us
    pallas_call x1, Pallas kernels, ctx_scatter(): pl.pallas_call(functools.partial(_scatter_kernel, n), out_shape=jax.Shape...  42.9 us
    pallas_call x1, Pallas kernels, ctx_gather(): pl.pallas_call(functools.partial(_gather_kernel, n), out_shape=jax.ShapeD...  42.1 us
    all_gather x4, blocking collectives, gather_rows(): return lax.all_gather(rows_low, 'tp', axis=0, tiled=True)  30.9 us
    psum x1, blocking collectives, per_device(): gain_flat = lax.psum(jnp.concatenate(gain_parts), 'tp')  13.1 us
  transfers between devices with their start and end apart: 4, of which 3 were waited for; matrix products, arithmetic and copies ran while one was open for 11% of the time, Pallas kernels for 39%

profile of v7, /device:TPU:28, one launch (start us, length us, event | category | flops | bytes accessed | tf_op | source)
XLA Modules:
  0.0 597.2 jit_solution(15954840436570347880)
XLA Ops:
  10.2 8.1 %all_gather.12 = bf16[128,1024]{1,0:T(8,128)(2,1)S(1)} all-gather(bf16[32,1024]{1,0:T(8,128)(2,1)S(1)} %fusion.43), channel_id=1, replica_groups=mesh['ctx'=32,'tp'=4] {'tp'}, dimensions={0}, use_global_device_ids=true | all-gather | bytes 327680 | tf_op jit(solution)/shard_map/all_gather | solution.py:329
  27.0 42.1 %shard_map.237 = bf16[4096,256]{1,0:T(8,128)(2,1)} custom-call(bf16[128,256]{1,0:T(8,128)(2,1)} %pad_maximum_fusion.2.part_ref), custom_call_target="tpu_custom_call" | custom-call | tf_op jit(solution)/shard_map/pallas_call | solution.py:67
  69.1 1.7 copy.76
  70.8 1.7 fusion.82
  72.5 1.5 copy.77
  74.0 2.0 fusion.86
  77.8 1.4 subtract_convert_fusion
  79.2 1.5 concatenate.38
  80.7 1.6 copy.79
  82.3 1.5 concatenate.39
  83.8 1.6 copy.80
  86.0 1.4 multiply_add_fusion.2
  87.4 1.4 add.168
  88.8 2.3 copy.81
  91.9 2.0 fusion.2
  95.2 2.0 fusion.85
  97.2 1.7 copy.82
  98.9 1.7 convert_element_type.134
  100.5 2.0 convolution_convert_fusion.8
  102.6 8.0 %all_gather.14 = bf16[128,1024]{1,0:T(8,128)(2,1)} all-gather(bf16[32,1024]{1,0:T(8,128)(2,1)S(1)} %copy-done.33), channel_id=1, replica_groups=mesh['ctx'=32,'tp'=4] {'tp'}, dimensions={0}, use_global_device_ids=true | all-gather | bytes 327680 | tf_op jit(solution)/shard_map/all_gather | solution.py:329
  110.6 20.3 %reduce-scatter.5.cloned.1.call-done = bf16[32,1024]{1,0:T(8,128)(2,1)} async-done(((bf16[128,1024]{1,0:T(8,128)(2,1)}), bf16[32,1024]{1,0:T(8,128)(2,1)}) %reduce-scatter.5.cloned.1.call-update) | async-done | bytes 65552 | tf_op jit(solution)/shard_map/reduce_scatter | solution.py:333
  133.0 7.3 %all_gather.13 = bf16[128,1024]{1,0:T(8,128)(2,1)S(1)} all-gather(bf16[32,1024]{1,0:T(8,128)(2,1)S(1)} %multiply_convert_fusion.3), channel_id=1, replica_groups=mesh['ctx'=32,'tp'=4] {'tp'}, dimensions={0}, use_global_device_ids=true | all-gather | bytes 327680 | tf_op jit(solution)/shard_map/all_gather | solution.py:329
  140.3 2.3 fusion.87
  143.2 1.7 multiply_convert_fusion
  145.8 1.6 fusion.31
  151.3 1.6 copy.90
  156.8 17.1 %reduce-scatter.9.cloned.1.call-done = bf16[32,1024]{1,0:T(8,128)(2,1)} async-done(((bf16[128,1024]{1,0:T(8,128)(2,1)}), bf16[32,1024]{1,0:T(8,128)(2,1)}) %reduce-scatter.9.cloned.1.call-update) | async-done | bytes 65552 | tf_op jit(solution)/shard_map/reduce_scatter | solution.py:333
  173.9 1.5 fusion.51
  177.0 7.5 %all_gather.15 = bf16[128,1024]{1,0:T(8,128)(2,1)S(1)} all-gather(bf16[32,1024]{1,0:T(8,128)(2,1)S(1)} %fusion.77), channel_id=1, replica_groups=mesh['ctx'=32,'tp'=4] {'tp'}, dimensions={0}, use_global_device_ids=true | all-gather | bytes 327680 | tf_op jit(solution)/shard_map/all_gather | solution.py:329
  185.2 2.0 convolution_convert_fusion.9
  187.2 1.6 reshape.328
  188.8 1.7 copy.84
  191.7 4.9 fusion.16
  196.7 1.7 fusion.1
  198.4 1.5 fusion.17
  200.0 1.8 convolution_bitcast_fusion.2
  201.8 4.4 reshape.330
  206.2 4.4 reshape.331
  210.6 5.0 maximum_bitcast_fusion
  215.6 5.5 copy.93
  221.2 42.9 %shard_map.238 = f32[128,256]{1,0:T(8,128)} custom-call(bf16[4096,256]{1,0:T(8,128)(2,1)} %bitcast.191), custom_call_target="tpu_custom_call" | custom-call | tf_op jit(solution)/shard_map/pallas_call | solution.py:120
  266.3 1.9 copy.85
  270.7 1.7 copy.89
  272.3 1.7 copy.86
  278.0 1.9 fusion.28
  280.2 2.2 convolution_convert_fusion.7
  282.4 2.1 fusion.27
  284.7 1.8 fusion.30
  286.5 1.9 fusion.29
  288.4 2.0 fusion.26
  290.4 3.3 fusion.8
  293.7 2.3 fusion.7
  296.0 2.4 fusion.10.whole_ref
  298.3 8.0 %reduce-scatter.11.cloned.1.call-done = bf16[32,1024]{1,0:T(8,128)(2,1)} async-done(((bf16[128,1024]{1,0:T(8,128)(2,1)}), bf16[32,1024]{1,0:T(8,128)(2,1)}) %reduce-scatter.11.cloned.1.call-update) | async-done | bytes 65552 | tf_op jit(solution)/shard_map/reduce_scatter | solution.py:333
  307.5 13.1 %psum.7 = f32[2176]{0:T(1024)S(1)} all-reduce(f32[2176]{0:T(1024)S(1)} %concatenate.47), channel_id=1, replica_groups=mesh['ctx'=32,'tp'=4] {'tp'}, use_global_device_ids=true, to_apply=%region_23.24 | all-reduce | flops 2176 | bytes 17408 | tf_op jit(solution)/shard_map/psum | solution.py:515
  321.2 232.6 %shard_map.239 = (bf16[1024,4224]{1,0:T(8,128)(2,1)}, f32[8,384]{1,0:T(8,128)}) custom-call(bf16[1024,4224]{1,0:T(8,128)(2,1)} %fusion.10.whole_ref, f32[8,384]{1,0:T(8,128)} %reshape.333.extra_ref), custom_call_target="tpu_custom_call" | custom-call | tf_op jit(solution)/shard_map/pallas_call | solution.py:232
  553.8 10.5 %convert_element_type.165 = f32[1024,4224]{1,0:T(8,128)} convert(bf16[1024,4224]{1,0:T(8,128)(2,1)} %get-tuple-element.16) | non-fusion elementwise | flops 4325376 | bytes 25952256 | tf_op jit(solution)/shard_map/convert_element_type | solution.py:523
  564.3 5.2 slice_bitcast_fusion
  569.5 1.7 slice_bitcast_fusion.1
  571.2 4.3 fusion.80
  576.7 2.1 slice.109
  578.8 6.2 %copy.103 = f32[1152,1024]{1,0:T(8,128)} copy(f32[1152,1024]{0,1:T(8,128)} %slice_bitcast_fusion) | data formatting | bytes 9437184
  586.9 2.1 fusion.81
  588.9 1.8 fusion.46
  (183 shorter events, 44.0 us)
Async XLA Ops:
  7.2 136.0 %copy-start = (bf16[1152,1024]{1,0:T(8,128)(2,1)S(1)}, bf16[1152,1024]{1,0:T(8,128)(2,1)}, u32[]{:S(2)}) copy-start(bf16[1152,1024]{1,0:T(8,128)(2,1)} %param.26) | copy-start | bytes 7077892
  7.2 123.7 %reduce-scatter.5.cloned.1.call-start = ((), (), s32[]{:S(2)}) async-start(), calls=%async_computation.4 | async-start | bytes 327680 | tf_op jit(solution)/shard_map/reduce_scatter | solution.py:333
  9.3 0.9 copy-start.49
  18.3 54.2 %copy-start.5 = (bf16[128,1024]{1,0:T(8,128)(2,1)}, bf16[128,1024]{1,0:T(8,128)(2,1)S(1)}, u32[]{:S(2)}) copy-start(bf16[128,1024]{1,0:T(8,128)(2,1)S(1)} %all_gather.12) | copy-start | bytes 786436
  19.7 52.8 %copy-start.29 = (f32[128,128]{0,1:T(8,128)}, f32[128,128]{0,1:T(8,128)S(1)}, u32[]{:S(2)}) copy-start(f32[128,128]{0,1:T(8,128)S(1)} %get-tuple-element.96) | copy-start | bytes 196612
  19.7 5.3 copy-start.46
  24.3 48.3 %copy-start.35 = (f32[128,32]{0,1:T(8,128)}, f32[128,32]{0,1:T(8,128)S(1)}, u32[]{:S(2)}) copy-start(f32[128,32]{0,1:T(8,128)S(1)} %get-tuple-element.94) | copy-start | bytes 49156
  77.0 16.9 %copy-start.17 = (f32[128,256]{0,1:T(8,128)}, f32[128,256]{0,1:T(8,128)S(1)}, u32[]{:S(2)}) copy-start(f32[128,256]{0,1:T(8,128)S(1)} %copy.78) | copy-start | bytes 393220
  77.1 2.1 copy-start.42
  91.9 3.2 copy-start.14
  91.9 3.2 copy-start.31
  94.0 3.2 copy-start.3
  94.0 3.2 copy-start.41
  95.1 2.0 copy-start.44
  95.1 7.5 %copy-start.33 = (bf16[32,1024]{1,0:T(8,128)(2,1)S(1)}, bf16[32,1024]{1,0:T(8,128)(2,1)}, u32[]{:S(2)}) copy-start(bf16[32,1024]{1,0:T(8,128)(2,1)} %param.27) | copy-start | bytes 196612
  95.1 35.8 %copy-start.11 = (bf16[32,1024]{1,0:T(8,128)(2,1)S(1)}, bf16[32,1024]{1,0:T(8,128)(2,1)}, u32[]{:S(2)}) copy-start(bf16[32,1024]{1,0:T(8,128)(2,1)} %param.14) | copy-start | bytes 196612
  102.6 71.4 %reduce-scatter.9.cloned.1.call-start = ((), (), s32[]{:S(2)}) async-start(), calls=%async_computation.6 | async-start | bytes 327680 | tf_op jit(solution)/shard_map/reduce_scatter | solution.py:333
  130.9 11.7 %copy-start.8 = (bf16[1024,1152]{1,0:T(8,128)(2,1)S(1)}, bf16[1024,1152]{1,0:T(8,128)(2,1)}, u32[]{:S(2)}) copy-start(bf16[1024,1152]{1,0:T(8,128)(2,1)} %param.25) | copy-start | bytes 7077892
  130.9 12.2 %copy-start.27 = (bf16[128,1024]{1,0:T(8,128)(2,1)S(1)}, bf16[128,1024]{1,0:T(8,128)(2,1)}, u32[]{:S(2)}) copy-start(bf16[128,1024]{1,0:T(8,128)(2,1)} %all_gather.14) | copy-start | bytes 786436
  132.1 10.5 %copy-start.47 = (f32[32]{0:T(128)}, f32[32]{0:T(128)S(1)}, u32[]{:S(2)}) copy-start(f32[32]{0:T(128)S(1)} %add_rsqrt_fusion.2) | copy-start | bytes 388
  140.3 2.3 copy-start.9
  142.6 2.3 copy-start.7
  144.9 0.9 copy-start.20
  144.9 0.9 copy-start.23
  144.9 29.0 %copy-start.19 = (bf16[32,1024]{1,0:T(8,128)(2,1)S(1)}, bf16[32,1024]{1,0:T(8,128)(2,1)}, u32[]{:S(2)}) copy-start(bf16[32,1024]{1,0:T(8,128)(2,1)} %reduce-scatter.5.cloned.1.call-done) | copy-start | bytes 196612
  147.4 158.9 %reduce-scatter.11.cloned.1.call-start = ((), (), s32[]{:S(2)}) async-start(), calls=%async_computation.7 | async-start | bytes 327680 | tf_op jit(solution)/shard_map/reduce_scatter | solution.py:333
  175.5 0.6 copy-start.53
  184.5 0.7 copy-start.12
  190.5 6.1 %copy-start.4 = (f32[2,2,2048,64,2]{2,3,4,1,0:T(8,128)S(1)}, f32[2,2,2048,64,2]{2,3,4,1,0:T(8,128)}, u32[]{:S(2)}) copy-start(f32[2,2,2048,64,2]{2,3,4,1,0:T(8,128)} %copy-done.3) | copy-start | bytes 12582916
  190.5 6.1 %copy-start.15 = (pred[64,2048]{1,0:T(8,128)(4,1)S(1)}, pred[64,2048]{1,0:T(8,128)(4,1)}, u32[]{:S(2)}) copy-start(pred[64,2048]{1,0:T(8,128)(4,1)} %copy-done.14) | copy-start | bytes 393220
  190.5 6.1 %copy-start.32 = (bf16[2,2048,128]{1,2,0:T(8,128)(2,1)S(1)}, bf16[2,2048,128]{1,2,0:T(8,128)(2,1)}, u32[]{:S(2)}) copy-start(bf16[2,2048,128]{1,2,0:T(8,128)(2,1)} %copy.81) | copy-start | bytes 3145732
  190.5 6.1 %copy-start.34 = (bf16[2,64,2,2,64]{1,4,3,2,0:T(8,128)(2,1)S(1)}, bf16[2,64,2,2,64]{1,4,3,2,0:T(8,128)(2,1)}, u32[]{:S(2)}) copy-start(bf16[2,64,2,2,64]{1,4,3,2,0:T(8,128)(2,1)} %copy.84) | copy-start | bytes 196612
  190.5 6.1 %copy-start.51 = (f32[2,2,2,64]{3,2,1,0:T(2,128)S(1)}, f32[2,2,2,64]{3,2,1,0:T(2,128)}, u32[]{:S(2)}) copy-start(f32[2,2,2,64]{3,2,1,0:T(2,128)} %log_add_fusion) | copy-start | bytes 6148
  196.6 1.8 copy-start.25
  196.6 1.8 copy-start.26
  215.6 49.4 %copy-start.36 = (f32[128,32]{0,1:T(8,128)S(1)}, f32[128,32]{0,1:T(8,128)}, u32[]{:S(2)}) copy-start(f32[128,32]{0,1:T(8,128)} %copy-done.35) | copy-start | bytes 49156
  215.6 49.4 %copy-start.30 = (f32[128,128]{0,1:T(8,128)S(1)}, f32[128,128]{0,1:T(8,128)}, u32[]{:S(2)}) copy-start(f32[128,128]{0,1:T(8,128)} %copy-done.29) | copy-start | bytes 196612
  215.6 49.5 %copy-start.52 = (f32[64]{0:T(128)S(1)}, f32[64]{0:T(128)}, u32[]{:S(2)}) copy-start(f32[64]{0:T(128)} %param.21) | copy-start | bytes 772
  215.6 53.7 %copy-start.18 = (f32[128,256]{0,1:T(8,128)S(1)}, f32[128,256]{0,1:T(8,128)}, u32[]{:S(2)}) copy-start(f32[128,256]{0,1:T(8,128)} %copy-done.17) | copy-start | bytes 393220
  215.6 53.7 %copy-start.48 = (f32[64]{0:T(128)S(1)}, f32[64]{0:T(128)}, u32[]{:S(2)}) copy-start(f32[64]{0:T(128)} %param.20) | copy-start | bytes 772
  215.6 58.3 %copy-start.21 = (f32[128,256]{1,0:T(8,128)S(1)}, f32[128,256]{1,0:T(8,128)}, u32[]{:S(2)}) copy-start(f32[128,256]{1,0:T(8,128)} %fusion.86) | copy-start | bytes 393220
  221.2 53.9 %copy-start.16 = (bf16[1024,256]{1,0:T(8,128)(2,1)S(1)}, bf16[1024,256]{1,0:T(8,128)(2,1)}, u32[]{:S(2)}) copy-start(bf16[1024,256]{1,0:T(8,128)(2,1)} %param.17) | copy-start | bytes 1572868
  270.0 12.4 %copy-start.6 = (bf16[128,1024]{1,0:T(8,128)(2,1)S(1)}, bf16[128,1024]{1,0:T(8,128)(2,1)}, u32[]{:S(2)}) copy-start(bf16[128,1024]{1,0:T(8,128)(2,1)} %copy-done.5) | copy-start | bytes 786436
  275.1 0.6 copy-start.38
  275.7 12.7 %copy-start.13 = (bf16[128,1024]{1,0:T(8,128)(2,1)S(1)}, bf16[128,1024]{1,0:T(8,128)(2,1)}, u32[]{:S(2)}) copy-start(bf16[128,1024]{1,0:T(8,128)(2,1)} %copy-done.12) | copy-start | bytes 786436
  276.7 5.7 copy-start.37
  276.7 13.7 %copy-start.10 = (bf16[128,1024]{1,0:T(8,128)(2,1)S(1)}, bf16[128,1024]{1,0:T(8,128)(2,1)}, u32[]{:S(2)}) copy-start(bf16[128,1024]{1,0:T(8,128)(2,1)} %copy-done.9) | copy-start | bytes 786436
  279.9 309.0 %reduce-scatter.7.cloned.1.call-start = ((), (), s32[]{:S(2)}) async-start(), calls=%async_computation.5 | async-start | bytes 327680 | tf_op jit(solution)/shard_map/reduce_scatter | solution.py:333
  282.4 11.3 %copy-start.24 = (bf16[128,1152]{1,0:T(8,128)(2,1)S(1)}, bf16[128,1152]{1,0:T(8,128)(2,1)}, u32[]{:S(2)}) copy-start(bf16[128,1152]{1,0:T(8,128)(2,1)} %copy-done.23) | copy-start | bytes 884740
  282.4 13.6 %copy-start.22 = (bf16[128,1152]{1,0:T(8,128)(2,1)S(1)}, bf16[128,1152]{1,0:T(8,128)(2,1)}, u32[]{:S(2)}) copy-start(bf16[128,1152]{1,0:T(8,128)(2,1)} %get-tuple-element.70) | copy-start | bytes 884740
  282.4 13.5 %copy-start.28 = (bf16[128,1024]{1,0:T(8,128)(2,1)S(1)}, bf16[128,1024]{1,0:T(8,128)(2,1)}, u32[]{:S(2)}) copy-start(bf16[128,1024]{1,0:T(8,128)(2,1)} %all_gather.14) | copy-start | bytes 786436
  290.4 16.0 %copy-start.40 = (f32[1024]{0:T(1024)S(1)}, f32[1024]{0:T(1024)}, u32[]{:S(2)}) copy-start(f32[1024]{0:T(1024)} %param.16) | copy-start | bytes 12292
  290.4 16.0 %copy-start.50 = (f32[32]{0:T(128)S(1)}, f32[32]{0:T(128)}, u32[]{:S(2)}) copy-start(f32[32]{0:T(128)} %copy-done.49) | copy-start | bytes 388
  290.4 17.0 %copy-start.43 = (f32[1024]{0:T(1024)S(1)}, f32[1024]{0:T(1024)}, u32[]{:S(2)}) copy-start(f32[1024]{0:T(1024)} %get-tuple-element.56) | copy-start | bytes 12292
  564.3 6.9 %copy-start.2 = (bf16[1024,4224]{1,0:T(8,128)(2,1)S(1)}, bf16[1024,4224]{1,0:T(8,128)(2,1)}, u32[]{:S(2)}) copy-start(bf16[1024,4224]{1,0:T(8,128)(2,1)} %get-tuple-element.16) | copy-start | bytes 25952260
  571.2 4.4 copy-start.45
  578.8 11.9 %copy-start.1 = (bf16[1152,1024]{1,0:T(8,128)(2,1)S(1)}, bf16[1152,1024]{1,0:T(8,128)(2,1)}, u32[]{:S(2)}) copy-start(bf16[1152,1024]{1,0:T(8,128)(2,1)} %param.26) | copy-start | bytes 7077892
  585.0 4.0 copy-start.39
Sparse Core Ops, SparseCore 0:
  102.7 28.2 reduce-scatter.4
  147.6 26.3 reduce-scatter.8
  280.0 26.2 reduce-scatter.10
  309.0 42.4 reduce-scatter.6
